TPU v7x, 128 devices: a whole 4x4x4 slice. The times are simulated.
128 devices in a mesh: section: 4 (over y_hi, core), seq: 32 (over y_lo, x, z).
Axes of the slice: x: 4, y: 4 (y_hi: 2, y_lo: 2; y = y_hi * 2 + y_lo), z: 4, core: 2. Of those that a mesh axis runs over, the one named last changes fastest.
Arguments:
- activations: bfloat16 [4, 4352, 1024], P('section', 'seq'), may hold values from -60 to 60
- incoming: bfloat16 [4, 4352, 1024], P('section', 'seq'), may hold values from -6 to 6
- w_query: bfloat16 [4, 1024, 512], P('section'), may hold values from -0.1875 to 0.1875
- w_key: bfloat16 [4, 1024, 512], P('section'), may hold values from -0.1875 to 0.1875
- w_value: bfloat16 [4, 1024, 512], P('section'), may hold values from -0.1875 to 0.1875
- w_out: bfloat16 [4, 512, 2048], P('section'), may hold values from -0.25 to 0.25
- block_ids: int32 [4352], replicated, may hold values from 0 to 135, never falling along the last dimension, each value on 1 to 256 neighbouring positions
- flip_order: int32 [4, 136], P('section'), may hold values from 0 to 135, each once within a row
Outputs:
- carry_out: bfloat16 [4, 4352, 1024], P('section', 'seq')
- grad_query: float32 [4, 1024, 512], P('section', 'seq')
- grad_key: float32 [4, 1024, 512], P('section', 'seq')
- grad_value: float32 [4, 1024, 512], P('section', 'seq')
- grad_out: float32 [4, 512, 2048], P('section', 'seq')
Inputs may be any that keep to these rules, and one draw needn't show every extreme that they name: `block_ids`: block ids never fall along the sequence; each block holds 1 to 256 tokens, one exactly 256. `flip_order`: each row is a permutation.
All inputs are finite; a program needn't handle non-finite values.
Results may differ from a plain program's by a relative error of at most 0.03.
Values may be sent and summed in bfloat16 or wider, within the bound.
A program may use at most 128 MiB of HBM per device.

v0:
```python
import jax
import jax.numpy as jnp
from jax import lax
from jax.sharding import PartitionSpec as P

HEADS = 8
HEAD_DIM = 64


EPSILON = 1e-06


def partner(block, axis, stride):
    count = lax.axis_size(axis)
    route = []
    for low in range(count):
        high = low | 1 << stride
        if high != low and high < count:
            route += [(low, high), (high, low)]
    return lax.ppermute(block, axis, route)


def shifted(block, axis, distance):
    devices = range(lax.axis_size(axis))
    route = [(i - distance, i) for i in devices if i - distance in devices]
    return lax.ppermute(block, axis, route)


def split_heads(matrix):
    return matrix.reshape(matrix.shape[0], HEADS, HEAD_DIM)


def head_major(matrix):
    return jnp.transpose(split_heads(matrix), (1, 0, 2))


def unit_heads(projected):
    parts = split_heads(projected)
    factor = lax.rsqrt(jnp.mean(parts * parts, axis=-1, keepdims=True) + EPSILON)
    return (parts * factor, factor)


def unit_back(grad_heads, unit, factor):
    return factor * (grad_heads - unit * jnp.mean(grad_heads * unit, axis=-1, keepdims=True))


def mirror(rows):
    for bit in range(lax.axis_size("seq").bit_length() - 1):
        rows = partner(rows, "seq", bit)
    return rows


def to_previous(rows):
    return shifted(rows, "section", -1)


def shards(activations, incoming, w_query, w_key, w_value, w_out, block_ids, flip_order):
    field = activations[0].astype(jnp.float32)
    upstream = incoming[0].astype(jnp.float32)
    weight_query = w_query[0]
    weight_key = w_key[0]
    weight_value = w_value[0]
    weight_out = w_out[0]
    flip_row = flip_order[0]
    rows = field.shape[0]
    width = field.shape[1]
    inner = weight_query.shape[1]
    scale = HEAD_DIM ** (-0.5)
    first = lax.axis_index("seq") * rows
    my_blocks = lax.dynamic_slice_in_dim(block_ids, first, rows)
    row_scale = lax.rsqrt(jnp.mean(field * field, axis=-1, keepdims=True) + EPSILON)
    unit_rows = field * row_scale
    normed = unit_rows.astype(jnp.bfloat16)
    query_raw = jnp.dot(normed, weight_query, preferred_element_type=jnp.float32)
    key_raw = jnp.dot(normed, weight_key, preferred_element_type=jnp.float32)
    values = jnp.dot(normed, weight_value, preferred_element_type=jnp.float32).astype(jnp.bfloat16)
    query_unit, query_scale = unit_heads(query_raw)
    key_unit, key_scale = unit_heads(key_raw)
    queries = query_unit.astype(jnp.bfloat16).reshape(rows, inner)
    keys = key_unit.astype(jnp.bfloat16).reshape(rows, inner)
    keys_all, values_all = (
        lax.all_gather(keys, "seq", axis=0, tiled=True),
        lax.all_gather(values, "seq", axis=0, tiled=True),
    )
    allowed = block_ids[None, :] <= my_blocks[:, None]
    query_heads = head_major(queries)
    key_heads_all = head_major(keys_all)
    value_heads_all = head_major(values_all)

    def probabilities(query_part, key_part):
        scores = jnp.dot(query_part, key_part.T, preferred_element_type=jnp.float32) * scale
        numerator = jnp.where(allowed, jnp.exp(scores), 0.0)
        denominator = jnp.sum(numerator, axis=-1, keepdims=True)
        return (numerator / denominator, denominator)

    def forward_head(operands):
        query_part, key_part, value_part = operands
        probs, denominator = probabilities(query_part, key_part)
        out_part = jnp.dot(
            probs.astype(jnp.bfloat16), value_part, preferred_element_type=jnp.float32
        ).astype(jnp.bfloat16)
        return (out_part, denominator[:, 0])

    heads_out, denominators = lax.map(forward_head, (query_heads, key_heads_all, value_heads_all))
    attended = jnp.transpose(heads_out, (1, 0, 2)).reshape(rows, inner)
    affine = jnp.dot(attended, weight_out, preferred_element_type=jnp.float32)
    shift_part = affine[:, :width]
    log_scale = affine[:, width:]
    factor = jnp.exp(-log_scale)
    latent = (field - shift_part) * factor
    grad_affine = jnp.concatenate([-upstream * factor, 1.0 - upstream * latent], axis=-1).astype(
        jnp.bfloat16
    )
    out_term = jnp.dot(attended.T, grad_affine, preferred_element_type=jnp.float32)
    grad_attn = jnp.dot(grad_affine, weight_out.T, preferred_element_type=jnp.float32).astype(
        jnp.bfloat16
    )
    correction = jnp.sum(
        split_heads(grad_attn.astype(jnp.float32)) * split_heads(attended.astype(jnp.float32)),
        axis=-1,
    )
    grad_heads = head_major(grad_attn)
    correction_heads = jnp.transpose(correction)[:, :, None]

    def backward_head(operands):
        query_part, key_part, value_part, grad_part, corr_part = operands
        probs, denominator = probabilities(query_part, key_part)
        grad_probs = jnp.dot(grad_part, value_part.T, preferred_element_type=jnp.float32)
        grad_scores = (probs * (grad_probs - corr_part)).astype(jnp.bfloat16)
        grad_qpart = jnp.dot(grad_scores, key_part, preferred_element_type=jnp.float32) * scale
        grad_kpart = jnp.dot(grad_scores.T, query_part, preferred_element_type=jnp.float32) * scale
        grad_vpart = jnp.dot(
            probs.astype(jnp.bfloat16).T, grad_part, preferred_element_type=jnp.float32
        )
        return (grad_qpart, grad_kpart, grad_vpart)

    grad_qheads, grad_kall, grad_vall = lax.map(
        backward_head, (query_heads, key_heads_all, value_heads_all, grad_heads, correction_heads)
    )
    key_terms = jnp.transpose(grad_kall, (1, 0, 2)).reshape(-1, inner)
    value_terms = jnp.transpose(grad_vall, (1, 0, 2)).reshape(-1, inner)
    grad_kunit, grad_vsum = (
        lax.psum_scatter(
            key_terms.astype(jnp.bfloat16), "seq", scatter_dimension=0, tiled=True
        ).astype(jnp.float32),
        lax.psum_scatter(
            value_terms.astype(jnp.bfloat16), "seq", scatter_dimension=0, tiled=True
        ).astype(jnp.float32),
    )
    grad_queries = (
        unit_back(jnp.transpose(grad_qheads, (1, 0, 2)), query_unit, query_scale)
        .reshape(rows, inner)
        .astype(jnp.bfloat16)
    )
    grad_keys = (
        unit_back(split_heads(grad_kunit), key_unit, key_scale)
        .reshape(rows, inner)
        .astype(jnp.bfloat16)
    )
    grad_values = grad_vsum.astype(jnp.bfloat16)
    query_term = jnp.dot(normed.T, grad_queries, preferred_element_type=jnp.float32)
    key_term = jnp.dot(normed.T, grad_keys, preferred_element_type=jnp.float32)
    value_term = jnp.dot(normed.T, grad_values, preferred_element_type=jnp.float32)
    sums = (
        lax.psum_scatter(
            query_term.astype(jnp.bfloat16), "seq", scatter_dimension=0, tiled=True
        ).astype(jnp.float32),
        lax.psum_scatter(
            key_term.astype(jnp.bfloat16), "seq", scatter_dimension=0, tiled=True
        ).astype(jnp.float32),
        lax.psum_scatter(
            value_term.astype(jnp.bfloat16), "seq", scatter_dimension=0, tiled=True
        ).astype(jnp.float32),
        lax.psum_scatter(
            out_term.astype(jnp.bfloat16), "seq", scatter_dimension=0, tiled=True
        ).astype(jnp.float32),
    )
    grad_normed = jnp.dot(grad_queries, weight_query.T, preferred_element_type=jnp.float32)
    grad_normed = grad_normed + jnp.dot(grad_keys, weight_key.T, preferred_element_type=jnp.float32)
    grad_normed = grad_normed + jnp.dot(
        grad_values, weight_value.T, preferred_element_type=jnp.float32
    )
    grad_input = upstream * factor + row_scale * (
        grad_normed - unit_rows * jnp.mean(grad_normed * unit_rows, axis=-1, keepdims=True)
    )
    grad_input = grad_input.astype(jnp.bfloat16)
    moved = mirror(to_previous(grad_input))
    carry = jnp.take(moved, flip_row, axis=0)
    return (carry[None], sums[0][None], sums[1][None], sums[2][None], sums[3][None])


def solution(mesh):
    in_specs = (
        P("section", "seq", None),
        P("section", "seq", None),
        P("section", None, None),
        P("section", None, None),
        P("section", None, None),
        P("section", None, None),
        P(),
        P("section", None),
    )
    out_specs = (
        P("section", "seq", None),
        P("section", "seq", None),
        P("section", "seq", None),
        P("section", "seq", None),
        P("section", "seq", None),
    )
    return jax.shard_map(shards, mesh=mesh, in_specs=in_specs, out_specs=out_specs, check_vma=False)
```

profile of v0, /device:TPU:0, one launch (start us, length us, event | category | flops | bytes accessed | tf_op | source)
XLA Modules:
  0.0 1467.9 jit_solution(6070266999776228398)
XLA Ops:
  8.5 2.3 copy.43
  16.0 2.3 convolution_convert_fusion.4
  22.7 153.8 %all-gather.3.cloned.1.call-done = bf16[4352,512]{1,0:T(8,128)(2,1)} async-done(((bf16[136,512]{1,0:T(8,128)(2,1)}), bf16[4352,512]{1,0:T(8,128)(2,1)}) %all-gather.3.cloned.1.call-update) | async-done | bytes 4456464 | tf_op jit(solution)/shard_map/all_gather | solution.py:82
  176.5 6.5 copy.45
  183.0 9.2 copy.48
  192.2 144.8 %all-gather.5.cloned.1.call-done = bf16[4352,512]{1,0:T(8,128)(2,1)} async-done(((bf16[136,512]{1,0:T(8,128)(2,1)}), bf16[4352,512]{1,0:T(8,128)(2,1)}) %all-gather.5.cloned.1.call-update) | async-done | bytes 4456464 | tf_op jit(solution)/shard_map/all_gather | solution.py:83
  337.1 6.5 copy.46
  343.5 9.2 copy.49
  352.7 31.7 %while.26 = (s32[]{:T(128)}, bf16[8,136,64]{1,2,0:T(8,128)(2,1)S(1)}, bf16[8,136,64]{2,1,0:T(8,128)(2,1)S(1)}, bf16[8,4352,64]{2,1,0:T(8,128)(2,1)}, bf16[8,4352...) while((s32[]{:T(128)}, bf16[8,136,64]{1,2,0:T(8,128)(2,1)S(1)}, ...), condition=%wide.region_5.6_spmd.clone, body=%wide.region_3.5_spmd.clone.sunk | while | flops 155079040 | bytes 7055989 | solution.py:104
  352.7 2.0 fusion.137
  356.7 2.0 fusion.137
  360.7 2.0 fusion.137
  364.6 2.0 fusion.137
  368.6 2.0 fusion.137
  372.5 2.0 fusion.137
  376.5 2.0 fusion.137
  380.5 2.0 fusion.137
  394.2 76.1 %while.27 = (s32[]{:T(128)}, f32[8,136,64]{1,2,0:T(8,128)}, bf16[8,4352,64]{1,2,0:T(8,128)(2,1)}, bf16[8,4352,64]{1,2,0:T(8,128)(2,1)}, bf16[8,136,64]{2,1,0:T(8...) while((s32[]{:T(128)}, f32[8,136,64]{1,2,0:T(8,128)}, ...), condition=%wide.region_9.10_spmd.clone, body=%wide.region_7.9_spmd.clone.sunk | while | flops 385003904 | bytes 16456953 | solution.py:137
  394.2 2.0 fusion.147
  399.3 2.0 fusion.150
  401.3 2.5 fusion.149
  403.8 2.0 fusion.147
  410.8 2.5 fusion.149
  413.2 2.0 fusion.147
  420.2 2.5 fusion.149
  422.7 2.0 fusion.147
  429.7 2.5 fusion.149
  432.2 2.0 fusion.147
  439.3 2.5 fusion.149
  441.8 2.0 fusion.147
  448.8 2.5 fusion.149
  451.3 2.0 fusion.147
  458.3 2.5 fusion.149
  460.8 2.0 fusion.147
  467.8 2.5 fusion.149
  470.3 6.6 copy.56
  476.9 6.5 copy.58
  486.5 2.1 convolution_convert_fusion
  488.8 158.3 %reduce-scatter.19.cloned.1.call-done = bf16[136,512]{1,0:T(8,128)(2,1)} async-done(((bf16[4352,512]{1,0:T(8,128)(2,1)}), bf16[136,512]{1,0:T(8,128)(2,1)}) %reduce-scatter.19.cloned.1.call-update) | async-done | bytes 139280
  653.4 161.8 %reduce-scatter.21.cloned.1.call-done = bf16[136,512]{1,0:T(8,128)(2,1)} async-done(((bf16[4352,512]{1,0:T(8,128)(2,1)}), bf16[136,512]{1,0:T(8,128)(2,1)}) %reduce-scatter.21.cloned.1.call-update) | async-done | bytes 139280
  818.7 2.2 collective-permute-done
  822.5 5.4 collective-permute-done.1
  827.9 8.1 collective-permute-done.2
  836.1 6.9 collective-permute-done.3
  843.0 133.7 %reduce-scatter.11.cloned.1.call-done = bf16[32,512]{1,0:T(8,128)(2,1)} async-done(((bf16[1024,512]{1,0:T(8,128)(2,1)}), bf16[32,512]{1,0:T(8,128)(2,1)}) %reduce-scatter.11.cloned.1.call-update) | async-done | bytes 32784 | tf_op jit(solution)/shard_map/reduce_scatter | solution.py:165
  978.2 161.6 %reduce-scatter.17.cloned.1.call-done = bf16[16,2048]{1,0:T(8,128)(2,1)} async-done(((bf16[512,2048]{1,0:T(8,128)(2,1)}), bf16[16,2048]{1,0:T(8,128)(2,1)}) %reduce-scatter.17.cloned.1.call-update) | async-done | bytes 65552 | tf_op jit(solution)/shard_map/reduce_scatter | solution.py:174
  1143.0 157.0 %reduce-scatter.13.cloned.1.call-done = bf16[32,512]{1,0:T(8,128)(2,1)} async-done(((bf16[1024,512]{1,0:T(8,128)(2,1)}), bf16[32,512]{1,0:T(8,128)(2,1)}) %reduce-scatter.13.cloned.1.call-update) | async-done | bytes 32784 | tf_op jit(solution)/shard_map/reduce_scatter | solution.py:168
  1301.4 158.3 %reduce-scatter.15.cloned.1.call-done = bf16[32,512]{1,0:T(8,128)(2,1)} async-done(((bf16[1024,512]{1,0:T(8,128)(2,1)}), bf16[32,512]{1,0:T(8,128)(2,1)}) %reduce-scatter.15.cloned.1.call-update) | async-done | bytes 32784 | tf_op jit(solution)/shard_map/reduce_scatter | solution.py:171
  (160 shorter events, 95.9 us)
Async XLA Ops:
  7.2 379.8 %copy-start = (bf16[1,512,2048]{2,1,0:T(8,128)(2,1)S(1)}, bf16[1,512,2048]{2,1,0:T(8,128)(2,1)}, u32[]{:S(2)}) copy-start(bf16[1,512,2048]{2,1,0:T(8,128)(2,1)} %param.17) | copy-start | bytes 6291460
  7.2 3.6 copy-start.2
  7.2 169.3 %all-gather.3.cloned.1.call-start = ((), (), s32[]{:S(2)}) async-start(), calls=%async_computation.6 | async-start | bytes 4595712 | tf_op jit(solution)/shard_map/all_gather | solution.py:82
  10.8 7.6 copy-start.7
  12.7 0.8 copy-start.3
  16.0 321.1 %all-gather.5.cloned.1.call-start = ((), (), s32[]{:S(2)}) async-start(), calls=%async_computation.7 | async-start | bytes 4595712 | tf_op jit(solution)/shard_map/all_gather | solution.py:83
  18.3 628.8 %reduce-scatter.19.cloned.1.call-start = ((), (), s32[]{:S(2)}) async-start(), calls=%async_computation.12 | async-start | bytes 4595712
  18.4 4.2 copy-start.23
  21.5 0.8 copy-start.5
  343.5 9.2 copy-start.21
  384.4 0.7 copy-start.19
  385.3 0.7 copy-start.9
  389.5 0.7 copy-start.15
  389.5 0.8 copy-start.17
  476.9 338.3 %reduce-scatter.21.cloned.1.call-start = ((), (), s32[]{:S(2)}) async-start(), calls=%async_computation.13 | async-start | bytes 4595712
  483.4 1.0 copy-start.6
  483.4 1.2 copy-start.12
  483.4 493.3 %reduce-scatter.11.cloned.1.call-start = ((), (), s32[]{:S(2)}) async-start(), calls=%async_computation.8 | async-start | bytes 1081344 | tf_op jit(solution)/shard_map/reduce_scatter | solution.py:165
  484.6 1.8 copy-start.13
  484.6 1.8 copy-start.16
  484.6 1.9 copy-start.18
  486.4 161.8 %copy-start.4 = (f32[136,8,64]{0,2,1:T(8,128)S(1)}, f32[136,8,64]{0,2,1:T(8,128)}, u32[]{:S(2)}) copy-start(f32[136,8,64]{0,2,1:T(8,128)} %copy-done.3) | copy-start | bytes 835588
  486.4 653.4 %reduce-scatter.17.cloned.1.call-start = ((), (), s32[]{:S(2)}) async-start(), calls=%async_computation.11 | async-start | bytes 2162688 | tf_op jit(solution)/shard_map/reduce_scatter | solution.py:174
  488.6 162.2 %copy-start.8 = (bf16[1,1024,512]{2,1,0:T(8,128)(2,1)S(1)}, bf16[1,1024,512]{2,1,0:T(8,128)(2,1)}, u32[]{:S(2)}) copy-start(bf16[1,1024,512]{2,1,0:T(8,128)(2,1)} %param.14) | copy-start | bytes 3145732
  488.6 811.4 %reduce-scatter.13.cloned.1.call-start = ((), (), s32[]{:S(2)}) async-start(), calls=%async_computation.9 | async-start | bytes 1081344 | tf_op jit(solution)/shard_map/reduce_scatter | solution.py:168
  648.4 0.7 copy-start.10
  650.7 0.9 copy-start.11
  650.7 809.0 %reduce-scatter.15.cloned.1.call-start = ((), (), s32[]{:S(2)}) async-start(), calls=%async_computation.10 | async-start | bytes 1081344 | tf_op jit(solution)/shard_map/reduce_scatter | solution.py:171
  651.6 165.5 %copy-start.14 = (bf16[1,136,1024]{2,1,0:T(8,128)(2,1)S(1)}, bf16[1,136,1024]{2,1,0:T(8,128)(2,1)}, u32[]{:S(2)}) copy-start(bf16[1,136,1024]{2,1,0:T(8,128)(2,1)} %param.13) | copy-start | bytes 835588
  815.2 5.7 copy-start.20
  817.1 18.9 %copy-start.22 = (s32[1,136]{1,0:T(1,128)S(1)}, s32[1,136]{1,0:T(1,128)}, u32[]{:S(2)}) copy-start(s32[1,136]{1,0:T(1,128)} %param.19) | copy-start | bytes 1636
  817.4 3.5 collective-permute-start
  820.9 7.0 collective-permute-start.1
  820.9 640.2 %copy-start.1 = (bf16[1,512,2048]{2,1,0:T(8,128)(2,1)S(1)}, bf16[1,512,2048]{2,1,0:T(8,128)(2,1)}, u32[]{:S(2)}) copy-start(bf16[1,512,2048]{2,1,0:T(8,128)(2,1)} %param.17) | copy-start | bytes 6291460
  827.9 8.1 collective-permute-start.2
  836.1 6.9 collective-permute-start.3
  843.0 135.1 %collective-permute-start.4 = (bf16[136,1024]{1,0:T(8,128)(2,1)S(1)}, bf16[136,1024]{1,0:T(8,128)(2,1)S(1)}, u32[]{:S(2)}, u32[]{:S(2)}) collective-permute-start(bf16[136,1024]{1,0:T(8,128)(2,1)S(1)} %collective-permute-done.3), channel_id=1, source_target_pairs={{0,8},{8,0},{1,9},{9,1},{2,10},{10,2},{3,11},{11,3},{4,12},{12,4},... | collective-permute-start | bytes 835592 | tf_op jit(solution)/shard_map/ppermute | solution.py:20
  978.2 163.2 %collective-permute-start.5 = (bf16[136,1024]{1,0:T(8,128)(2,1)S(1)}, bf16[136,1024]{1,0:T(8,128)(2,1)S(1)}, u32[]{:S(2)}, u32[]{:S(2)}) collective-permute-start(bf16[136,1024]{1,0:T(8,128)(2,1)S(1)} %collective-permute-done.4), channel_id=1, source_target_pairs={{0,16},{16,0},{1,17},{17,1},{2,18},{18,2},{3,19},{19,3},{4,20},{20... | collective-permute-start | bytes 835592 | tf_op jit(solution)/shard_map/ppermute | solution.py:20
Sparse Core Ops, SparseCore 0:
  16.1 160.3 all-gather.2
  178.2 158.8 all-gather.4
  477.0 170.0 reduce-scatter.18
  649.5 165.6 reduce-scatter.20
  817.4 159.3 reduce-scatter.10
  979.1 160.6 reduce-scatter.16
  1142.2 157.7 reduce-scatter.12
  1302.4 157.1 reduce-scatter.14
where the time goes:
time: 1470 us
  waiting for transfers between devices  1250 us (85%)
  matrix products  127 us (9%)
  local copies, waits for them, and re-layouts  60.4 us (4%)
    unnamed x10, waiting for transfers between devices  320 us
    reduce_scatter x1, waiting for transfers between devices, shards(): lax.psum_scatter(out_term.astype(jnp.bfloat16), 'seq', scatter_dimension=...  162 us
    reduce_scatter x1, waiting for transfers between devices, shards(): lax.psum_scatter(value_term.astype(jnp.bfloat16), 'seq', scatter_dimensio...  158 us
    reduce_scatter x1, waiting for transfers between devices, shards(): lax.psum_scatter(key_term.astype(jnp.bfloat16), 'seq', scatter_dimension=...  157 us
    all_gather x1, waiting for transfers between devices, shards(): lax.all_gather(keys, 'seq', axis=0, tiled=True)  154 us
    all_gather x1, waiting for transfers between devices, shards(): lax.all_gather(values, 'seq', axis=0, tiled=True)  145 us
    reduce_scatter x1, waiting for transfers between devices, shards(): lax.psum_scatter(query_term.astype(jnp.bfloat16), 'seq', scatter_dimensio...  134 us
    unnamed x58, local copies, waits for them, and re-layouts  42.5 us
  transfers between devices with their start and end apart: 14, of which 12 were waited for; matrix products, arithmetic and copies ran while one was open for 3% of the time, Pallas kernels for 0%

commit v1 on v0

v1 whole, which is shorter than its diff:
```python
import jax
import jax.numpy as jnp
from jax import lax
from jax.experimental import pallas as pl
from jax.experimental.pallas import tpu as pltpu
from jax.sharding import PartitionSpec as P

HEADS = 8
HEAD_DIM = 64
EPSILON = 1e-06
N_SEQ = 32
TOK = 136
TOKENS = 4352
D = 1024
INNER = 512
KT = 256
REACH = TOK + 255
BF = jnp.bfloat16
F32 = jnp.float32
MESH = pl.DeviceIdType.MESH
VMEM = pl.BlockSpec(memory_space=pltpu.VMEM)
ANY = pl.BlockSpec(memory_space=pl.ANY)
BIG = 60 * 1024 * 1024


def dot(a, b):
    return jnp.dot(a, b, preferred_element_type=F32)


def dot_t(a, b):
    return lax.dot_general(a, b, (((1,), (1,)), ((), ())), preferred_element_type=F32)


def left_half(shape):
    return lax.broadcasted_iota(jnp.int32, shape, 1) < HEAD_DIM


def swap(slab):
    return pltpu.roll(slab, HEAD_DIM, 1)


def per_head_sum(slab, left):
    low = jnp.sum(jnp.where(left, slab, 0.0), axis=-1, keepdims=True)
    high = jnp.sum(jnp.where(left, 0.0, slab), axis=-1, keepdims=True)
    return jnp.where(left, low, high)


def unit_scale(slab, left):
    return lax.rsqrt(per_head_sum(slab * slab, left) * (1.0 / HEAD_DIM) + EPSILON)


def project_body(act, wq, wk, wv, normed, q_raw, k_raw, q_pack, kv_pack):
    field = act[...].astype(F32)
    scale = lax.rsqrt(jnp.mean(field * field, axis=-1, keepdims=True) + EPSILON)
    normed[...] = (field * scale).astype(BF)
    left = left_half((TOK, 128))
    for block in range(2):
        columns = pl.ds(256 * block, 256)
        q = dot(normed[...], wq[:, columns])
        k = dot(normed[...], wk[:, columns])
        v = dot(normed[...], wv[:, columns])
        q_raw[:, columns] = q
        k_raw[:, columns] = k
        for half in range(2):
            head = 4 * block + 2 * half
            q_slab = q[:, 128 * half : 128 * half + 128]
            k_slab = k[:, 128 * half : 128 * half + 128]
            v_slab = v[:, 128 * half : 128 * half + 128]
            q_slab = (q_slab * unit_scale(q_slab, left)).astype(BF).astype(F32) * 0.125
            k_slab = k_slab * unit_scale(k_slab, left)
            q_pack[head] = jnp.where(left, q_slab, 0.0).astype(BF)
            q_pack[head + 1] = jnp.where(left, swap(q_slab), 0.0).astype(BF)
            kv_pack[head] = jnp.where(left, k_slab, swap(v_slab)).astype(BF)
            kv_pack[head + 1] = jnp.where(left, swap(k_slab), v_slab).astype(BF)


def tile_bounds(first):
    whole = lax.div(first, KT)
    end = lax.min(lax.div(first + REACH + KT - 1, KT), TOKENS // KT)
    return whole, end


def forward_body(q_all, kv, q_ids, k_ids, out, inverse):
    group = lax.rem(lax.axis_index("seq"), 4)

    def chunk(i, _):
        whole, end = tile_bounds((4 * i + group) * TOK)
        q = q_all[i]
        ids = q_ids[i]

        def tile(j, carry, masked):
            total, mass = carry
            block = kv[pl.ds(pl.multiple_of(j * KT, KT), KT), :]
            p = jnp.exp(dot_t(q, block))
            if masked:
                p = jnp.where(k_ids[j] <= ids, p, 0.0)
            mass = mass + (p[:, :128] + p[:, 128:])
            total = total + dot(p.astype(BF), block)
            return total, mass

        zero = jnp.zeros((TOK, 128), F32)
        carry = lax.fori_loop(0, whole, lambda j, c: tile(j, c, False), (zero, zero))
        total, mass = lax.fori_loop(whole, end, lambda j, c: tile(j, c, True), carry)
        one_over = 1.0 / jnp.sum(mass, axis=-1, keepdims=True)
        out[i] = (total * one_over).astype(BF)
        inverse[i] = jnp.broadcast_to(one_over, (TOK, 128))
        return 0

    lax.fori_loop(0, HEADS, chunk, 0)


def backward_body(q_all, g_all, out, inverse, kv, q_ids, k_ids, dq, dkv, total):
    group = lax.rem(lax.axis_index("seq"), 4)
    total[...] = jnp.zeros_like(total)

    def chunk(i, _):
        whole, end = tile_bounds((4 * i + group) * TOK)
        q = q_all[i]
        g = g_all[i]
        ids = q_ids[i]
        one_over = inverse[i][:, :1]
        correction = jnp.sum(g.astype(F32) * out[i].astype(F32), axis=-1, keepdims=True)
        q_turned = jnp.transpose(q.astype(F32))[:HEAD_DIM].astype(BF)
        g_turned = jnp.transpose(g.astype(F32))[HEAD_DIM:].astype(BF)

        def tile(j, acc, masked):
            at = pl.ds(pl.multiple_of(j * KT, KT), KT)
            block = kv[at, :]
            p = jnp.exp(dot_t(q, block)) * one_over
            if masked:
                p = jnp.where(k_ids[j] <= ids, p, 0.0)
            ds = (p * (dot_t(g, block) - correction)).astype(BF)
            total[:HEAD_DIM, at] += dot(q_turned, ds)
            total[HEAD_DIM:, at] += dot(g_turned, p.astype(BF))
            return acc + dot(ds, block)

        acc = jnp.zeros((TOK, 128), F32)
        acc = lax.fori_loop(0, whole, lambda j, c: tile(j, c, False), acc)
        acc = lax.fori_loop(whole, end, lambda j, c: tile(j, c, True), acc)
        dq[i] = (acc * 0.125).astype(BF)
        return 0

    lax.fori_loop(0, HEADS, chunk, 0)

    def turn(j, _):
        at = pl.ds(pl.multiple_of(j * KT, KT), KT)
        dkv[at, :] = jnp.transpose(total[:, at]).astype(BF)
        return 0

    lax.fori_loop(0, TOKENS // KT, turn, 0)


def affine_body(act, up, att_all, w_out, g_pack, carry_part, out_term, att, att_turned, grad):
    left = left_half((TOK, 128))
    for pair in range(HEADS // 2):
        low = att_all[2 * pair].astype(F32)
        high = att_all[2 * pair + 1].astype(F32)
        slab = jnp.where(left, swap(low), high)
        att[:, 128 * pair : 128 * pair + 128] = slab.astype(BF)
        att_turned[128 * pair : 128 * pair + 128, :] = jnp.transpose(slab).astype(BF)
    for block in range(4):
        columns = pl.ds(256 * block, 256)
        behind = pl.ds(D + 256 * block, 256)
        shift = dot(att[...], w_out[:, columns])
        factor = jnp.exp(-dot(att[...], w_out[:, behind]))
        upstream = up[:, columns].astype(F32)
        latent = (act[:, columns].astype(F32) - shift) * factor
        scaled = upstream * factor
        carry_part[:, columns] = scaled
        grad[:, columns] = (-scaled).astype(BF)
        grad[:, behind] = (1.0 - upstream * latent).astype(BF)
    for block in range(2):
        g = dot_t(grad[...], w_out[pl.ds(256 * block, 256), :])
        for half in range(2):
            head = 4 * block + 2 * half
            slab = g[:, 128 * half : 128 * half + 128]
            g_pack[head] = jnp.where(left, 0.0, swap(slab)).astype(BF)
            g_pack[head + 1] = jnp.where(left, 0.0, slab).astype(BF)
    for block in range(8):
        columns = pl.ds(256 * block, 256)
        out_term[:, columns] = dot(att_turned[...], grad[:, columns]).astype(BF)


def finish_body(act, normed, carry_part, q_raw, k_raw, dq_all, dkv_parts, wq, wk, wv,
                grad_input, terms, grads, gn, normed_turned):
    left = left_half((TOK, 128))

    def unit_back(grad, raw):
        scale = unit_scale(raw, left)
        unit = raw * scale
        return scale * (grad - unit * (per_head_sum(grad * unit, left) * (1.0 / HEAD_DIM)))

    def keys_of(head):
        part = [dkv_parts[4 * head + i].astype(F32) for i in range(4)]
        return (part[0] + part[1]) + (part[2] + part[3])

    for pair in range(HEADS // 2):
        at = pl.ds(128 * pair, 128)
        low, high = dq_all[2 * pair].astype(F32), dq_all[2 * pair + 1].astype(F32)
        q_grad = jnp.where(left, low, swap(high))
        low, high = keys_of(2 * pair), keys_of(2 * pair + 1)
        k_grad = jnp.where(left, low, swap(high))
        v_grad = jnp.where(left, swap(low), high)
        grads[0, :, at] = unit_back(q_grad, q_raw[:, at]).astype(BF)
        grads[1, :, at] = unit_back(k_grad, k_raw[:, at]).astype(BF)
        grads[2, :, at] = v_grad.astype(BF)
    for block in range(8):
        at = pl.ds(128 * block, 128)
        normed_turned[at, :] = jnp.transpose(normed[:, at].astype(F32)).astype(BF)
    for block in range(4):
        at = pl.ds(256 * block, 256)
        gn[:, at] = dot_t(grads[0], wq[at, :]) + dot_t(grads[1], wk[at, :]) + dot_t(grads[2], wv[at, :])
    field = act[...].astype(F32)
    scale = lax.rsqrt(jnp.mean(field * field, axis=-1, keepdims=True) + EPSILON)
    unit = field * scale
    grad_normed = gn[...]
    mean = jnp.mean(grad_normed * unit, axis=-1, keepdims=True)
    grad_input[...] = (carry_part[...] + scale * (grad_normed - unit * mean)).astype(BF)
    for which in range(3):
        for block in range(2):
            terms[:, INNER * which + 256 * block : INNER * which + 256 * block + 256] = dot(
                normed_turned[...], grads[which, :, 256 * block : 256 * block + 256]
            ).astype(BF)


def local_call(body, outs, scratch=(), name=None):
    return pl.pallas_call(
        body,
        out_shape=[jax.ShapeDtypeStruct(shape, dtype) for shape, dtype in outs],
        out_specs=[VMEM] * len(outs),
        scratch_shapes=[pltpu.VMEM(shape, dtype) for shape, dtype in scratch],
        compiler_params=pltpu.CompilerParams(vmem_limit_bytes=BIG),
        name=name,
    )


def exchange(full, plane, by_head, identity, name):
    n_full, n_plane = (0 if full is None else 1), (0 if plane is None else 1)

    def body(*refs):
        refs = list(refs)
        sources = [refs.pop(0) for _ in range(n_full + n_plane)]
        targets = [refs.pop(0) for _ in range(n_full + n_plane)]
        full_send, full_recv, plane_send, plane_recv, local_sem = refs
        me = lax.axis_index("seq")
        mine = lax.div(me, 4)
        count, stride = (N_SEQ, 1) if n_full else (HEADS, 4)

        barrier = pltpu.get_barrier_semaphore()

        def greet(k, _):
            pl.semaphore_signal(barrier, inc=1, device_id={"seq": lax.rem(me + stride * k, N_SEQ)}, device_id_type=MESH)
            return 0

        lax.fori_loop(1, count, greet, 0)
        pl.semaphore_wait(barrier, count - 1)

        def full_copy(k):
            peer = lax.rem(me + k, N_SEQ)
            return pltpu.make_async_remote_copy(
                src_ref=sources[0].at[lax.div(peer, 4) if by_head else peer],
                dst_ref=targets[0].at[me],
                send_sem=full_send.at[k],
                recv_sem=full_recv.at[k],
                device_id={"seq": peer},
                device_id_type=MESH,
            )

        def plane_copy(k):
            peer = lax.rem(me + 4 * k, N_SEQ)
            return pltpu.make_async_remote_copy(
                src_ref=sources[-1].at[lax.div(peer, 4)],
                dst_ref=targets[-1].at[mine],
                send_sem=plane_send.at[k],
                recv_sem=plane_recv.at[k],
                device_id={"seq": peer},
                device_id_type=MESH,
            )

        local = []
        if n_plane:
            local.append(pltpu.make_async_copy(sources[-1].at[mine], targets[-1].at[mine], local_sem.at[1]))
            lax.fori_loop(1, HEADS, lambda k, c: (plane_copy(k).start(), c)[1], 0)
        if n_full:
            local.append(pltpu.make_async_copy(sources[0].at[mine if by_head else me], targets[0].at[me], local_sem.at[0]))
            lax.fori_loop(1, N_SEQ, lambda k, c: (full_copy(k).start(), c)[1], 0)
        for copy in local:
            copy.start()
        for copy in local:
            copy.wait()
        if n_plane:
            lax.fori_loop(1, HEADS, lambda k, c: (plane_copy(k).wait(), c)[1], 0)
        if n_full:
            lax.fori_loop(1, N_SEQ, lambda k, c: (full_copy(k).wait(), c)[1], 0)

    arrays, outs = [], []
    if n_full:
        arrays.append(full)
        outs.append(jax.ShapeDtypeStruct((N_SEQ, TOK, 128), BF))
    if n_plane:
        arrays.append(plane)
        outs.append(jax.ShapeDtypeStruct((HEADS, TOK, 128), BF))
    return pl.pallas_call(
        body,
        out_shape=outs,
        in_specs=[ANY] * len(arrays),
        out_specs=[ANY] * len(outs),
        scratch_shapes=[
            pltpu.SemaphoreType.DMA((N_SEQ,)),
            pltpu.SemaphoreType.DMA((N_SEQ,)),
            pltpu.SemaphoreType.DMA((HEADS,)),
            pltpu.SemaphoreType.DMA((HEADS,)),
            pltpu.SemaphoreType.DMA((2,)),
        ],
        compiler_params=pltpu.CompilerParams(collective_id=identity, has_side_effects=True),
        name=name,
    )(*arrays)


def sums_body(terms, out_term, rows, sums, out_sum, moved, parts, out_parts,
              send, recv, out_send, out_recv, local_sem, carry_sem):
    me = lax.axis_index("seq")
    section = lax.axis_index("section")
    before, after = lax.rem(section + 3, 4), lax.rem(section + 1, 4)
    across = N_SEQ - 1 - me
    barrier = pltpu.get_barrier_semaphore()

    def greet(k, _):
        pl.semaphore_signal(barrier, inc=1, device_id={"seq": lax.rem(me + k, N_SEQ)}, device_id_type=MESH)
        return 0

    lax.fori_loop(1, N_SEQ, greet, 0)
    for other in (before, after):
        pl.semaphore_signal(barrier, inc=1, device_id={"section": other, "seq": across}, device_id_type=MESH)
    pl.semaphore_wait(barrier, N_SEQ + 1)

    carry = pltpu.make_async_remote_copy(
        src_ref=rows, dst_ref=moved, send_sem=carry_sem.at[0], recv_sem=carry_sem.at[1],
        device_id={"section": before, "seq": across}, device_id_type=MESH,
    )
    carry.start()

    def term_copy(k):
        peer = lax.rem(me + k, N_SEQ)
        return pltpu.make_async_remote_copy(
            src_ref=terms.at[pl.ds(pl.multiple_of(peer * 32, 32), 32), :], dst_ref=parts.at[k],
            send_sem=send.at[k], recv_sem=recv.at[k], device_id={"seq": peer}, device_id_type=MESH,
        )

    def out_copy(k):
        peer = lax.rem(me + k, N_SEQ)
        return pltpu.make_async_remote_copy(
            src_ref=out_term.at[pl.ds(pl.multiple_of(peer * 16, 16), 16), :], dst_ref=out_parts.at[k],
            send_sem=out_send.at[k], recv_sem=out_recv.at[k], device_id={"seq": peer}, device_id_type=MESH,
        )

    def begin(k, _):
        term_copy(k).start()
        out_copy(k).start()
        return 0

    lax.fori_loop(1, N_SEQ, begin, 0)
    own = [
        pltpu.make_async_copy(terms.at[pl.ds(pl.multiple_of(me * 32, 32), 32), :], parts.at[0], local_sem.at[0]),
        pltpu.make_async_copy(out_term.at[pl.ds(pl.multiple_of(me * 16, 16), 16), :], out_parts.at[0], local_sem.at[1]),
    ]
    for copy in own:
        copy.start()
    for copy in own:
        copy.wait()
    sums[...] = parts[0].astype(F32)
    out_sum[...] = out_parts[0].astype(F32)

    def add(k, _):
        term_copy(k).wait()
        sums[...] += parts[k].astype(F32)
        out_copy(k).wait()
        out_sum[...] += out_parts[k].astype(F32)
        return 0

    lax.fori_loop(1, N_SEQ, add, 0)
    carry.wait()


def reduce_terms(terms, out_term, rows):
    return pl.pallas_call(
        sums_body,
        out_shape=[
            jax.ShapeDtypeStruct((32, 3 * INNER), F32),
            jax.ShapeDtypeStruct((16, 2 * D), F32),
            jax.ShapeDtypeStruct((TOK, D), BF),
        ],
        in_specs=[ANY, ANY, ANY],
        out_specs=[VMEM, VMEM, ANY],
        scratch_shapes=[
            pltpu.VMEM((N_SEQ, 32, 3 * INNER), BF),
            pltpu.VMEM((N_SEQ, 16, 2 * D), BF),
            pltpu.SemaphoreType.DMA((N_SEQ,)),
            pltpu.SemaphoreType.DMA((N_SEQ,)),
            pltpu.SemaphoreType.DMA((N_SEQ,)),
            pltpu.SemaphoreType.DMA((N_SEQ,)),
            pltpu.SemaphoreType.DMA((2,)),
            pltpu.SemaphoreType.DMA((2,)),
        ],
        compiler_params=pltpu.CompilerParams(
            collective_id=5, has_side_effects=True, vmem_limit_bytes=BIG
        ),
        name="sums",
    )(terms, out_term, rows)


def shards(activations, incoming, w_query, w_key, w_value, w_out, block_ids, flip_order):
    act, up = activations[0], incoming[0]
    wq, wk, wv, wo = w_query[0], w_key[0], w_value[0], w_out[0]
    group = lax.rem(lax.axis_index("seq"), 4)
    by_chunk = block_ids.reshape(HEADS, 4, TOK)
    q_ids = lax.dynamic_index_in_dim(by_chunk, group, 1, keepdims=False)[:, :, None]
    k_ids = block_ids.reshape(TOKENS // KT, 1, KT)

    normed, q_raw, k_raw, q_pack, kv_pack = local_call(
        project_body,
        [((TOK, D), BF), ((TOK, INNER), F32), ((TOK, INNER), F32), ((HEADS, TOK, 128), BF), ((HEADS, TOK, 128), BF)],
        name="project",
    )(act, wq, wk, wv)
    kv_all, q_all = exchange(kv_pack, q_pack, True, 1, "spread")
    kv = kv_all.reshape(TOKENS, 128)
    out, inverse = local_call(
        forward_body, [((HEADS, TOK, 128), BF), ((HEADS, TOK, 128), F32)], name="attend"
    )(q_all, kv, q_ids, k_ids)
    (att_all,) = exchange(None, out, True, 2, "attended")
    g_pack, carry_part, out_term = local_call(
        affine_body,
        [((HEADS, TOK, 128), BF), ((TOK, D), F32), ((INNER, 2 * D), BF)],
        [((TOK, INNER), BF), ((INNER, TOK), BF), ((TOK, 2 * D), BF)],
        name="affine",
    )(act, up, att_all, wo)
    (g_all,) = exchange(None, g_pack, True, 3, "grad_attn")
    dq, dkv = local_call(
        backward_body,
        [((HEADS, TOK, 128), BF), ((TOKENS, 128), BF)],
        [((128, TOKENS), F32)],
        name="attend_back",
    )(q_all, g_all, out, inverse, kv, q_ids, k_ids)
    dkv_parts, dq_all = exchange(dkv.reshape(N_SEQ, TOK, 128), dq, False, 4, "gather_grads")
    grad_input, terms = local_call(
        finish_body,
        [((TOK, D), BF), ((D, 3 * INNER), BF)],
        [((3, TOK, INNER), BF), ((TOK, D), F32), ((D, TOK), BF)],
        name="finish",
    )(act, normed, carry_part, q_raw, k_raw, dq_all, dkv_parts, wq, wk, wv)
    sums, out_sum, moved = reduce_terms(terms, out_term, grad_input)
    carry = jnp.take(moved, flip_order[0], axis=0)
    carry = jnp.where(lax.axis_index("section") == 3, jnp.zeros_like(carry), carry)
    return (
        carry[None],
        sums[None, :, :INNER],
        sums[None, :, INNER : 2 * INNER],
        sums[None, :, 2 * INNER :],
        out_sum[None],
    )


def solution(mesh):
    by_both = P("section", "seq", None)
    by_layer = P("section", None, None)
    in_specs = (by_both, by_both, by_layer, by_layer, by_layer, by_layer, P(), P("section", None))
    return jax.shard_map(shards, mesh=mesh, in_specs=in_specs, out_specs=(by_both,) * 5, check_vma=False)
```

time: 1470 us -> 272 us (0.19)
  the two profiles are of different devices: /device:TPU:0 before, /device:TPU:97 now
where the time goes in v1:
time: 272 us
  Pallas kernels  264 us (97%)
  local copies, waits for them, and re-layouts  6 us (2%)
    pallas_call x1, Pallas kernels, reduce_terms(): pl.pallas_call(sums_body, out_shape=[jax.ShapeDtypeStruct((32, 3 * INNER)...  119 us
    pallas_call x4, Pallas kernels, exchange(): pl.pallas_call(body, out_shape=outs, in_specs=[ANY] * len(arrays), out_sp...  60.2 us
    pallas_call x1, Pallas kernels, shards(): local_call(backward_body, [((HEADS, TOK, 128), BF), ((TOKENS, 128), BF)],...  37.8 us
    pallas_call x1, Pallas kernels, shards(): local_call(forward_body, [((HEADS, TOK, 128), BF), ((HEADS, TOK, 128), F3...  30.7 us
    pallas_call x1, Pallas kernels, shards(): local_call(finish_body, [((TOK, D), BF), ((D, 3 * INNER), BF)], [((3, TOK...  7.79 us

profile of v1, /device:TPU:97, one launch (start us, length us, event | category | flops | bytes accessed | tf_op | source)
XLA Modules:
  0.0 271.8 jit_solution(6489574028049530400)
XLA Ops:
  0.6 0.8 reshape.84
  1.5 1.0 broadcast_in_dim.37.q_ids
  2.5 0.0 copy-start.2
  2.5 3.9 %project.1 = (bf16[136,1024]{1,0:T(8,128)(2,1)}, f32[136,512]{1,0:T(8,128)}, f32[136,512]{1,0:T(8,128)}, bf16[8,136,128]{2,1,0:T(8,128)(2,1)}, bf16[8,136,128]{2,1,0:T(8,128)(2,1)}) custom-call(bf16[136,1024]{1,0:T(8,128)(2,1)} %bitcast.31, bf16[1024,512]{1,0:T(8,128)(2,1)} %bitcast.25, bf16[1024,512]{1,0:T(8,128)(2,1)} %bitcast.27, bf16[1024,512]{1,0:T(8,128)(2,1)} %bitcast.29), custom_call_target="tpu_custom_call" | custom-call | tf_op jit(solution)/shard_map/project/pallas_call | solution.py:420
  6.5 27.4 %spread.1 = (bf16[32,136,128]{2,1,0:T(8,128)(2,1)}, bf16[8,136,128]{2,1,0:T(8,128)(2,1)}) custom-call(bf16[8,136,128]{2,1,0:T(8,128)(2,1)} %get-tuple-element.27.refs_0_, bf16[8,136,128]{2,1,0:T(8,128)(2,1)} %get-tuple-element.28.refs_1_), custom_call_target="tpu_custom_call" | custom-call | tf_op jit(solution)/shard_map/spread/pallas_call | solution.py:303
  33.8 0.0 copy-done.2
  33.8 0.6 reshape.85.k_ids
  34.5 30.7 %attend.1 = (bf16[8,136,128]{2,1,0:T(8,128)(2,1)}, f32[8,136,128]{2,1,0:T(8,128)}) custom-call(bf16[8,136,128]{2,1,0:T(8,128)(2,1)} %get-tuple-element.29.q_all, bf16[4352,128]{1,0:T(8,128)(2,1)} %bitcast.23, s32[8,136,1]{2,1,0:T(8,128)} %broadcast_in_dim.37.q_ids, s32[17,1,256]{2,1,0:T(1,128)} %reshape.85.k_ids), custom_call_target="tpu_custom_call" | custom-call | tf_op jit(solution)/shard_map/attend/pallas_call | solution.py:427
  65.2 7.0 %attended.1.att_all = bf16[8,136,128]{2,1,0:T(8,128)(2,1)} custom-call(bf16[8,136,128]{2,1,0:T(8,128)(2,1)} %get-tuple-element.31.refs_0_.out), custom_call_target="tpu_custom_call" | custom-call | tf_op jit(solution)/shard_map/attended/pallas_call | solution.py:303
  72.2 5.1 %affine.1 = (bf16[8,136,128]{2,1,0:T(8,128)(2,1)}, f32[136,1024]{1,0:T(8,128)}, bf16[512,2048]{1,0:T(8,128)(2,1)}) custom-call(bf16[136,1024]{1,0:T(8,128)(2,1)} %bitcast.32, bf16[136,1024]{1,0:T(8,128)(2,1)} %bitcast.36, bf16[8,136,128]{2,1,0:T(8,128)(2,1)} %attended.1.att_all, bf16[512,2048]{1,0:T(8,128)(2,1)} %bitcast.34), custom_call_target="tpu_custom_call" | custom-call | tf_op jit(solution)/shard_map/affine/pallas_call | solution.py:431
  77.2 6.9 %grad_attn.1.g_all = bf16[8,136,128]{2,1,0:T(8,128)(2,1)} custom-call(bf16[8,136,128]{2,1,0:T(8,128)(2,1)} %get-tuple-element.35.refs_0_), custom_call_target="tpu_custom_call" | custom-call | tf_op jit(solution)/shard_map/grad_attn/pallas_call | solution.py:303
  84.1 37.8 %attend_back.1 = (bf16[8,136,128]{2,1,0:T(8,128)(2,1)}, bf16[4352,128]{1,0:T(8,128)(2,1)}) custom-call(bf16[8,136,128]{2,1,0:T(8,128)(2,1)} %get-tuple-element.29.q_all, bf16[8,136,128]{2,1,0:T(8,128)(2,1)} %grad_attn.1.g_all, bf16[8,136,128]{2,1,0:T(8,128)(2,1)} %get-tuple-element.31.refs_0_.out, f32[8,136,128]{2,1,0:T(8,128)} %get-tuple-element.36.inverse, ...), custom_call_target="tpu_custom_call" | custom-call | tf_op jit(solution)/shard_map/attend_back/pallas_call | solution.py:438
  121.9 18.9 %gather_grads.1 = (bf16[32,136,128]{2,1,0:T(8,128)(2,1)}, bf16[8,136,128]{2,1,0:T(8,128)(2,1)}) custom-call(bf16[32,136,128]{2,1,0:T(8,128)(2,1)} %bitcast.35, bf16[8,136,128]{2,1,0:T(8,128)(2,1)} %get-tuple-element.38.refs_1_), custom_call_target="tpu_custom_call" | custom-call | tf_op jit(solution)/shard_map/gather_grads/pallas_call | solution.py:303
  140.8 7.8 %finish.1 = (bf16[136,1024]{1,0:T(8,128)(2,1)}, bf16[1024,1536]{1,0:T(8,128)(2,1)}) custom-call(bf16[136,1024]{1,0:T(8,128)(2,1)} %bitcast.33, bf16[136,1024]{1,0:T(8,128)(2,1)} %get-tuple-element.26.normed, f32[136,1024]{1,0:T(8,128)} %get-tuple-element.32.carry_part, f32[136,512]{1,0:T(8,128)} %get-tuple-element.33.q_raw, ...), custom_call_target="tpu_custom_call" | custom-call | tf_op jit(solution)/shard_map/finish/pallas_call | solution.py:445
  148.6 0.0 copy-start.3
  148.6 118.8 %sums.1 = (f32[32,1536]{1,0:T(8,128)}, f32[16,2048]{1,0:T(8,128)}, bf16[136,1024]{1,0:T(8,128)(2,1)}) custom-call(bf16[1024,1536]{1,0:T(8,128)(2,1)} %get-tuple-element.41.terms, bf16[512,2048]{1,0:T(8,128)(2,1)} %get-tuple-element.42.out_term, bf16[136,1024]{1,0:T(8,128)(2,1)} %get-tuple-element.43.rows), custom_call_target="tpu_custom_call" | custom-call | tf_op jit(solution)/shard_map/sums/pallas_call | solution.py:386
  267.4 0.0 copy-start
  267.4 0.0 copy-start.1
  267.4 0.0 copy-done.3
  267.5 2.1 gather_fusion
  269.7 0.8 fusion
  270.5 0.0 copy-done
  270.5 0.7 slice_bitcast_fusion
  271.1 0.0 copy-done.1
  271.1 0.7 copy.16
  (4 shorter events, 0.0 us)
Async XLA Ops:
  2.5 31.3 %copy-start.2 = (s32[4352]{0:T(1024)S(1)}, s32[4352]{0:T(1024)}, u32[]{:S(2)}) copy-start(s32[4352]{0:T(1024)} %param.14) | copy-start | bytes 52228
  148.6 118.8 %copy-start.3 = (s32[1,136]{1,0:T(1,128)S(1)}, s32[1,136]{1,0:T(1,128)}, u32[]{:S(2)}) copy-start(s32[1,136]{1,0:T(1,128)} %param.15) | copy-start | bytes 1636
  267.4 3.0 %copy-start = (f32[32,1536]{1,0:T(8,128)S(1)}, f32[32,1536]{1,0:T(8,128)}, u32[]{:S(2)}) copy-start(f32[32,1536]{1,0:T(8,128)} %get-tuple-element.45) | copy-start | bytes 589828
  267.4 3.7 %copy-start.1 = (f32[16,2048]{1,0:T(8,128)S(1)}, f32[16,2048]{1,0:T(8,128)}, u32[]{:S(2)}) copy-start(f32[16,2048]{1,0:T(8,128)} %get-tuple-element.46) | copy-start | bytes 393220

commit v2 on v1

--- a/solution.py
+++ b/solution.py
@@ -14,7 +14,7 @@
 D = 1024
 INNER = 512
 KT = 256
-REACH = TOK + 255
+WIDE = 512
 BF = jnp.bfloat16
 F32 = jnp.float32
 MESH = pl.DeviceIdType.MESH
@@ -74,73 +74,67 @@
             kv_pack[head + 1] = jnp.where(left, swap(k_slab), v_slab).astype(BF)
 
 
-def tile_bounds(first):
-    whole = lax.div(first, KT)
-    end = lax.min(lax.div(first + REACH + KT - 1, KT), TOKENS // KT)
-    return whole, end
-
-
 def forward_body(q_all, kv, q_ids, k_ids, out, inverse):
-    group = lax.rem(lax.axis_index("seq"), 4)
-
-    def chunk(i, _):
-        whole, end = tile_bounds((4 * i + group) * TOK)
-        q = q_all[i]
-        ids = q_ids[i]
-
-        def tile(j, carry, masked):
+    def pair(a, last):
+        rows = pl.ds(2 * TOK * a if last else pl.multiple_of(2 * TOK * a, 2 * TOK), 2 * TOK)
+        q = q_all[rows, :]
+
+        def tile(j, carry, masked, width=WIDE):
             total, mass = carry
-            block = kv[pl.ds(pl.multiple_of(j * KT, KT), KT), :]
+            block = kv[pl.ds(j * WIDE if last and masked else pl.multiple_of(j * WIDE, WIDE), width), :]
             p = jnp.exp(dot_t(q, block))
             if masked:
-                p = jnp.where(k_ids[j] <= ids, p, 0.0)
-            mass = mass + (p[:, :128] + p[:, 128:])
+                p = jnp.where(k_ids[j][:, :width] <= q_ids[rows, :], p, 0.0)
+            for part in range(width // 128):
+                mass = mass + p[:, 128 * part : 128 * part + 128]
             total = total + dot(p.astype(BF), block)
             return total, mass
 
-        zero = jnp.zeros((TOK, 128), F32)
-        carry = lax.fori_loop(0, whole, lambda j, c: tile(j, c, False), (zero, zero))
-        total, mass = lax.fori_loop(whole, end, lambda j, c: tile(j, c, True), carry)
+        zero = jnp.zeros((2 * TOK, 128), F32)
+        carry = lax.fori_loop(0, 2 * a, lambda j, c: tile(j, c, False), (zero, zero))
+        carry = tile(2 * a, carry, True)
+        carry = tile(2 * a + 1, carry, True)
+        total, mass = tile(2 * a + 2, carry, True, WIDE // 2 if last else WIDE)
         one_over = 1.0 / jnp.sum(mass, axis=-1, keepdims=True)
-        out[i] = (total * one_over).astype(BF)
-        inverse[i] = jnp.broadcast_to(one_over, (TOK, 128))
-        return 0
-
-    lax.fori_loop(0, HEADS, chunk, 0)
+        out[rows, :] = (total * one_over).astype(BF)
+        inverse[rows, :] = jnp.broadcast_to(one_over, (2 * TOK, 128))
+
+    lax.fori_loop(0, 3, lambda a, c: (pair(a, False), c)[1], 0)
+    pair(3, True)
 
 
 def backward_body(q_all, g_all, out, inverse, kv, q_ids, k_ids, dq, dkv, total):
-    group = lax.rem(lax.axis_index("seq"), 4)
     total[...] = jnp.zeros_like(total)
 
-    def chunk(i, _):
-        whole, end = tile_bounds((4 * i + group) * TOK)
-        q = q_all[i]
-        g = g_all[i]
-        ids = q_ids[i]
-        one_over = inverse[i][:, :1]
-        correction = jnp.sum(g.astype(F32) * out[i].astype(F32), axis=-1, keepdims=True)
+    def pair(a, last):
+        rows = pl.ds(2 * TOK * a if last else pl.multiple_of(2 * TOK * a, 2 * TOK), 2 * TOK)
+        q = q_all[rows, :]
+        g = g_all[rows, :]
+        one_over = inverse[rows, :][:, :1]
+        correction = jnp.sum(g.astype(F32) * out[rows, :].astype(F32), axis=-1, keepdims=True)
         q_turned = jnp.transpose(q.astype(F32))[:HEAD_DIM].astype(BF)
         g_turned = jnp.transpose(g.astype(F32))[HEAD_DIM:].astype(BF)
 
-        def tile(j, acc, masked):
-            at = pl.ds(pl.multiple_of(j * KT, KT), KT)
+        def tile(j, acc, masked, width=WIDE):
+            at = pl.ds(j * WIDE if last and masked else pl.multiple_of(j * WIDE, WIDE), width)
             block = kv[at, :]
             p = jnp.exp(dot_t(q, block)) * one_over
             if masked:
-                p = jnp.where(k_ids[j] <= ids, p, 0.0)
+                p = jnp.where(k_ids[j][:, :width] <= q_ids[rows, :], p, 0.0)
             ds = (p * (dot_t(g, block) - correction)).astype(BF)
             total[:HEAD_DIM, at] += dot(q_turned, ds)
             total[HEAD_DIM:, at] += dot(g_turned, p.astype(BF))
             return acc + dot(ds, block)
 
-        acc = jnp.zeros((TOK, 128), F32)
-        acc = lax.fori_loop(0, whole, lambda j, c: tile(j, c, False), acc)
-        acc = lax.fori_loop(whole, end, lambda j, c: tile(j, c, True), acc)
-        dq[i] = (acc * 0.125).astype(BF)
-        return 0
-
-    lax.fori_loop(0, HEADS, chunk, 0)
+        acc = jnp.zeros((2 * TOK, 128), F32)
+        acc = lax.fori_loop(0, 2 * a, lambda j, c: tile(j, c, False), acc)
+        acc = tile(2 * a, acc, True)
+        acc = tile(2 * a + 1, acc, True)
+        acc = tile(2 * a + 2, acc, True, WIDE // 2 if last else WIDE)
+        dq[rows, :] = (acc * 0.125).astype(BF)
+
+    lax.fori_loop(0, 3, lambda a, c: (pair(a, False), c)[1], 0)
+    pair(3, True)
 
     def turn(j, _):
         at = pl.ds(pl.multiple_of(j * KT, KT), KT)
@@ -150,8 +144,42 @@
     lax.fori_loop(0, TOKENS // KT, turn, 0)
 
 
+def place():
+    me = lax.axis_index("seq")
+    x, z = lax.rem(lax.div(me, 4), 4), lax.rem(me, 4)
+    return ring_bits(lax.div(me, 16), x, z)
+
+
+def ring_bits(y, x, z):
+    return (y, lax.rem(lax.div(x + 1, 2), 2), lax.div(x, 2), lax.rem(lax.div(z + 1, 2), 2), lax.div(z, 2))
+
+
+def neighbours():
+    me = lax.axis_index("seq")
+    x, z = lax.rem(lax.div(me, 4), 4), lax.rem(me, 4)
+    return (
+        lax.rem(me + 16, N_SEQ),
+        me + 4 * (1 - 2 * lax.rem(x, 2)),
+        me + 4 * (3 - 2 * x),
+        me + 1 - 2 * lax.rem(z, 2),
+        me + 3 - 2 * z,
+    )
+
+
+def slot(stream, owner, bits):
+    y, x, z = owner // 16, owner // 4 % 4, owner % 4
+    theirs = (y, (x + 1) // 2 % 2, x // 2, (z + 1) // 2 % 2, z // 2)
+    at = 0
+    for step in range(5):
+        split = (stream + step) % 5
+        apart = 1 - bits[split] if theirs[split] else bits[split]
+        at = at + apart * (16 >> step)
+    return at
+
+
 def affine_body(act, up, att_all, w_out, g_pack, carry_part, out_term, att, att_turned, grad):
     left = left_half((TOK, 128))
+    bits = place()
     for pair in range(HEADS // 2):
         low = att_all[2 * pair].astype(F32)
         high = att_all[2 * pair + 1].astype(F32)
@@ -178,11 +206,47 @@
             g_pack[head + 1] = jnp.where(left, 0.0, slab).astype(BF)
     for block in range(8):
         columns = pl.ds(256 * block, 256)
-        out_term[:, columns] = dot(att_turned[...], grad[:, columns]).astype(BF)
-
-
-def finish_body(act, normed, carry_part, q_raw, k_raw, dq_all, dkv_parts, wq, wk, wv,
-                grad_input, terms, grads, gn, normed_turned):
+        term = dot(att_turned[...], grad[:, columns]).astype(BF)
+        stream = block // 4
+        for owner in range(N_SEQ):
+            at = slot(3 + stream, owner, bits)
+            for half in range(2):
+                row = 16 * (2 * (block % 4) + half)
+                out_term[stream, at, row : row + 16, :] = term[16 * owner : 16 * owner + 16, 128 * half : 128 * half + 128]
+
+
+def finish_body(act, normed, carry_part, q_raw, k_raw, dq_all, dkv_parts, wq, wk, wv, out_term, flip,
+                carry_out, sum_q, sum_k, sum_v, sum_out,
+                grads, gn, normed_turned, grad_input, moved, terms, acc, got0, got1, got2, got3, got4,
+                send, recv, carry_sem):
+    section = lax.axis_index("section")
+    across = N_SEQ - 1 - lax.axis_index("seq")
+    before, after = lax.rem(section + 3, 4), lax.rem(section + 1, 4)
+    near = neighbours()
+    bits = place()
+    barrier = pltpu.get_barrier_semaphore()
+    for peer in near:
+        pl.semaphore_signal(barrier, inc=1, device_id={"seq": peer}, device_id_type=MESH)
+    for other in (before, after):
+        pl.semaphore_signal(barrier, inc=1, device_id={"section": other, "seq": across}, device_id_type=MESH)
+    pl.semaphore_wait(barrier, 7)
+
+    got = (got0, got1, got2, got3, got4)
+
+    def hop(stream, step):
+        half = 16 >> step
+        if step:
+            source = acc.at[stream, pl.ds(half, half)]
+        else:
+            source = terms.at[stream, pl.ds(half, half)] if stream < 3 else out_term.at[stream - 3, pl.ds(half, half)]
+        return pltpu.make_async_remote_copy(
+            src_ref=source, dst_ref=got[step].at[stream], send_sem=send.at[stream, step],
+            recv_sem=recv.at[stream, step], device_id={"seq": near[(stream + step) % 5]}, device_id_type=MESH,
+        )
+
+    for stream in (3, 4):
+        hop(stream, 0).start()
+
     left = left_half((TOK, 128))
 
     def unit_back(grad, raw):
@@ -207,6 +271,15 @@
     for block in range(8):
         at = pl.ds(128 * block, 128)
         normed_turned[at, :] = jnp.transpose(normed[:, at].astype(F32)).astype(BF)
+    for stream in range(3):
+        for block in range(2):
+            term = dot(normed_turned[...], grads[stream, :, 256 * block : 256 * block + 256]).astype(BF)
+            for owner in range(N_SEQ):
+                at = slot(stream, owner, bits)
+                for half in range(2):
+                    row = 32 * (2 * block + half)
+                    terms[stream, at, row : row + 32, :] = term[32 * owner : 32 * owner + 32, 128 * half : 128 * half + 128]
+        hop(stream, 0).start()
     for block in range(4):
         at = pl.ds(256 * block, 256)
         gn[:, at] = dot_t(grads[0], wq[at, :]) + dot_t(grads[1], wk[at, :]) + dot_t(grads[2], wv[at, :])
@@ -216,11 +289,78 @@
     grad_normed = gn[...]
     mean = jnp.mean(grad_normed * unit, axis=-1, keepdims=True)
     grad_input[...] = (carry_part[...] + scale * (grad_normed - unit * mean)).astype(BF)
-    for which in range(3):
-        for block in range(2):
-            terms[:, INNER * which + 256 * block : INNER * which + 256 * block + 256] = dot(
-                normed_turned[...], grads[which, :, 256 * block : 256 * block + 256]
-            ).astype(BF)
+    carry = pltpu.make_async_remote_copy(
+        src_ref=grad_input, dst_ref=moved, send_sem=carry_sem.at[0], recv_sem=carry_sem.at[1],
+        device_id={"section": before, "seq": across}, device_id_type=MESH,
+    )
+    carry.start()
+
+    def add(stream, step, first, count):
+        def one(i, _):
+            if step:
+                mine = acc[stream, i]
+            else:
+                mine = terms[stream, i] if stream < 3 else out_term[stream - 3, i]
+            acc[stream, i] = (mine.astype(F32) + got[step][stream, i].astype(F32)).astype(BF)
+            return 0
+
+        lax.fori_loop(first, first + count, one, 0)
+
+    for step in range(4):
+        half = 8 >> step
+        for stream in (3, 4, 0, 1, 2):
+            hop(stream, step).wait_recv()
+            add(stream, step, half, half)
+            hop(stream, step + 1).start()
+            add(stream, step, 0, half)
+    for stream in (3, 4, 0, 1, 2):
+        hop(stream, 4).wait_recv()
+        result = acc[stream, 0].astype(F32) + got4[stream, 0].astype(F32)
+        if stream < 3:
+            target = (sum_q, sum_k, sum_v)[stream]
+            for part in range(4):
+                target[:, 128 * part : 128 * part + 128] = result[32 * part : 32 * part + 32]
+        else:
+            for part in range(8):
+                column = 1024 * (stream - 3) + 128 * part
+                sum_out[:, column : column + 128] = result[16 * part : 16 * part + 16]
+    carry.wait()
+    chosen = (flip[...] == lax.broadcasted_iota(jnp.int32, (TOK, TOK), 1)).astype(BF)
+    last = (section + jnp.zeros((TOK, 1), jnp.int32)) == 3
+    for block in range(4):
+        at = pl.ds(256 * block, 256)
+        carry_out[:, at] = jnp.where(last, 0.0, dot(chosen, moved[:, at])).astype(BF)
+    for step in range(5):
+        for stream in range(5):
+            hop(stream, step).wait_send()
+
+
+def finish(*operands):
+    return pl.pallas_call(
+        finish_body,
+        out_shape=[jax.ShapeDtypeStruct((TOK, D), BF)]
+        + [jax.ShapeDtypeStruct((32, INNER), F32)] * 3
+        + [jax.ShapeDtypeStruct((16, 2 * D), F32)],
+        in_specs=[VMEM] * len(operands),
+        out_specs=[VMEM] * 5,
+        scratch_shapes=[
+            pltpu.VMEM((3, TOK, INNER), BF),
+            pltpu.VMEM((TOK, D), F32),
+            pltpu.VMEM((D, TOK), BF),
+            pltpu.VMEM((TOK, D), BF),
+            pltpu.VMEM((TOK, D), BF),
+            pltpu.VMEM((3, N_SEQ, 128, 128), BF),
+            pltpu.VMEM((5, 16, 128, 128), BF),
+        ]
+        + [pltpu.VMEM((5, 16 >> step, 128, 128), BF) for step in range(5)]
+        + [
+            pltpu.SemaphoreType.DMA((5, 5)),
+            pltpu.SemaphoreType.DMA((5, 5)),
+            pltpu.SemaphoreType.DMA((2,)),
+        ],
+        compiler_params=pltpu.CompilerParams(collective_id=5, has_side_effects=True, vmem_limit_bytes=BIG),
+        name="finish",
+    )(*operands)
 
 
 def local_call(body, outs, scratch=(), name=None):
@@ -317,105 +457,13 @@
     )(*arrays)
 
 
-def sums_body(terms, out_term, rows, sums, out_sum, moved, parts, out_parts,
-              send, recv, out_send, out_recv, local_sem, carry_sem):
-    me = lax.axis_index("seq")
-    section = lax.axis_index("section")
-    before, after = lax.rem(section + 3, 4), lax.rem(section + 1, 4)
-    across = N_SEQ - 1 - me
-    barrier = pltpu.get_barrier_semaphore()
-
-    def greet(k, _):
-        pl.semaphore_signal(barrier, inc=1, device_id={"seq": lax.rem(me + k, N_SEQ)}, device_id_type=MESH)
-        return 0
-
-    lax.fori_loop(1, N_SEQ, greet, 0)
-    for other in (before, after):
-        pl.semaphore_signal(barrier, inc=1, device_id={"section": other, "seq": across}, device_id_type=MESH)
-    pl.semaphore_wait(barrier, N_SEQ + 1)
-
-    carry = pltpu.make_async_remote_copy(
-        src_ref=rows, dst_ref=moved, send_sem=carry_sem.at[0], recv_sem=carry_sem.at[1],
-        device_id={"section": before, "seq": across}, device_id_type=MESH,
-    )
-    carry.start()
-
-    def term_copy(k):
-        peer = lax.rem(me + k, N_SEQ)
-        return pltpu.make_async_remote_copy(
-            src_ref=terms.at[pl.ds(pl.multiple_of(peer * 32, 32), 32), :], dst_ref=parts.at[k],
-            send_sem=send.at[k], recv_sem=recv.at[k], device_id={"seq": peer}, device_id_type=MESH,
-        )
-
-    def out_copy(k):
-        peer = lax.rem(me + k, N_SEQ)
-        return pltpu.make_async_remote_copy(
-            src_ref=out_term.at[pl.ds(pl.multiple_of(peer * 16, 16), 16), :], dst_ref=out_parts.at[k],
-            send_sem=out_send.at[k], recv_sem=out_recv.at[k], device_id={"seq": peer}, device_id_type=MESH,
-        )
-
-    def begin(k, _):
-        term_copy(k).start()
-        out_copy(k).start()
-        return 0
-
-    lax.fori_loop(1, N_SEQ, begin, 0)
-    own = [
-        pltpu.make_async_copy(terms.at[pl.ds(pl.multiple_of(me * 32, 32), 32), :], parts.at[0], local_sem.at[0]),
-        pltpu.make_async_copy(out_term.at[pl.ds(pl.multiple_of(me * 16, 16), 16), :], out_parts.at[0], local_sem.at[1]),
-    ]
-    for copy in own:
-        copy.start()
-    for copy in own:
-        copy.wait()
-    sums[...] = parts[0].astype(F32)
-    out_sum[...] = out_parts[0].astype(F32)
-
-    def add(k, _):
-        term_copy(k).wait()
-        sums[...] += parts[k].astype(F32)
-        out_copy(k).wait()
-        out_sum[...] += out_parts[k].astype(F32)
-        return 0
-
-    lax.fori_loop(1, N_SEQ, add, 0)
-    carry.wait()
-
-
-def reduce_terms(terms, out_term, rows):
-    return pl.pallas_call(
-        sums_body,
-        out_shape=[
-            jax.ShapeDtypeStruct((32, 3 * INNER), F32),
-            jax.ShapeDtypeStruct((16, 2 * D), F32),
-            jax.ShapeDtypeStruct((TOK, D), BF),
-        ],
-        in_specs=[ANY, ANY, ANY],
-        out_specs=[VMEM, VMEM, ANY],
-        scratch_shapes=[
-            pltpu.VMEM((N_SEQ, 32, 3 * INNER), BF),
-            pltpu.VMEM((N_SEQ, 16, 2 * D), BF),
-            pltpu.SemaphoreType.DMA((N_SEQ,)),
-            pltpu.SemaphoreType.DMA((N_SEQ,)),
-            pltpu.SemaphoreType.DMA((N_SEQ,)),
-            pltpu.SemaphoreType.DMA((N_SEQ,)),
-            pltpu.SemaphoreType.DMA((2,)),
-            pltpu.SemaphoreType.DMA((2,)),
-        ],
-        compiler_params=pltpu.CompilerParams(
-            collective_id=5, has_side_effects=True, vmem_limit_bytes=BIG
-        ),
-        name="sums",
-    )(terms, out_term, rows)
-
-
 def shards(activations, incoming, w_query, w_key, w_value, w_out, block_ids, flip_order):
     act, up = activations[0], incoming[0]
     wq, wk, wv, wo = w_query[0], w_key[0], w_value[0], w_out[0]
     group = lax.rem(lax.axis_index("seq"), 4)
     by_chunk = block_ids.reshape(HEADS, 4, TOK)
-    q_ids = lax.dynamic_index_in_dim(by_chunk, group, 1, keepdims=False)[:, :, None]
-    k_ids = block_ids.reshape(TOKENS // KT, 1, KT)
+    q_ids = lax.dynamic_index_in_dim(by_chunk, group, 1, keepdims=False).reshape(HEADS * TOK, 1)
+    k_ids = jnp.pad(block_ids, (0, 9 * WIDE - TOKENS)).reshape(9, 1, WIDE)
 
     normed, q_raw, k_raw, q_pack, kv_pack = local_call(
         project_body,
@@ -424,40 +472,31 @@
     )(act, wq, wk, wv)
     kv_all, q_all = exchange(kv_pack, q_pack, True, 1, "spread")
     kv = kv_all.reshape(TOKENS, 128)
+    q_all = q_all.reshape(HEADS * TOK, 128)
     out, inverse = local_call(
-        forward_body, [((HEADS, TOK, 128), BF), ((HEADS, TOK, 128), F32)], name="attend"
+        forward_body, [((HEADS * TOK, 128), BF), ((HEADS * TOK, 128), F32)], name="attend"
     )(q_all, kv, q_ids, k_ids)
-    (att_all,) = exchange(None, out, True, 2, "attended")
+    (att_all,) = exchange(None, out.reshape(HEADS, TOK, 128), True, 2, "attended")
     g_pack, carry_part, out_term = local_call(
         affine_body,
-        [((HEADS, TOK, 128), BF), ((TOK, D), F32), ((INNER, 2 * D), BF)],
+        [((HEADS, TOK, 128), BF), ((TOK, D), F32), ((2, N_SEQ, 128, 128), BF)],
         [((TOK, INNER), BF), ((INNER, TOK), BF), ((TOK, 2 * D), BF)],
         name="affine",
     )(act, up, att_all, wo)
     (g_all,) = exchange(None, g_pack, True, 3, "grad_attn")
     dq, dkv = local_call(
         backward_body,
-        [((HEADS, TOK, 128), BF), ((TOKENS, 128), BF)],
+        [((HEADS * TOK, 128), BF), ((TOKENS, 128), BF)],
         [((128, TOKENS), F32)],
         name="attend_back",
-    )(q_all, g_all, out, inverse, kv, q_ids, k_ids)
-    dkv_parts, dq_all = exchange(dkv.reshape(N_SEQ, TOK, 128), dq, False, 4, "gather_grads")
-    grad_input, terms = local_call(
-        finish_body,
-        [((TOK, D), BF), ((D, 3 * INNER), BF)],
-        [((3, TOK, INNER), BF), ((TOK, D), F32), ((D, TOK), BF)],
-        name="finish",
-    )(act, normed, carry_part, q_raw, k_raw, dq_all, dkv_parts, wq, wk, wv)
-    sums, out_sum, moved = reduce_terms(terms, out_term, grad_input)
-    carry = jnp.take(moved, flip_order[0], axis=0)
-    carry = jnp.where(lax.axis_index("section") == 3, jnp.zeros_like(carry), carry)
-    return (
-        carry[None],
-        sums[None, :, :INNER],
-        sums[None, :, INNER : 2 * INNER],
-        sums[None, :, 2 * INNER :],
-        out_sum[None],
+    )(q_all, g_all.reshape(HEADS * TOK, 128), out, inverse, kv, q_ids, k_ids)
+    dkv_parts, dq_all = exchange(
+        dkv.reshape(N_SEQ, TOK, 128), dq.reshape(HEADS, TOK, 128), False, 4, "gather_grads"
     )
+    carry, sum_q, sum_k, sum_v, sum_out = finish(
+        act, normed, carry_part, q_raw, k_raw, dq_all, dkv_parts, wq, wk, wv, out_term, flip_order.reshape(TOK, 1)
+    )
+    return carry[None], sum_q[None], sum_k[None], sum_v[None], sum_out[None]
 
 
 def solution(mesh):

time: 272 us -> 165 us (0.61)
  the two profiles are of different devices: /device:TPU:97 before, /device:TPU:0 now
where the time goes in v2:
time: 165 us; the launch traced here: 164 us
  Pallas kernels  153 us (93%)
  local copies, waits for them, and re-layouts  10.2 us (6%)
    pallas_call x4, Pallas kernels, exchange(): pl.pallas_call(body, out_shape=outs, in_specs=[ANY] * len(arrays), out_sp...  66.4 us
    pallas_call x1, Pallas kernels, finish(): pl.pallas_call(finish_body, out_shape=[jax.ShapeDtypeStruct((TOK, D), BF)...  47.8 us
    pallas_call x1, Pallas kernels, shards(): local_call(backward_body, [((HEADS * TOK, 128), BF), ((TOKENS, 128), BF)]...  19.5 us
    pallas_call x1, Pallas kernels, shards(): local_call(forward_body, [((HEADS * TOK, 128), BF), ((HEADS * TOK, 128),...  9.99 us
    unnamed x9, local copies, waits for them, and re-layouts  7.68 us
    pallas_call x1, Pallas kernels, shards(): local_call(affine_body, [((HEADS, TOK, 128), BF), ((TOK, D), F32), ((2, N...  5.3 us
    pallas_call x1, Pallas kernels, shards(): local_call(project_body, [((TOK, D), BF), ((TOK, INNER), F32), ((TOK, INN...  3.93 us

profile of v2, /device:TPU:0, one launch (start us, length us, event | category | flops | bytes accessed | tf_op | source)
XLA Modules:
  0.0 163.8 jit_solution(17461508866538892121)
XLA Ops:
  0.6 0.0 copy-start
  0.6 3.9 %project.1 = (bf16[136,1024]{1,0:T(8,128)(2,1)}, f32[136,512]{1,0:T(8,128)}, f32[136,512]{1,0:T(8,128)}, bf16[8,136,128]{2,1,0:T(8,128)(2,1)}, bf16[8,136,128]{2,1,0:T(8,128)(2,1)}) custom-call(bf16[136,1024]{1,0:T(8,128)(2,1)} %bitcast.26, bf16[1024,512]{1,0:T(8,128)(2,1)} %bitcast.20, bf16[1024,512]{1,0:T(8,128)(2,1)} %bitcast.22, bf16[1024,512]{1,0:T(8,128)(2,1)} %bitcast.24), custom_call_target="tpu_custom_call" | custom-call | tf_op jit(solution)/shard_map/project/pallas_call | solution.py:468
  4.6 26.6 %spread.1 = (bf16[32,136,128]{2,1,0:T(8,128)(2,1)}, bf16[8,136,128]{2,1,0:T(8,128)(2,1)}) custom-call(bf16[8,136,128]{2,1,0:T(8,128)(2,1)} %get-tuple-element.27.refs_0_, bf16[8,136,128]{2,1,0:T(8,128)(2,1)} %get-tuple-element.28.refs_1_), custom_call_target="tpu_custom_call" | custom-call | tf_op jit(solution)/shard_map/spread/pallas_call | solution.py:443
  31.1 0.0 copy-done
  31.2 0.1 reshape.43
  31.3 1.0 reshape.51.q_ids
  32.3 0.6 reshape.45.k_ids
  33.0 10.0 %attend.1 = (bf16[1088,128]{1,0:T(8,128)(2,1)}, f32[1088,128]{1,0:T(8,128)}) custom-call(bf16[1088,128]{1,0:T(8,128)(2,1)} %bitcast.33, bf16[4352,128]{1,0:T(8,128)(2,1)} %bitcast.18, s32[1088,1]{1,0:T(8,128)} %reshape.51.q_ids, s32[9,1,512]{2,1,0:T(1,128)} %reshape.45.k_ids), custom_call_target="tpu_custom_call" | custom-call | tf_op jit(solution)/shard_map/attend/pallas_call | solution.py:476
  43.0 7.9 %attended.1.att_all = bf16[8,136,128]{2,1,0:T(8,128)(2,1)} custom-call(bf16[8,136,128]{2,1,0:T(8,128)(2,1)} %bitcast.31), custom_call_target="tpu_custom_call" | custom-call | tf_op jit(solution)/shard_map/attended/pallas_call | solution.py:443
  50.8 5.3 %affine.1 = (bf16[8,136,128]{2,1,0:T(8,128)(2,1)}, f32[136,1024]{1,0:T(8,128)}, bf16[2,32,128,128]{3,2,1,0:T(8,128)(2,1)}) custom-call(bf16[136,1024]{1,0:T(8,128)(2,1)} %bitcast.27, bf16[136,1024]{1,0:T(8,128)(2,1)} %bitcast.35, bf16[8,136,128]{2,1,0:T(8,128)(2,1)} %attended.1.att_all, bf16[512,2048]{1,0:T(8,128)(2,1)} %bitcast.29), custom_call_target="tpu_custom_call" | custom-call | tf_op jit(solution)/shard_map/affine/pallas_call | solution.py:480
  56.1 8.3 %grad_attn.1 = bf16[8,136,128]{2,1,0:T(8,128)(2,1)} custom-call(bf16[8,136,128]{2,1,0:T(8,128)(2,1)} %get-tuple-element.35.refs_0_), custom_call_target="tpu_custom_call" | custom-call | tf_op jit(solution)/shard_map/grad_attn/pallas_call | solution.py:443
  64.4 19.5 %attend_back.1 = (bf16[1088,128]{1,0:T(8,128)(2,1)}, bf16[4352,128]{1,0:T(8,128)(2,1)}) custom-call(bf16[1088,128]{1,0:T(8,128)(2,1)} %bitcast.34, bf16[1088,128]{1,0:T(8,128)(2,1)} %bitcast.32, bf16[1088,128]{1,0:T(8,128)(2,1)} %get-tuple-element.31.out, f32[1088,128]{1,0:T(8,128)} %get-tuple-element.36.inverse, bf16[4352,128]{1,0:T(8,128)(2,1)} %bitcast.19, ...), custom_call_target="tpu_custom_call" | custom-call | tf_op jit(solution)/shard_map/attend_back/pallas_call | solution.py:487
  83.9 0.0 copy-start.1
  83.9 23.7 %gather_grads.1 = (bf16[32,136,128]{2,1,0:T(8,128)(2,1)}, bf16[8,136,128]{2,1,0:T(8,128)(2,1)}) custom-call(bf16[32,136,128]{2,1,0:T(8,128)(2,1)} %bitcast.30, bf16[8,136,128]{2,1,0:T(8,128)(2,1)} %bitcast.37), custom_call_target="tpu_custom_call" | custom-call | tf_op jit(solution)/shard_map/gather_grads/pallas_call | solution.py:443
  107.6 0.0 copy-done.1
  107.6 0.7 copy.15.flip
  108.3 47.8 %finish.1 = (bf16[136,1024]{1,0:T(8,128)(2,1)}, f32[32,512]{1,0:T(8,128)}, f32[32,512]{1,0:T(8,128)}, f32[32,512]{1,0:T(8,128)}, f32[16,2048]{1,0:T(8,128)}) custom-call(bf16[136,1024]{1,0:T(8,128)(2,1)} %bitcast.28, bf16[136,1024]{1,0:T(8,128)(2,1)} %get-tuple-element.26.normed, f32[136,1024]{1,0:T(8,128)} %get-tuple-element.32.carry_part, ...), custom_call_target="tpu_custom_call" | custom-call | tf_op jit(solution)/shard_map/finish/pallas_call | solution.py:339
  156.1 1.7 %copy.21 = bf16[1,136,1024]{2,1,0:T(8,128)(2,1)} copy(bf16[1,136,1024]{2,1,0:T(8,128)(2,1)} %bitcast.36) | data formatting | bytes 557056
  157.8 1.5 copy.22
  159.2 1.5 copy.23
  160.7 1.5 copy.24
  162.2 1.6 copy.25
  (2 shorter events, 0.0 us)
Async XLA Ops:
  0.6 30.5 %copy-start = (s32[4352]{0:T(1024)S(1)}, s32[4352]{0:T(1024)}, u32[]{:S(2)}) copy-start(s32[4352]{0:T(1024)} %param.14) | copy-start | bytes 52228
  83.9 23.7 %copy-start.1 = (s32[1,136]{1,0:T(1,128)S(1)}, s32[1,136]{1,0:T(1,128)}, u32[]{:S(2)}) copy-start(s32[1,136]{1,0:T(1,128)} %param.15) | copy-start | bytes 1636

commit v3 on v0

v3 whole, which is shorter than its diff:
```python
import jax
import jax.numpy as jnp
from jax import lax
from jax.experimental import pallas as pl
from jax.experimental.pallas import tpu as pltpu
from jax.sharding import PartitionSpec as P

HEADS = 8
HEAD_DIM = 64
EPSILON = 1e-06
N_SEQ = 32
TOK = 136
TOKENS = 4352
D = 1024
INNER = 512
WIDE = 512
KEYS = 9 * WIDE
NEAR_ROWS = 64
BF = jnp.bfloat16
F32 = jnp.float32
MESH = pl.DeviceIdType.MESH
VMEM = pl.BlockSpec(memory_space=pltpu.VMEM)
ANY = pl.BlockSpec(memory_space=pl.ANY)
BIG = 60 * 1024 * 1024


def dot(a, b):
    return jnp.dot(a, b, preferred_element_type=F32)


def dot_t(a, b):
    return lax.dot_general(a, b, (((1,), (1,)), ((), ())), preferred_element_type=F32)


def left_half(shape):
    return lax.broadcasted_iota(jnp.int32, shape, 1) < HEAD_DIM


def swap(slab):
    return pltpu.roll(slab, HEAD_DIM, 1)


def per_head_sum(slab, left):
    low = jnp.sum(jnp.where(left, slab, 0.0), axis=-1, keepdims=True)
    high = jnp.sum(jnp.where(left, 0.0, slab), axis=-1, keepdims=True)
    return jnp.where(left, low, high)


def unit_scale(slab, left):
    return lax.rsqrt(per_head_sum(slab * slab, left) * (1.0 / HEAD_DIM) + EPSILON)


def place():
    me = lax.axis_index("seq")
    x, z = lax.rem(lax.div(me, 4), 4), lax.rem(me, 4)
    return ring_bits(lax.div(me, 16), x, z)


def ring_bits(y, x, z):
    return (y, lax.rem(lax.div(x + 1, 2), 2), lax.div(x, 2), lax.rem(lax.div(z + 1, 2), 2), lax.div(z, 2))


def neighbours():
    me = lax.axis_index("seq")
    x, z = lax.rem(lax.div(me, 4), 4), lax.rem(me, 4)
    return (
        lax.rem(me + 16, N_SEQ),
        me + 4 * (1 - 2 * lax.rem(x, 2)),
        me + 4 * (3 - 2 * x),
        me + 1 - 2 * lax.rem(z, 2),
        me + 3 - 2 * z,
    )


def spread_out(groups):
    counts = [groups // 5 + (1 if stream < groups % 5 else 0) for stream in range(5)]
    places = [(stream, 16 * row) for stream in range(5) for row in range(counts[stream])]
    return [16 * count for count in counts], places


TERM_ROWS, TERM_PLACES = spread_out(24)
OUT_ROWS, OUT_PLACES = spread_out(16)


def slot(stream, owner, bits):
    y, x, z = owner // 16, owner // 4 % 4, owner % 4
    theirs = (y, (x + 1) // 2 % 2, x // 2, (z + 1) // 2 % 2, z // 2)
    at = 0
    for step in range(5):
        split = (stream + step) % 5
        apart = 1 - bits[split] if theirs[split] else bits[split]
        at = at + apart * (16 >> step)
    return at


class Halving:
    def __init__(self, terms, acc, got, send, recv, near):
        self.terms, self.acc, self.got, self.send, self.recv, self.near = terms, acc, got, send, recv, near

    def hop(self, stream, step):
        half = 16 >> step
        return pltpu.make_async_remote_copy(
            src_ref=(self.acc if step else self.terms)[stream].at[pl.ds(half, half)],
            dst_ref=self.got[stream].at[pl.ds(32 - (32 >> step), half)],
            send_sem=self.send.at[stream, step],
            recv_sem=self.recv.at[stream, step],
            device_id={"seq": self.near[(stream + step) % 5]},
            device_id_type=MESH,
        )

    def add(self, stream, step, first, count):
        mine = (self.acc if step else self.terms)[stream]
        acc, got = self.acc[stream], self.got[stream]
        behind = 32 - (32 >> step)
        width = min(count, 4)

        def one(i, _):
            at = first + width * i
            total = mine[pl.ds(at, width)].astype(F32) + got[pl.ds(behind + at, width)].astype(F32)
            acc[pl.ds(at, width)] = total.astype(BF)
            return 0

        if count == width:
            one(0, 0)
        else:
            lax.fori_loop(0, count // width, one, 0)

    def advance(self, stream, step):
        half = 8 >> step
        self.hop(stream, step).wait_recv()
        self.add(stream, step, half, half)
        self.hop(stream, step + 1).start()
        self.add(stream, step, 0, half)

    def result(self, stream):
        self.hop(stream, 4).wait_recv()
        return self.acc[stream][0].astype(F32) + self.got[stream][30].astype(F32)

    def drain(self):
        for step in range(5):
            for stream in range(5):
                self.hop(stream, step).wait_send()


def halving_scratch(rows):
    return (
        [pltpu.VMEM((N_SEQ, count, 128), BF) for count in rows]
        + [pltpu.VMEM((16, count, 128), BF) for count in rows]
        + [pltpu.VMEM((31, count, 128), BF) for count in rows]
        + [pltpu.SemaphoreType.DMA((5, 5)), pltpu.SemaphoreType.DMA((5, 5))]
    )


def chunk_rows(index):
    return pl.ds(pl.multiple_of(index * TOK, 8), TOK)


def layer_body(*refs):
    refs = list(refs)

    def take(count):
        taken = refs[:count]
        del refs[:count]
        return taken

    act_in, up_in, wq_in, wk_in, wv_in, wo_in, ids = take(7)
    sum_q, sum_k, sum_v, sum_out, moved = take(5)
    act, up, wq, wk, wv, wo = take(6)
    normed, normed_turned, q_raw, k_raw, q_pack, kv_pack = take(6)
    kv, q_all, g_all, q_ids, out, inverse, att_all, att, att_turned, affine_grad, g_pack, carry_part = take(12)
    total, dkv, dq, dkv_parts, dq_all, grads, gn, grad_input = take(8)
    out_refs = take(17)
    term_refs = take(17)
    (load, kv_send, kv_recv, q_send, q_recv, z_send, z_recv, f_send, f_recv, att_send, att_recv,
     g_send, g_recv, dq_send, dq_recv, dkv_send, dkv_recv, local, carry_sem) = refs

    me = lax.axis_index("seq")
    section = lax.axis_index("section")
    mine, group = lax.div(me, 4), lax.rem(me, 4)
    near, bits = neighbours(), place()
    across = N_SEQ - 1 - me
    before, after = lax.rem(section + 3, 4), lax.rem(section + 1, 4)
    z_next, z_back = 4 * mine + lax.rem(group + 1, 4), 4 * mine + lax.rem(group + 3, 4)

    loads = [
        pltpu.make_async_copy(source, target, load.at[i])
        for i, (source, target) in enumerate(
            ((act_in, act), (wq_in, wq), (wk_in, wk), (wv_in, wv), (wo_in, wo), (up_in, up))
        )
    ]
    for copy in loads:
        copy.start()

    barrier = pltpu.get_barrier_semaphore()

    def greet(k, _):
        pl.semaphore_signal(barrier, inc=1, device_id={"seq": lax.rem(me + k, N_SEQ)}, device_id_type=MESH)
        return 0

    lax.fori_loop(1, N_SEQ, greet, 0)
    for other in (before, after):
        pl.semaphore_signal(barrier, inc=1, device_id={"section": other, "seq": across}, device_id_type=MESH)

    def remote(source, target, send, recv, peer):
        return pltpu.make_async_remote_copy(
            src_ref=source, dst_ref=target, send_sem=send, recv_sem=recv,
            device_id={"seq": peer}, device_id_type=MESH,
        )

    def loop(first, end, do):
        def one(k, c):
            do(k)
            return c

        lax.fori_loop(first, end, one, 0)

    left = left_half((TOK, 128))
    out_sum = Halving(out_refs[:5], out_refs[5:10], out_refs[10:15], out_refs[15], out_refs[16], near)
    term_sum = Halving(term_refs[:5], term_refs[5:10], term_refs[10:15], term_refs[15], term_refs[16], near)

    loads[0].wait()
    field = act[...].astype(F32)
    row_scale = lax.rsqrt(jnp.mean(field * field, axis=-1, keepdims=True) + EPSILON)
    normed[...] = (field * row_scale).astype(BF)
    for copy in loads[1:4]:
        copy.wait()
    for block in range(2):
        columns = pl.ds(256 * block, 256)
        q = dot(normed[...], wq[:, columns])
        k = dot(normed[...], wk[:, columns])
        v = dot(normed[...], wv[:, columns])
        q_raw[:, columns] = q
        k_raw[:, columns] = k
        for half in range(2):
            head = 4 * block + 2 * half
            q_slab = q[:, 128 * half : 128 * half + 128]
            k_slab = k[:, 128 * half : 128 * half + 128]
            v_slab = v[:, 128 * half : 128 * half + 128]
            q_slab = (q_slab * unit_scale(q_slab, left)).astype(BF).astype(F32) * 0.125
            k_slab = k_slab * unit_scale(k_slab, left)
            q_pack[head] = jnp.where(left, q_slab, 0.0).astype(BF)
            q_pack[head + 1] = jnp.where(left, swap(q_slab), 0.0).astype(BF)
            kv_pack[head] = jnp.where(left, k_slab, swap(v_slab)).astype(BF)
            kv_pack[head + 1] = jnp.where(left, swap(k_slab), v_slab).astype(BF)
    pl.semaphore_wait(barrier, N_SEQ + 1)

    def kv_copy(k):
        peer = lax.rem(mine + k, HEADS)
        return remote(kv_pack.at[peer], kv.at[chunk_rows(me)], kv_send.at[k], kv_recv.at[k], 4 * peer + group)

    def q_copy(k):
        peer = lax.rem(mine + k, HEADS)
        return remote(q_pack.at[peer], q_all.at[chunk_rows(mine)], q_send.at[k], q_recv.at[k], 4 * peer + group)

    loop(1, HEADS, lambda k: kv_copy(k).start())
    own = [
        pltpu.make_async_copy(kv_pack.at[mine], kv.at[chunk_rows(me)], local.at[0]),
        pltpu.make_async_copy(q_pack.at[mine], q_all.at[chunk_rows(mine)], local.at[1]),
    ]
    for copy in own:
        copy.start()
    loop(1, HEADS, lambda k: q_copy(k).start())
    kv[pl.ds(TOKENS, KEYS - TOKENS), :] = jnp.zeros((KEYS - TOKENS, 128), BF)
    total[...] = jnp.zeros_like(total)
    own[0].wait()

    def row_of(k, place):
        return 4 * lax.rem(mine - k + HEADS, HEADS) + place

    def z_copy(k, way):
        rows = kv.at[chunk_rows(row_of(k, group))]
        return remote(rows, rows, z_send.at[way, k], z_recv.at[way, k], z_back if way else z_next)

    def f_copy(k, way):
        token = row_of(k, lax.rem(group + (1 if way else 3), 4)) * TOK
        if way:
            rows = kv.at[pl.ds(pl.multiple_of(token + NEAR_ROWS, 8), TOK - NEAR_ROWS)]
        else:
            rows = kv.at[pl.ds(pl.multiple_of(token, 8), NEAR_ROWS)]
        return remote(rows, rows, f_send.at[way, k], f_recv.at[way, k], z_back if way else z_next)

    def relay(k):
        for way in range(2):
            z_copy(k, way).start()

    def forward(k):
        for way in range(2):
            z_copy(k, way).wait_recv()
            f_copy(k, way).start()

    relay(0)

    def pipe(k):
        kv_copy(k).wait_recv()
        relay(k)
        forward(k - 1)

    loop(1, HEADS, pipe)

    turned = jnp.transpose(ids[...].astype(F32)).astype(jnp.int32)
    for row in range(TOKENS // 128):
        q_ids[128 * row : 128 * row + 128, :] = turned[:, row : row + 1]
    for block in range(8):
        at = pl.ds(128 * block, 128)
        normed_turned[at, :] = jnp.transpose(normed[:, at].astype(F32)).astype(BF)
    own[1].wait()
    loop(1, HEADS, lambda k: q_copy(k).wait_recv())
    forward(HEADS - 1)

    def landed(k):
        for way in range(2):
            f_copy(k, way).wait_recv()

    loop(0, HEADS, landed)

    def seen(a, j, width):
        columns = []
        for half in range(2):
            first = pl.multiple_of((4 * (2 * a + half) + group) * TOK, 8)
            columns.append(q_ids[pl.ds(first, TOK), :])
        column = jnp.concatenate(columns, axis=0)
        return jnp.concatenate(
            [ids[pl.ds(4 * j + part, 1), :] <= column for part in range(width // 128)], axis=1
        )

    def pair_rows(a):
        return pl.ds(a * 2 * TOK if isinstance(a, int) else pl.multiple_of(a * 2 * TOK, 16), 2 * TOK)

    def tile_at(j, width):
        return pl.ds(j * WIDE if isinstance(j, int) else pl.multiple_of(j * WIDE, WIDE), width)

    def attend(a, last):
        rows = pair_rows(a)
        q = q_all[rows, :]

        def tile(j, carry, masked, width=WIDE):
            summed, mass = carry
            block = kv[tile_at(j, width), :]
            p = jnp.exp(dot_t(q, block))
            if masked:
                p = jnp.where(seen(a, j, width), p, 0.0)
            for part in range(width // 128):
                mass = mass + p[:, 128 * part : 128 * part + 128]
            return summed + dot(p.astype(BF), block), mass

        zero = jnp.zeros((2 * TOK, 128), F32)
        carry = lax.fori_loop(0, 2 * a, lambda j, c: tile(j, c, False), (zero, zero))
        carry = tile(2 * a, carry, True)
        carry = tile(2 * a + 1, carry, True)
        summed, mass = tile(2 * a + 2, carry, True, WIDE // 2 if last else WIDE)
        one_over = 1.0 / jnp.sum(mass, axis=-1, keepdims=True)
        result = (summed * one_over).astype(BF)
        out[rows, :] = result
        inverse[rows, :] = jnp.broadcast_to(one_over, (2 * TOK, 128))
        return result

    def att_copy(chunk):
        k = lax.rem(chunk - mine + HEADS, HEADS)
        return remote(out.at[chunk_rows(chunk)], att_all.at[mine], att_send.at[k], att_recv.at[k], 4 * chunk + group)

    def attend_and_send(a, last):
        attend(a, last)
        for half in range(2):
            chunk = 2 * a + half

            @pl.when(chunk != mine)
            def _():
                att_copy(chunk).start()

            @pl.when(chunk == mine)
            def _():
                pltpu.make_async_copy(out.at[chunk_rows(chunk)], att_all.at[mine], local.at[0]).start()

    loop(0, 3, lambda a: attend_and_send(a, False))
    attend_and_send(3, True)

    loads[4].wait()
    loads[5].wait()
    pltpu.make_async_copy(out.at[chunk_rows(mine)], att_all.at[mine], local.at[0]).wait()

    def att_arrived(k):
        peer = lax.rem(mine + k, HEADS)
        att_copy(peer).wait_recv()

    loop(1, HEADS, att_arrived)
    for pair in range(HEADS // 2):
        low = att_all[2 * pair].astype(F32)
        high = att_all[2 * pair + 1].astype(F32)
        slab = jnp.where(left, swap(low), high)
        att[:, 128 * pair : 128 * pair + 128] = slab.astype(BF)
        att_turned[128 * pair : 128 * pair + 128, :] = jnp.transpose(slab).astype(BF)
    for block in range(4):
        columns = pl.ds(256 * block, 256)
        behind = pl.ds(D + 256 * block, 256)
        shift = dot(att[...], wo[:, columns])
        factor = jnp.exp(-dot(att[...], wo[:, behind]))
        upstream = up[:, columns].astype(F32)
        latent = (act[:, columns].astype(F32) - shift) * factor
        scaled = upstream * factor
        carry_part[:, columns] = scaled
        affine_grad[:, columns] = (-scaled).astype(BF)
        affine_grad[:, behind] = (1.0 - upstream * latent).astype(BF)

    def g_copy(head):
        k = lax.rem(head - mine + HEADS, HEADS)
        return remote(g_pack.at[head], g_all.at[chunk_rows(mine)], g_send.at[k], g_recv.at[k], 4 * head + group)

    def g_own():
        return pltpu.make_async_copy(g_pack.at[mine], g_all.at[chunk_rows(mine)], local.at[1])

    for block in range(2):
        g = dot_t(affine_grad[...], wo[pl.ds(256 * block, 256), :])
        for half in range(2):
            head = 4 * block + 2 * half
            slab = g[:, 128 * half : 128 * half + 128]
            g_pack[head] = jnp.where(left, 0.0, swap(slab)).astype(BF)
            g_pack[head + 1] = jnp.where(left, 0.0, slab).astype(BF)
        for head in range(4 * block, 4 * block + 4):

            @pl.when(mine != head)
            def _():
                g_copy(head).start()

    g_own().start()
    for block in range(8):
        columns = pl.ds(256 * block, 256)
        term = dot(att_turned[...], affine_grad[:, columns]).astype(BF)
        for owner in range(N_SEQ):
            for half in range(2):
                stream, row = OUT_PLACES[2 * block + half]
                out_sum.terms[stream][slot(stream, owner, bits), row : row + 16, :] = term[
                    16 * owner : 16 * owner + 16, 128 * half : 128 * half + 128
                ]
    for stream in range(5):
        out_sum.hop(stream, 0).start()

    g_own().wait()
    loop(1, HEADS, lambda k: g_copy(lax.rem(mine + k, HEADS)).wait_recv())

    def attend_back(a, last):
        rows = pair_rows(a)
        q = q_all[rows, :]
        g = g_all[rows, :]
        one_over = inverse[rows, :][:, :1]
        correction = jnp.sum(g.astype(F32) * out[rows, :].astype(F32), axis=-1, keepdims=True)
        q_turned = jnp.transpose(q.astype(F32))[:HEAD_DIM].astype(BF)
        g_turned = jnp.transpose(g.astype(F32))[HEAD_DIM:].astype(BF)

        def tile(j, acc, masked, width=WIDE):
            at = tile_at(j, width)
            block = kv[at, :]
            p = jnp.exp(dot_t(q, block)) * one_over
            if masked:
                p = jnp.where(seen(a, j, width), p, 0.0)
            ds = (p * (dot_t(g, block) - correction)).astype(BF)
            total[:HEAD_DIM, at] += dot(q_turned, ds)
            total[HEAD_DIM:, at] += dot(g_turned, p.astype(BF))
            return acc + dot(ds, block)

        acc = jnp.zeros((2 * TOK, 128), F32)
        acc = lax.fori_loop(0, 2 * a, lambda j, c: tile(j, c, False), acc)
        acc = tile(2 * a, acc, True)
        acc = tile(2 * a + 1, acc, True)
        acc = tile(2 * a + 2, acc, True, WIDE // 2 if last else WIDE)
        dq[rows, :] = (acc * 0.125).astype(BF)

    def dq_copy(chunk):
        k = lax.rem(chunk - mine + HEADS, HEADS)
        return remote(dq.at[chunk_rows(chunk)], dq_all.at[mine], dq_send.at[k], dq_recv.at[k], 4 * chunk + group)

    def dq_own():
        return pltpu.make_async_copy(dq.at[chunk_rows(mine)], dq_all.at[mine], local.at[2])

    def dkv_copy(owner):
        k = lax.rem(owner - me + N_SEQ, N_SEQ)
        return remote(dkv.at[chunk_rows(owner)], dkv_parts.at[me], dkv_send.at[k], dkv_recv.at[k], owner)

    def dkv_own():
        return pltpu.make_async_copy(dkv.at[chunk_rows(me)], dkv_parts.at[me], local.at[3])

    def send_keys(owner):
        @pl.when(owner != me)
        def _():
            dkv_copy(owner).start()

        @pl.when(owner == me)
        def _():
            dkv_own().start()

    for a in (3, 2, 1, 0):
        attend_back(a, a == 3)
        for half in range(2):
            chunk = 2 * a + half

            @pl.when(chunk != mine)
            def _():
                dq_copy(chunk).start()

            @pl.when(chunk == mine)
            def _():
                dq_own().start()

        first_tile = 2 * a + 1 if a else 0
        end_tile = 2 * a + 3
        for half_tile in range(2 * first_tile, min(2 * end_tile, TOKENS // 256)):
            at = pl.ds(256 * half_tile, 256)
            dkv[at, :] = jnp.transpose(total[:, at]).astype(BF)
        first_owner = -(-WIDE * first_tile // TOK)
        end_owner = min(-(-WIDE * end_tile // TOK), N_SEQ)
        loop(first_owner, end_owner, send_keys)
        for stream in range(5):
            out_sum.advance(stream, 3 - a)

    def unit_back(grad, raw):
        scale = unit_scale(raw, left)
        unit = raw * scale
        return scale * (grad - unit * (per_head_sum(grad * unit, left) * (1.0 / HEAD_DIM)))

    def keys_of(head):
        part = [dkv_parts[4 * head + i].astype(F32) for i in range(4)]
        return (part[0] + part[1]) + (part[2] + part[3])

    def term_of(which):
        for block in range(2):
            term = dot(normed_turned[...], grads[which, :, 256 * block : 256 * block + 256]).astype(BF)
            for owner in range(N_SEQ):
                for part in range(4):
                    slab, half = part // 2, part % 2
                    stream, row = TERM_PLACES[8 * which + 4 * block + 2 * slab + half]
                    top = 32 * owner + 16 * half
                    term_sum.terms[stream][slot(stream, owner, bits), row : row + 16, :] = term[
                        top : top + 16, 128 * slab : 128 * slab + 128
                    ]

    dq_own().wait()
    loop(1, HEADS, lambda k: dq_copy(lax.rem(mine + k, HEADS)).wait_recv())
    for pair in range(HEADS // 2):
        at = pl.ds(128 * pair, 128)
        low, high = dq_all[2 * pair].astype(F32), dq_all[2 * pair + 1].astype(F32)
        grads[0, :, at] = unit_back(jnp.where(left, low, swap(high)), q_raw[:, at]).astype(BF)
    term_of(0)
    term_sum.hop(0, 0).start()
    for block in range(4):
        at = pl.ds(256 * block, 256)
        gn[:, at] = dot_t(grads[0], wq[at, :])
    dkv_own().wait()
    loop(1, N_SEQ, lambda k: dkv_copy(lax.rem(me + k, N_SEQ)).wait_recv())
    for pair in range(HEADS // 2):
        at = pl.ds(128 * pair, 128)
        low, high = keys_of(2 * pair), keys_of(2 * pair + 1)
        grads[1, :, at] = unit_back(jnp.where(left, low, swap(high)), k_raw[:, at]).astype(BF)
        grads[2, :, at] = jnp.where(left, swap(low), high).astype(BF)
    term_of(1)
    term_sum.hop(1, 0).start()
    term_sum.hop(2, 0).start()
    term_of(2)
    term_sum.hop(3, 0).start()
    term_sum.hop(4, 0).start()
    for block in range(4):
        at = pl.ds(256 * block, 256)
        gn[:, at] += dot_t(grads[1], wk[at, :]) + dot_t(grads[2], wv[at, :])
    field = act[...].astype(F32)
    row_scale = lax.rsqrt(jnp.mean(field * field, axis=-1, keepdims=True) + EPSILON)
    unit = field * row_scale
    grad_normed = gn[...]
    mean = jnp.mean(grad_normed * unit, axis=-1, keepdims=True)
    grad_input[...] = (carry_part[...] + row_scale * (grad_normed - unit * mean)).astype(BF)
    carry = pltpu.make_async_remote_copy(
        src_ref=grad_input, dst_ref=moved, send_sem=carry_sem.at[0], recv_sem=carry_sem.at[1],
        device_id={"section": before, "seq": across}, device_id_type=MESH,
    )
    carry.start()
    for stream in range(5):
        result = out_sum.result(stream)
        for part in range(16):
            if OUT_PLACES[part][0] == stream:
                row = OUT_PLACES[part][1]
                sum_out[:, 128 * part : 128 * part + 128] = result[row : row + 16]
    for step in range(4):
        for stream in range(5):
            term_sum.advance(stream, step)
    for stream in range(5):
        result = term_sum.result(stream)
        for part in range(24):
            if TERM_PLACES[part][0] == stream:
                row = TERM_PLACES[part][1]
                target = (sum_q, sum_k, sum_v)[part // 8]
                column, top = 128 * (part % 8 // 2), 16 * (part % 2)
                target[top : top + 16, column : column + 128] = result[row : row + 16]
    carry.wait()

    def left_all(k):
        kv_copy(k).wait_send()
        q_copy(k).wait_send()
        att_copy(lax.rem(mine + k, HEADS)).wait_send()
        g_copy(lax.rem(mine + k, HEADS)).wait_send()
        dq_copy(lax.rem(mine + k, HEADS)).wait_send()

    loop(1, HEADS, left_all)

    def left_z(k):
        for way in range(2):
            z_copy(k, way).wait_send()
            f_copy(k, way).wait_send()

    loop(0, HEADS, left_z)
    loop(1, N_SEQ, lambda k: dkv_copy(lax.rem(me + k, N_SEQ)).wait_send())
    out_sum.drain()
    term_sum.drain()


def whole_layer(*operands):
    eight, full = (HEADS * TOK, 128), (TOK, D)
    scratch = [
        (full, BF), (full, BF), ((D, INNER), BF), ((D, INNER), BF), ((D, INNER), BF), ((INNER, 2 * D), BF),
        (full, BF), ((D, TOK), BF), ((TOK, INNER), F32), ((TOK, INNER), F32), ((HEADS, TOK, 128), BF), ((HEADS, TOK, 128), BF),
        ((KEYS, 128), BF), (eight, BF), (eight, BF), ((TOKENS, 1), jnp.int32), (eight, BF), (eight, F32),
        ((HEADS, TOK, 128), BF), ((TOK, INNER), BF), ((INNER, TOK), BF), ((TOK, 2 * D), BF), ((HEADS, TOK, 128), BF), (full, F32),
        ((128, KEYS), F32), ((KEYS, 128), BF), (eight, BF), ((N_SEQ, TOK, 128), BF), ((HEADS, TOK, 128), BF),
        ((3, TOK, INNER), BF), (full, F32), (full, BF),
    ]
    dma = pltpu.SemaphoreType.DMA
    return pl.pallas_call(
        layer_body,
        out_shape=[jax.ShapeDtypeStruct((32, INNER), F32)] * 3
        + [jax.ShapeDtypeStruct((16, 2 * D), F32), jax.ShapeDtypeStruct((TOK, D), BF)],
        in_specs=[ANY] * 6 + [VMEM],
        out_specs=[VMEM] * 5,
        scratch_shapes=[pltpu.VMEM(shape, dtype) for shape, dtype in scratch]
        + halving_scratch(OUT_ROWS)
        + halving_scratch(TERM_ROWS)
        + [dma((6,)), dma((8,)), dma((8,)), dma((8,)), dma((8,)), dma((2, 8)), dma((2, 8)), dma((2, 8)), dma((2, 8))]
        + [dma((8,)), dma((8,)), dma((8,)), dma((8,)), dma((8,)), dma((8,)), dma((N_SEQ,)), dma((N_SEQ,)), dma((4,)), dma((2,))],
        compiler_params=pltpu.CompilerParams(collective_id=1, has_side_effects=True, vmem_limit_bytes=BIG),
        name="layer",
    )(*operands)


def hand_out_body(sum_q, sum_k, sum_v, sum_out, moved, flip, carry, out_q, out_k, out_v, out_out):
    out_q[...] = sum_q[...]
    out_k[...] = sum_k[...]
    out_v[...] = sum_v[...]
    out_out[...] = sum_out[...]
    turned = (flip[...] == lax.broadcasted_iota(jnp.int32, (TOK, TOK), 0)).astype(F32)
    chosen = jnp.transpose(turned).astype(BF)
    last = (lax.axis_index("section") + jnp.zeros((TOK, 1), jnp.int32)) == 3
    for block in range(4):
        at = pl.ds(256 * block, 256)
        carry[:, at] = jnp.where(last, 0.0, dot(chosen, moved[:, at])).astype(BF)


def hand_out(*operands):
    return pl.pallas_call(
        hand_out_body,
        out_shape=[jax.ShapeDtypeStruct((TOK, D), BF)]
        + [jax.ShapeDtypeStruct((32, INNER), F32)] * 3
        + [jax.ShapeDtypeStruct((16, 2 * D), F32)],
        in_specs=[VMEM] * 6,
        out_specs=[VMEM] * 5,
        name="hand_out",
    )(*operands)


def shards(activations, incoming, w_query, w_key, w_value, w_out, block_ids, flip_order):
    sums = whole_layer(
        activations[0], incoming[0], w_query[0], w_key[0], w_value[0], w_out[0], block_ids.reshape(TOKENS // 128, 128)
    )
    results = hand_out(*sums, flip_order)
    return tuple(result[None] for result in results)


def solution(mesh):
    by_both = P("section", "seq", None)
    by_layer = P("section", None, None)
    in_specs = (by_both, by_both, by_layer, by_layer, by_layer, by_layer, P(), P("section", None))
    return jax.shard_map(shards, mesh=mesh, in_specs=in_specs, out_specs=(by_both,) * 5, check_vma=False)
```

time: 1470 us -> 125 us (0.09)
  waiting for transfers between devices: 1250 us -> 0 us
  matrix products: 127 us -> 0 us
  Pallas kernels: 0 us -> 125 us
  local copies, waits for them, and re-layouts: 60.4 us -> 0 us
    reduce_scatter x4 -> x0, waiting for transfers between devices: 611 us -> none  [the longest x1 162 us: shards(): lax.psum_scatter(out_term.astype(jnp.bfloat16), 'seq', scatter_dimension=...]
    unnamed x10 -> x0, waiting for transfers between devices: 320 us -> none
    all_gather x2 -> x0, waiting for transfers between devices: 299 us -> none  [the longest x1 154 us: shards(): lax.all_gather(keys, 'seq', axis=0, tiled=True)]
    dot_general x68 -> x0, matrix products: 127 us -> none  [the longest x16 32.4 us: probabilities(): jnp.dot(query_part, key_part.T, preferred_element_type=jnp.float32) * scale]
    pallas_call x0 -> x2, Pallas kernels: none -> 125 us  [the longest x1 122 us: whole_layer(): pl.pallas_call(layer_body, out_shape=[jax.ShapeDtypeStruct((32, INNER), F...]
    unnamed x58 -> x0, local copies, waits for them, and re-layouts: 42.5 us -> none
    ppermute x6 -> x0, waiting for transfers between devices: 22.7 us -> none  [the longest x5 20.5 us: partner(): return lax.ppermute(block, axis, route)]
  transfers between devices with their start and end apart: 14 -> 0, of which waited for: 12 -> 0; matrix products, arithmetic and copies ran while one was open for 3% -> 0% of each run, Pallas kernels for 0% -> 0%
where the time goes in v3:
time: 125 us
  Pallas kernels  125 us (100%)
    pallas_call x1, Pallas kernels, whole_layer(): pl.pallas_call(layer_body, out_shape=[jax.ShapeDtypeStruct((32, INNER), F...  122 us

profile of v3, /device:TPU:0, one launch (start us, length us, event | category | flops | bytes accessed | tf_op | source)
XLA Modules:
  0.0 125.2 jit_solution(5563366514265177271)
XLA Ops:
  0.6 122.4 %layer.1 = (f32[32,512]{1,0:T(8,128)}, f32[32,512]{1,0:T(8,128)}, f32[32,512]{1,0:T(8,128)}, f32[16,2048]{1,0:T(8,128)}, bf16[136,1024]{1,0:T(8,128)(2,1)}) custom-call(bf16[136,1024]{1,0:T(8,128)(2,1)} %bitcast.16, bf16[136,1024]{1,0:T(8,128)(2,1)} %bitcast.17, bf16[1024,512]{1,0:T(8,128)(2,1)} %bitcast.13, bf16[1024,512]{1,0:T(8,128)(2,1)} %bitcast.14, ...), custom_call_target="tpu_custom_call" | custom-call | tf_op jit(solution)/shard_map/layer/pallas_call | solution.py:623
  123.0 2.2 %hand_out.1 = (bf16[136,1024]{1,0:T(8,128)(2,1)}, f32[32,512]{1,0:T(8,128)}, f32[32,512]{1,0:T(8,128)}, f32[32,512]{1,0:T(8,128)}, f32[16,2048]{1,0:T(8,128)}) custom-call(f32[32,512]{1,0:T(8,128)} %get-tuple-element.15.sum_q, f32[32,512]{1,0:T(8,128)} %get-tuple-element.16.sum_k, f32[32,512]{1,0:T(8,128)} %get-tuple-element.17.sum_v, ...), custom_call_target="tpu_custom_call" | custom-call | tf_op jit(solution)/shard_map/hand_out/pallas_call | solution.py:653

commit v4 on v3

--- a/solution.py
+++ b/solution.py
@@ -13,9 +13,9 @@
 TOKENS = 4352
 D = 1024
 INNER = 512
-WIDE = 512
-KEYS = 9 * WIDE
-NEAR_ROWS = 64
+CLASS = 8 * TOK
+CLASS_ROWS = 1152
+HALF = CLASS // 2
 BF = jnp.bfloat16
 F32 = jnp.float32
 MESH = pl.DeviceIdType.MESH
@@ -168,11 +168,13 @@
     act, up, wq, wk, wv, wo = take(6)
     normed, normed_turned, q_raw, k_raw, q_pack, kv_pack = take(6)
     kv, q_all, g_all, q_ids, out, inverse, att_all, att, att_turned, affine_grad, g_pack, carry_part = take(12)
-    total, dkv, dq, dkv_parts, dq_all, grads, gn, grad_input = take(8)
+    total, dkv, dq, dkv_all, dq_all, grads, gn, grad_input = take(8)
+    padded_ids, q_end, tokens, summed, mass, q_turned, g_turned, correction, from_back, from_next = take(10)
+    far_half = take(2)
     out_refs = take(17)
     term_refs = take(17)
     (load, kv_send, kv_recv, q_send, q_recv, z_send, z_recv, f_send, f_recv, att_send, att_recv,
-     g_send, g_recv, dq_send, dq_recv, dkv_send, dkv_recv, local, carry_sem) = refs
+     g_send, g_recv, dq_send, dq_recv, dkv_send, dkv_recv, local, carry_sem, back_send, back_recv) = refs
 
     me = lax.axis_index("seq")
     section = lax.axis_index("section")
@@ -246,7 +248,7 @@
 
     def kv_copy(k):
         peer = lax.rem(mine + k, HEADS)
-        return remote(kv_pack.at[peer], kv.at[chunk_rows(me)], kv_send.at[k], kv_recv.at[k], 4 * peer + group)
+        return remote(kv_pack.at[peer], kv.at[0, chunk_rows(mine)], kv_send.at[k], kv_recv.at[k], 4 * peer + group)
 
     def q_copy(k):
         peer = lax.rem(mine + k, HEADS)
@@ -254,125 +256,133 @@
 
     loop(1, HEADS, lambda k: kv_copy(k).start())
     own = [
-        pltpu.make_async_copy(kv_pack.at[mine], kv.at[chunk_rows(me)], local.at[0]),
+        pltpu.make_async_copy(kv_pack.at[mine], kv.at[0, chunk_rows(mine)], local.at[0]),
         pltpu.make_async_copy(q_pack.at[mine], q_all.at[chunk_rows(mine)], local.at[1]),
     ]
     for copy in own:
         copy.start()
     loop(1, HEADS, lambda k: q_copy(k).start())
-    kv[pl.ds(TOKENS, KEYS - TOKENS), :] = jnp.zeros((KEYS - TOKENS, 128), BF)
-    total[...] = jnp.zeros_like(total)
+    for place_of in range(4):
+        kv[place_of, CLASS:, :] = jnp.zeros((CLASS_ROWS - CLASS, 128), BF)
     own[0].wait()
 
-    def row_of(k, place):
-        return 4 * lax.rem(mine - k + HEADS, HEADS) + place
-
-    def z_copy(k, way):
-        rows = kv.at[chunk_rows(row_of(k, group))]
-        return remote(rows, rows, z_send.at[way, k], z_recv.at[way, k], z_back if way else z_next)
-
-    def f_copy(k, way):
-        token = row_of(k, lax.rem(group + (1 if way else 3), 4)) * TOK
-        if way:
-            rows = kv.at[pl.ds(pl.multiple_of(token + NEAR_ROWS, 8), TOK - NEAR_ROWS)]
-        else:
-            rows = kv.at[pl.ds(pl.multiple_of(token, 8), NEAR_ROWS)]
-        return remote(rows, rows, f_send.at[way, k], f_recv.at[way, k], z_back if way else z_next)
-
-    def relay(k):
+    def z_copy(chunk, way):
+        return remote(
+            kv.at[0, chunk_rows(chunk)], kv.at[1 + way, chunk_rows(chunk)],
+            z_send.at[way, chunk], z_recv.at[way, chunk], z_back if way else z_next,
+        )
+
+    def f_copy(chunk, way):
+        return remote(
+            kv.at[1 + way, chunk_rows(chunk)], kv.at[3, chunk_rows(chunk)],
+            f_send.at[chunk], f_recv.at[chunk], z_back if way else z_next,
+        )
+
+    def relay(chunk):
         for way in range(2):
-            z_copy(k, way).start()
-
-    def forward(k):
-        for way in range(2):
-            z_copy(k, way).wait_recv()
-            f_copy(k, way).start()
-
-    relay(0)
+            z_copy(chunk, way).start()
+
+    relay(mine)
 
     def pipe(k):
         kv_copy(k).wait_recv()
-        relay(k)
-        forward(k - 1)
+        relay(lax.rem(mine - k + HEADS, HEADS))
 
     loop(1, HEADS, pipe)
 
     turned = jnp.transpose(ids[...].astype(F32)).astype(jnp.int32)
     for row in range(TOKENS // 128):
         q_ids[128 * row : 128 * row + 128, :] = turned[:, row : row + 1]
+    padded_ids[: TOKENS // 128, :] = ids[...]
+    padded_ids[TOKENS // 128 :, :] = jnp.full((40 - TOKENS // 128, 128), TOKENS, jnp.int32)
+    for chunk in range(HEADS):
+        first = pl.multiple_of((4 * chunk + group) * TOK, 8)
+        row = lax.div(first, 128)
+        column = q_ids[pl.ds(first, TOK), :]
+        seen = jnp.zeros((TOK, 128), F32)
+        for behind in range(5):
+            seen = seen + jnp.where(padded_ids[pl.ds(row + behind, 1), :] <= column, 1.0, 0.0)
+        count = jnp.sum(seen, axis=-1, keepdims=True).astype(jnp.int32)
+        q_end[TOK * chunk : TOK * chunk + TOK, :] = count + 128 * row
+    lane = lax.broadcasted_iota(jnp.int32, (1, CLASS_ROWS), 1)
+    skipped = jnp.zeros((1, CLASS_ROWS), jnp.int32)
+    for chunk in range(1, HEADS + 1):
+        skipped = skipped + jnp.where(lane >= TOK * chunk, 3 * TOK, 0)
+    for place_of, apart in enumerate((0, 3, 1, 2)):
+        tokens[place_of] = lane + skipped + TOK * lax.rem(group + apart, 4)
     for block in range(8):
         at = pl.ds(128 * block, 128)
         normed_turned[at, :] = jnp.transpose(normed[:, at].astype(F32)).astype(BF)
     own[1].wait()
     loop(1, HEADS, lambda k: q_copy(k).wait_recv())
-    forward(HEADS - 1)
-
-    def landed(k):
-        for way in range(2):
-            f_copy(k, way).wait_recv()
-
-    loop(0, HEADS, landed)
-
-    def seen(a, j, width):
-        columns = []
-        for half in range(2):
-            first = pl.multiple_of((4 * (2 * a + half) + group) * TOK, 8)
-            columns.append(q_ids[pl.ds(first, TOK), :])
-        column = jnp.concatenate(columns, axis=0)
-        return jnp.concatenate(
-            [ids[pl.ds(4 * j + part, 1), :] <= column for part in range(width // 128)], axis=1
-        )
+
+    def tiles(a):
+        whole = [(512 * part, min(512, 256 * a - 512 * part), False) for part in range(-(-a // 2))]
+        return whole + [(256 * a, 384 if a == 3 else 512, True)]
 
     def pair_rows(a):
-        return pl.ds(a * 2 * TOK if isinstance(a, int) else pl.multiple_of(a * 2 * TOK, 16), 2 * TOK)
-
-    def tile_at(j, width):
-        return pl.ds(j * WIDE if isinstance(j, int) else pl.multiple_of(j * WIDE, WIDE), width)
-
-    def attend(a, last):
-        rows = pair_rows(a)
-        q = q_all[rows, :]
-
-        def tile(j, carry, masked, width=WIDE):
-            summed, mass = carry
-            block = kv[tile_at(j, width), :]
-            p = jnp.exp(dot_t(q, block))
-            if masked:
-                p = jnp.where(seen(a, j, width), p, 0.0)
-            for part in range(width // 128):
-                mass = mass + p[:, 128 * part : 128 * part + 128]
-            return summed + dot(p.astype(BF), block), mass
-
-        zero = jnp.zeros((2 * TOK, 128), F32)
-        carry = lax.fori_loop(0, 2 * a, lambda j, c: tile(j, c, False), (zero, zero))
-        carry = tile(2 * a, carry, True)
-        carry = tile(2 * a + 1, carry, True)
-        summed, mass = tile(2 * a + 2, carry, True, WIDE // 2 if last else WIDE)
-        one_over = 1.0 / jnp.sum(mass, axis=-1, keepdims=True)
-        result = (summed * one_over).astype(BF)
-        out[rows, :] = result
-        inverse[rows, :] = jnp.broadcast_to(one_over, (2 * TOK, 128))
-        return result
+        return pl.ds(2 * TOK * a, 2 * TOK)
+
+    def shown(a, place_of, first, width):
+        return tokens[place_of][:, first : first + width] < q_end[pair_rows(a), :]
 
     def att_copy(chunk):
         k = lax.rem(chunk - mine + HEADS, HEADS)
         return remote(out.at[chunk_rows(chunk)], att_all.at[mine], att_send.at[k], att_recv.at[k], 4 * chunk + group)
 
-    def attend_and_send(a, last):
-        attend(a, last)
-        for half in range(2):
-            chunk = 2 * a + half
-
-            @pl.when(chunk != mine)
+    summed[...] = jnp.zeros_like(summed)
+    mass[...] = jnp.zeros_like(mass)
+
+    def attend(place_of):
+        @pl.when(place_of == 1)
+        def _():
+            def pass_on(chunk):
+                z_copy(chunk, 0).wait_recv()
+                f_copy(chunk, 0).start()
+                z_copy(chunk + 4, 1).wait_recv()
+                f_copy(chunk + 4, 1).start()
+
+            loop(0, 4, pass_on)
+            loop(4, 8, lambda chunk: z_copy(chunk, 0).wait_recv())
+
+        @pl.when(place_of == 2)
+        def _():
+            loop(0, 4, lambda chunk: z_copy(chunk, 1).wait_recv())
+
+        @pl.when(place_of == 3)
+        def _():
+            loop(0, 4, lambda chunk: (f_copy(chunk, 0).wait_recv(), f_copy(chunk + 4, 1).wait_recv()))
+
+        for a in range(4):
+            rows = pair_rows(a)
+            q = q_all[rows, :]
+            for first, width, masked in tiles(a):
+                block = kv[place_of, first : first + width, :]
+                p = jnp.exp(dot_t(q, block))
+                if masked:
+                    p = jnp.where(shown(a, place_of, first, width), p, 0.0)
+                part_mass = p[:, :128]
+                for part in range(1, width // 128):
+                    part_mass = part_mass + p[:, 128 * part : 128 * part + 128]
+                mass[rows, :] += part_mass
+                summed[rows, :] += dot(p.astype(BF), block)
+
+            @pl.when(place_of == 3)
             def _():
-                att_copy(chunk).start()
-
-            @pl.when(chunk == mine)
-            def _():
-                pltpu.make_async_copy(out.at[chunk_rows(chunk)], att_all.at[mine], local.at[0]).start()
-
-    loop(0, 3, lambda a: attend_and_send(a, False))
-    attend_and_send(3, True)
+                one_over = 1.0 / jnp.sum(mass[rows, :], axis=-1, keepdims=True)
+                out[rows, :] = (summed[rows, :] * one_over).astype(BF)
+                inverse[rows, :] = one_over
+                for chunk in (2 * a, 2 * a + 1):
+
+                    @pl.when(mine != chunk)
+                    def _():
+                        att_copy(chunk).start()
+
+                    @pl.when(mine == chunk)
+                    def _():
+                        pltpu.make_async_copy(out.at[chunk_rows(chunk)], att_all.at[mine], local.at[0]).start()
+
+    loop(0, 4, attend)
 
     loads[4].wait()
     loads[5].wait()
@@ -437,32 +447,13 @@
     g_own().wait()
     loop(1, HEADS, lambda k: g_copy(lax.rem(mine + k, HEADS)).wait_recv())
 
-    def attend_back(a, last):
+    for a in range(4):
         rows = pair_rows(a)
-        q = q_all[rows, :]
-        g = g_all[rows, :]
-        one_over = inverse[rows, :][:, :1]
-        correction = jnp.sum(g.astype(F32) * out[rows, :].astype(F32), axis=-1, keepdims=True)
-        q_turned = jnp.transpose(q.astype(F32))[:HEAD_DIM].astype(BF)
-        g_turned = jnp.transpose(g.astype(F32))[HEAD_DIM:].astype(BF)
-
-        def tile(j, acc, masked, width=WIDE):
-            at = tile_at(j, width)
-            block = kv[at, :]
-            p = jnp.exp(dot_t(q, block)) * one_over
-            if masked:
-                p = jnp.where(seen(a, j, width), p, 0.0)
-            ds = (p * (dot_t(g, block) - correction)).astype(BF)
-            total[:HEAD_DIM, at] += dot(q_turned, ds)
-            total[HEAD_DIM:, at] += dot(g_turned, p.astype(BF))
-            return acc + dot(ds, block)
-
-        acc = jnp.zeros((2 * TOK, 128), F32)
-        acc = lax.fori_loop(0, 2 * a, lambda j, c: tile(j, c, False), acc)
-        acc = tile(2 * a, acc, True)
-        acc = tile(2 * a + 1, acc, True)
-        acc = tile(2 * a + 2, acc, True, WIDE // 2 if last else WIDE)
-        dq[rows, :] = (acc * 0.125).astype(BF)
+        g = g_all[rows, :].astype(F32)
+        correction[rows, :] = jnp.sum(g * out[rows, :].astype(F32), axis=-1, keepdims=True)
+        q_turned[a] = jnp.transpose(q_all[rows, :].astype(F32))[:HEAD_DIM].astype(BF)
+        g_turned[a] = jnp.transpose(g)[HEAD_DIM:].astype(BF)
+    summed[...] = jnp.zeros_like(summed)
 
     def dq_copy(chunk):
         k = lax.rem(chunk - mine + HEADS, HEADS)
@@ -471,45 +462,103 @@
     def dq_own():
         return pltpu.make_async_copy(dq.at[chunk_rows(mine)], dq_all.at[mine], local.at[2])
 
-    def dkv_copy(owner):
-        k = lax.rem(owner - me + N_SEQ, N_SEQ)
-        return remote(dkv.at[chunk_rows(owner)], dkv_parts.at[me], dkv_send.at[k], dkv_recv.at[k], owner)
+    def far_copy(way):
+        rows = pl.ds(HALF * way, HALF)
+        return remote(dkv.at[3, rows], far_half[way], back_send.at[way], back_recv.at[way], z_back if way else z_next)
+
+    def class_copy(way):
+        if way:
+            return remote(dkv.at[1], from_next, back_send.at[2], back_recv.at[2], z_back)
+        return remote(dkv.at[2], from_back, back_send.at[3], back_recv.at[3], z_next)
+
+    def dkv_copy(k):
+        peer = lax.rem(mine + k, HEADS)
+        return remote(dkv.at[0, chunk_rows(peer)], dkv_all.at[mine], dkv_send.at[k], dkv_recv.at[k], 4 * peer + group)
 
     def dkv_own():
-        return pltpu.make_async_copy(dkv.at[chunk_rows(me)], dkv_parts.at[me], local.at[3])
-
-    def send_keys(owner):
-        @pl.when(owner != me)
+        return pltpu.make_async_copy(dkv.at[0, chunk_rows(mine)], dkv_all.at[mine], local.at[3])
+
+    blocks = [(128 * part, 128) for part in range(8)] + [(1024, CLASS - 1024)]
+
+    def settle(place_of, extra):
+        for first, width in blocks:
+            value = jnp.transpose(total[:, first : first + 128])[:width]
+            for source, low, high in extra:
+                begin, end = max(first, low), min(first + width, high)
+                if begin == first and end == first + width:
+                    value = value + source[first - low : first - low + width, :].astype(F32)
+                elif begin < end:
+                    inside = source[begin - low : end - low, :].astype(F32)
+                    zeros = [jnp.zeros((begin - first, 128), F32), inside, jnp.zeros((first + width - end, 128), F32)]
+                    value = value + jnp.concatenate([z for z in zeros if z.shape[0]], axis=0)
+            dkv[place_of, first : first + width, :] = value.astype(BF)
+
+    def attend_back(n):
+        place_of = 3 - n
+        total[...] = jnp.zeros_like(total)
+        for a in (3, 2, 1, 0):
+            rows = pair_rows(a)
+            q = q_all[rows, :]
+            g = g_all[rows, :]
+            one_over = inverse[rows, :]
+            corr = correction[rows, :]
+            for first, width, masked in tiles(a):
+                block = kv[place_of, first : first + width, :]
+                p = jnp.exp(dot_t(q, block)) * one_over
+                if masked:
+                    p = jnp.where(shown(a, place_of, first, width), p, 0.0)
+                ds = (p * (dot_t(g, block) - corr)).astype(BF)
+                total[:HEAD_DIM, first : first + width] += dot(q_turned[a], ds)
+                total[HEAD_DIM:, first : first + width] += dot(g_turned[a], p.astype(BF))
+                summed[rows, :] += dot(ds, block)
+
+            @pl.when(n == 3)
+            def _():
+                dq[rows, :] = (summed[rows, :] * 0.125).astype(BF)
+                for chunk in (2 * a, 2 * a + 1):
+
+                    @pl.when(mine != chunk)
+                    def _():
+                        dq_copy(chunk).start()
+
+                    @pl.when(mine == chunk)
+                    def _():
+                        dq_own().start()
+
+        @pl.when(n == 0)
         def _():
-            dkv_copy(owner).start()
-
-        @pl.when(owner == me)
+            settle(3, [])
+            for way in range(2):
+                far_copy(way).start()
+
+        @pl.when(n == 1)
         def _():
+            far_copy(0).wait_recv()
+            settle(2, [(far_half[0], 0, HALF)])
+            class_copy(0).start()
+
+        @pl.when(n == 2)
+        def _():
+            far_copy(1).wait_recv()
+            settle(1, [(far_half[1], HALF, CLASS)])
+            class_copy(1).start()
+
+        @pl.when(n == 3)
+        def _():
+            for way in range(2):
+                class_copy(way).wait_recv()
+            settle(0, [(from_back, 0, CLASS), (from_next, 0, CLASS)])
+            loop(1, HEADS, lambda k: dkv_copy(k).start())
             dkv_own().start()
 
-    for a in (3, 2, 1, 0):
-        attend_back(a, a == 3)
-        for half in range(2):
-            chunk = 2 * a + half
-
-            @pl.when(chunk != mine)
+        for step in range(4):
+
+            @pl.when(n == step)
             def _():
-                dq_copy(chunk).start()
-
-            @pl.when(chunk == mine)
-            def _():
-                dq_own().start()
-
-        first_tile = 2 * a + 1 if a else 0
-        end_tile = 2 * a + 3
-        for half_tile in range(2 * first_tile, min(2 * end_tile, TOKENS // 256)):
-            at = pl.ds(256 * half_tile, 256)
-            dkv[at, :] = jnp.transpose(total[:, at]).astype(BF)
-        first_owner = -(-WIDE * first_tile // TOK)
-        end_owner = min(-(-WIDE * end_tile // TOK), N_SEQ)
-        loop(first_owner, end_owner, send_keys)
-        for stream in range(5):
-            out_sum.advance(stream, 3 - a)
+                for stream in range(5):
+                    out_sum.advance(stream, step)
+
+    loop(0, 4, attend_back)
 
     def unit_back(grad, raw):
         scale = unit_scale(raw, left)
@@ -517,8 +566,7 @@
         return scale * (grad - unit * (per_head_sum(grad * unit, left) * (1.0 / HEAD_DIM)))
 
     def keys_of(head):
-        part = [dkv_parts[4 * head + i].astype(F32) for i in range(4)]
-        return (part[0] + part[1]) + (part[2] + part[3])
+        return dkv_all[head].astype(F32)
 
     def term_of(which):
         for block in range(2):
@@ -544,7 +592,7 @@
         at = pl.ds(256 * block, 256)
         gn[:, at] = dot_t(grads[0], wq[at, :])
     dkv_own().wait()
-    loop(1, N_SEQ, lambda k: dkv_copy(lax.rem(me + k, N_SEQ)).wait_recv())
+    loop(1, HEADS, lambda k: dkv_copy(k).wait_recv())
     for pair in range(HEADS // 2):
         at = pl.ds(128 * pair, 128)
         low, high = keys_of(2 * pair), keys_of(2 * pair + 1)
@@ -595,16 +643,19 @@
         att_copy(lax.rem(mine + k, HEADS)).wait_send()
         g_copy(lax.rem(mine + k, HEADS)).wait_send()
         dq_copy(lax.rem(mine + k, HEADS)).wait_send()
+        dkv_copy(k).wait_send()
 
     loop(1, HEADS, left_all)
 
-    def left_z(k):
+    def left_z(chunk):
         for way in range(2):
-            z_copy(k, way).wait_send()
-            f_copy(k, way).wait_send()
+            z_copy(chunk, way).wait_send()
 
     loop(0, HEADS, left_z)
-    loop(1, N_SEQ, lambda k: dkv_copy(lax.rem(me + k, N_SEQ)).wait_send())
+    loop(0, 4, lambda chunk: (f_copy(chunk, 0).wait_send(), f_copy(chunk + 4, 1).wait_send()))
+    for way in range(2):
+        far_copy(way).wait_send()
+        class_copy(way).wait_send()
     out_sum.drain()
     term_sum.drain()
 
@@ -614,10 +665,13 @@
     scratch = [
         (full, BF), (full, BF), ((D, INNER), BF), ((D, INNER), BF), ((D, INNER), BF), ((INNER, 2 * D), BF),
         (full, BF), ((D, TOK), BF), ((TOK, INNER), F32), ((TOK, INNER), F32), ((HEADS, TOK, 128), BF), ((HEADS, TOK, 128), BF),
-        ((KEYS, 128), BF), (eight, BF), (eight, BF), ((TOKENS, 1), jnp.int32), (eight, BF), (eight, F32),
+        ((4, CLASS_ROWS, 128), BF), (eight, BF), (eight, BF), ((TOKENS, 1), jnp.int32), (eight, BF), ((CLASS, 1), F32),
         ((HEADS, TOK, 128), BF), ((TOK, INNER), BF), ((INNER, TOK), BF), ((TOK, 2 * D), BF), ((HEADS, TOK, 128), BF), (full, F32),
-        ((128, KEYS), F32), ((KEYS, 128), BF), (eight, BF), ((N_SEQ, TOK, 128), BF), ((HEADS, TOK, 128), BF),
+        ((128, CLASS_ROWS), F32), ((4, CLASS, 128), BF), (eight, BF), ((HEADS, TOK, 128), BF), ((HEADS, TOK, 128), BF),
         ((3, TOK, INNER), BF), (full, F32), (full, BF),
+        ((40, 128), jnp.int32), ((CLASS, 1), jnp.int32), ((4, 1, CLASS_ROWS), jnp.int32), (eight, F32), (eight, F32),
+        ((4, HEAD_DIM, 2 * TOK), BF), ((4, HEAD_DIM, 2 * TOK), BF), ((CLASS, 1), F32), (eight, BF), (eight, BF),
+        ((HALF, 128), BF), ((HALF, 128), BF),
     ]
     dma = pltpu.SemaphoreType.DMA
     return pl.pallas_call(
@@ -629,8 +683,9 @@
         scratch_shapes=[pltpu.VMEM(shape, dtype) for shape, dtype in scratch]
         + halving_scratch(OUT_ROWS)
         + halving_scratch(TERM_ROWS)
-        + [dma((6,)), dma((8,)), dma((8,)), dma((8,)), dma((8,)), dma((2, 8)), dma((2, 8)), dma((2, 8)), dma((2, 8))]
-        + [dma((8,)), dma((8,)), dma((8,)), dma((8,)), dma((8,)), dma((8,)), dma((N_SEQ,)), dma((N_SEQ,)), dma((4,)), dma((2,))],
+        + [dma((6,)), dma((8,)), dma((8,)), dma((8,)), dma((8,)), dma((2, 8)), dma((2, 8)), dma((8,)), dma((8,))]
+        + [dma((8,))] * 8
+        + [dma((4,)), dma((2,)), dma((4,)), dma((4,))],
         compiler_params=pltpu.CompilerParams(collective_id=1, has_side_effects=True, vmem_limit_bytes=BIG),
         name="layer",
     )(*operands)

time: 125 us -> 106 us (0.85)
  Pallas kernels: 125 us -> 105 us
    pallas_call x1, Pallas kernels: 122 us -> 103 us  [whole_layer(): pl.pallas_call(layer_body, out_shape=[jax.ShapeDtypeStruct((32, INNER), F...]
where the time goes in v4:
time: 106 us
  Pallas kernels  105 us (99%)
    pallas_call x1, Pallas kernels, whole_layer(): pl.pallas_call(layer_body, out_shape=[jax.ShapeDtypeStruct((32, INNER), F...  103 us
    pallas_call x1, Pallas kernels, hand_out(): pl.pallas_call(hand_out_body, out_shape=[jax.ShapeDtypeStruct((TOK, D), B...  2.16 us

profile of v4, /device:TPU:0, one launch (start us, length us, event | category | flops | bytes accessed | tf_op | source)
XLA Modules:
  0.0 105.8 jit_solution(7592121301642040716)
XLA Ops:
  0.6 103.0 %layer.1 = (f32[32,512]{1,0:T(8,128)}, f32[32,512]{1,0:T(8,128)}, f32[32,512]{1,0:T(8,128)}, f32[16,2048]{1,0:T(8,128)}, bf16[136,1024]{1,0:T(8,128)(2,1)}) custom-call(bf16[136,1024]{1,0:T(8,128)(2,1)} %bitcast.16, bf16[136,1024]{1,0:T(8,128)(2,1)} %bitcast.17, bf16[1024,512]{1,0:T(8,128)(2,1)} %bitcast.13, bf16[1024,512]{1,0:T(8,128)(2,1)} %bitcast.14, ...), custom_call_target="tpu_custom_call" | custom-call | tf_op jit(solution)/shard_map/layer/pallas_call | solution.py:677
  103.7 2.2 %hand_out.1 = (bf16[136,1024]{1,0:T(8,128)(2,1)}, f32[32,512]{1,0:T(8,128)}, f32[32,512]{1,0:T(8,128)}, f32[32,512]{1,0:T(8,128)}, f32[16,2048]{1,0:T(8,128)}) custom-call(f32[32,512]{1,0:T(8,128)} %get-tuple-element.15.sum_q, f32[32,512]{1,0:T(8,128)} %get-tuple-element.16.sum_k, f32[32,512]{1,0:T(8,128)} %get-tuple-element.17.sum_v, ...), custom_call_target="tpu_custom_call" | custom-call | tf_op jit(solution)/shard_map/hand_out/pallas_call | solution.py:708

commit v5 on v4

--- a/solution.py
+++ b/solution.py
@@ -15,7 +15,8 @@
 INNER = 512
 CLASS = 8 * TOK
 CLASS_ROWS = 1152
-HALF = CLASS // 2
+LOW = 512
+LONG = 80
 BF = jnp.bfloat16
 F32 = jnp.float32
 MESH = pl.DeviceIdType.MESH
@@ -44,6 +45,18 @@
     low = jnp.sum(jnp.where(left, slab, 0.0), axis=-1, keepdims=True)
     high = jnp.sum(jnp.where(left, 0.0, slab), axis=-1, keepdims=True)
     return jnp.where(left, low, high)
+
+
+def packed(near, far, left):
+    rest = jnp.concatenate([far[LONG:], jnp.zeros((2 * LONG - TOK, 128), F32)], axis=0)
+    return jnp.where(left[:LONG], near[:LONG], rest).astype(BF)
+
+
+def unpacked_pair(low, high, left):
+    low, high = low.astype(F32), high.astype(F32)
+    top = jnp.where(left[:LONG], low, swap(high))
+    rest = jnp.where(left[:LONG], swap(low), high)[: TOK - LONG]
+    return jnp.concatenate([top, rest], axis=0)
 
 
 def unit_scale(slab, left):
@@ -72,41 +85,54 @@
     )
 
 
-def spread_out(groups):
-    counts = [groups // 5 + (1 if stream < groups % 5 else 0) for stream in range(5)]
-    places = [(stream, 16 * row) for stream in range(5) for row in range(counts[stream])]
+ALL_LINKS = tuple(tuple((first + step) % 5 for step in range(5)) for first in range(5))
+FLAT_FIRST = ((0, 1, 2, 3, 4), (1, 2, 0, 4, 3), (2, 0, 1, 3, 4))
+
+
+def spread_out(groups, orders):
+    streams = len(orders)
+    counts = [groups // streams + (1 if stream < groups % streams else 0) for stream in range(streams)]
+    places = [(stream, 16 * row) for stream in range(streams) for row in range(counts[stream])]
     return [16 * count for count in counts], places
 
 
-TERM_ROWS, TERM_PLACES = spread_out(24)
-OUT_ROWS, OUT_PLACES = spread_out(16)
-
-
-def slot(stream, owner, bits):
+Q_ROWS, Q_PLACES = spread_out(8, ALL_LINKS)
+KV_ROWS, KV_PLACES = spread_out(16, ALL_LINKS)
+OUT_ROWS, OUT_PLACES = spread_out(16, FLAT_FIRST)
+
+
+def slot(order, owner, bits):
     y, x, z = owner // 16, owner // 4 % 4, owner % 4
     theirs = (y, (x + 1) // 2 % 2, x // 2, (z + 1) // 2 % 2, z // 2)
     at = 0
-    for step in range(5):
-        split = (stream + step) % 5
+    for step, split in enumerate(order):
         apart = 1 - bits[split] if theirs[split] else bits[split]
         at = at + apart * (16 >> step)
     return at
 
 
 class Halving:
-    def __init__(self, terms, acc, got, send, recv, near):
-        self.terms, self.acc, self.got, self.send, self.recv, self.near = terms, acc, got, send, recv, near
-
-    def hop(self, stream, step):
+    def __init__(self, refs, orders, near):
+        count = len(orders)
+        self.terms, self.acc, self.got = refs[:count], refs[count : 2 * count], refs[2 * count : 3 * count]
+        self.send, self.recv = refs[3 * count :]
+        self.orders, self.near, self.streams = orders, near, range(count)
+
+    def hop(self, stream, step, part):
         half = 16 >> step
+        first, size = (half // 2 * (1 - part), half // 2) if step < 4 else (0, 1)
         return pltpu.make_async_remote_copy(
-            src_ref=(self.acc if step else self.terms)[stream].at[pl.ds(half, half)],
-            dst_ref=self.got[stream].at[pl.ds(32 - (32 >> step), half)],
-            send_sem=self.send.at[stream, step],
-            recv_sem=self.recv.at[stream, step],
-            device_id={"seq": self.near[(stream + step) % 5]},
+            src_ref=(self.acc if step else self.terms)[stream].at[pl.ds(half + first, size)],
+            dst_ref=self.got[stream].at[pl.ds(32 - (32 >> step) + first, size)],
+            send_sem=self.send.at[stream, step, part],
+            recv_sem=self.recv.at[stream, step, part],
+            device_id={"seq": self.near[self.orders[stream][step]]},
             device_id_type=MESH,
         )
+
+    def start(self, stream, step):
+        for part in range(2 if step < 4 else 1):
+            self.hop(stream, step, part).start()
 
     def add(self, stream, step, first, count):
         mine = (self.acc if step else self.terms)[stream]
@@ -125,21 +151,25 @@
         else:
             lax.fori_loop(0, count // width, one, 0)
 
-    def advance(self, stream, step):
+    def advance(self, step):
         half = 8 >> step
-        self.hop(stream, step).wait_recv()
-        self.add(stream, step, half, half)
-        self.hop(stream, step + 1).start()
-        self.add(stream, step, 0, half)
+        for stream in self.streams:
+            self.hop(stream, step, 0).wait_recv()
+            self.add(stream, step, half, half)
+            self.start(stream, step + 1)
+        for stream in self.streams:
+            self.hop(stream, step, 1).wait_recv()
+            self.add(stream, step, 0, half)
 
     def result(self, stream):
-        self.hop(stream, 4).wait_recv()
+        self.hop(stream, 4, 0).wait_recv()
         return self.acc[stream][0].astype(F32) + self.got[stream][30].astype(F32)
 
     def drain(self):
         for step in range(5):
-            for stream in range(5):
-                self.hop(stream, step).wait_send()
+            for stream in self.streams:
+                for part in range(2 if step < 4 else 1):
+                    self.hop(stream, step, part).wait_send()
 
 
 def halving_scratch(rows):
@@ -147,7 +177,7 @@
         [pltpu.VMEM((N_SEQ, count, 128), BF) for count in rows]
         + [pltpu.VMEM((16, count, 128), BF) for count in rows]
         + [pltpu.VMEM((31, count, 128), BF) for count in rows]
-        + [pltpu.SemaphoreType.DMA((5, 5)), pltpu.SemaphoreType.DMA((5, 5))]
+        + [pltpu.SemaphoreType.DMA((len(rows), 5, 2)), pltpu.SemaphoreType.DMA((len(rows), 5, 2))]
     )
 
 
@@ -171,8 +201,8 @@
     total, dkv, dq, dkv_all, dq_all, grads, gn, grad_input = take(8)
     padded_ids, q_end, tokens, summed, mass, q_turned, g_turned, correction, from_back, from_next = take(10)
     far_half = take(2)
-    out_refs = take(17)
-    term_refs = take(17)
+    q_in, g_in, out_pack = take(3)
+    out_refs, q_refs, kv_refs = take(11), take(17), take(17)
     (load, kv_send, kv_recv, q_send, q_recv, z_send, z_recv, f_send, f_recv, att_send, att_recv,
      g_send, g_recv, dq_send, dq_recv, dkv_send, dkv_recv, local, carry_sem, back_send, back_recv) = refs
 
@@ -196,10 +226,13 @@
     barrier = pltpu.get_barrier_semaphore()
 
     def greet(k, _):
-        pl.semaphore_signal(barrier, inc=1, device_id={"seq": lax.rem(me + k, N_SEQ)}, device_id_type=MESH)
+        peer = 4 * lax.rem(mine + k, HEADS) + group
+        pl.semaphore_signal(barrier, inc=1, device_id={"seq": peer}, device_id_type=MESH)
         return 0
 
-    lax.fori_loop(1, N_SEQ, greet, 0)
+    lax.fori_loop(1, HEADS, greet, 0)
+    for peer in (z_next, z_back):
+        pl.semaphore_signal(barrier, inc=1, device_id={"seq": peer}, device_id_type=MESH)
     for other in (before, after):
         pl.semaphore_signal(barrier, inc=1, device_id={"section": other, "seq": across}, device_id_type=MESH)
 
@@ -217,8 +250,9 @@
         lax.fori_loop(first, end, one, 0)
 
     left = left_half((TOK, 128))
-    out_sum = Halving(out_refs[:5], out_refs[5:10], out_refs[10:15], out_refs[15], out_refs[16], near)
-    term_sum = Halving(term_refs[:5], term_refs[5:10], term_refs[10:15], term_refs[15], term_refs[16], near)
+    out_sum = Halving(out_refs, FLAT_FIRST, near)
+    q_sum = Halving(q_refs, ALL_LINKS, near)
+    kv_sum = Halving(kv_refs, ALL_LINKS, near)
 
     loads[0].wait()
     field = act[...].astype(F32)
@@ -240,11 +274,12 @@
             v_slab = v[:, 128 * half : 128 * half + 128]
             q_slab = (q_slab * unit_scale(q_slab, left)).astype(BF).astype(F32) * 0.125
             k_slab = k_slab * unit_scale(k_slab, left)
-            q_pack[head] = jnp.where(left, q_slab, 0.0).astype(BF)
-            q_pack[head + 1] = jnp.where(left, swap(q_slab), 0.0).astype(BF)
+            q_swap = swap(q_slab)
+            q_pack[head] = packed(q_slab, q_swap, left)
+            q_pack[head + 1] = packed(q_swap, q_slab, left)
             kv_pack[head] = jnp.where(left, k_slab, swap(v_slab)).astype(BF)
             kv_pack[head + 1] = jnp.where(left, swap(k_slab), v_slab).astype(BF)
-    pl.semaphore_wait(barrier, N_SEQ + 1)
+    pl.semaphore_wait(barrier, HEADS + 3)
 
     def kv_copy(k):
         peer = lax.rem(mine + k, HEADS)
@@ -252,12 +287,12 @@
 
     def q_copy(k):
         peer = lax.rem(mine + k, HEADS)
-        return remote(q_pack.at[peer], q_all.at[chunk_rows(mine)], q_send.at[k], q_recv.at[k], 4 * peer + group)
+        return remote(q_pack.at[peer], q_in.at[mine], q_send.at[k], q_recv.at[k], 4 * peer + group)
 
     loop(1, HEADS, lambda k: kv_copy(k).start())
     own = [
         pltpu.make_async_copy(kv_pack.at[mine], kv.at[0, chunk_rows(mine)], local.at[0]),
-        pltpu.make_async_copy(q_pack.at[mine], q_all.at[chunk_rows(mine)], local.at[1]),
+        pltpu.make_async_copy(q_pack.at[mine], q_in.at[mine], local.at[1]),
     ]
     for copy in own:
         copy.start()
@@ -315,6 +350,13 @@
         normed_turned[at, :] = jnp.transpose(normed[:, at].astype(F32)).astype(BF)
     own[1].wait()
     loop(1, HEADS, lambda k: q_copy(k).wait_recv())
+    short = left[:LONG]
+    for a in range(4):
+        parts = []
+        for chunk in (2 * a, 2 * a + 1):
+            q = q_in[chunk].astype(F32)
+            parts += [jnp.where(short, q, 0.0), jnp.where(short, swap(q), 0.0)[: TOK - LONG]]
+        q_all[2 * TOK * a : 2 * TOK * (a + 1), :] = jnp.concatenate(parts, axis=0).astype(BF)
 
     def tiles(a):
         whole = [(512 * part, min(512, 256 * a - 512 * part), False) for part in range(-(-a // 2))]
@@ -328,7 +370,7 @@
 
     def att_copy(chunk):
         k = lax.rem(chunk - mine + HEADS, HEADS)
-        return remote(out.at[chunk_rows(chunk)], att_all.at[mine], att_send.at[k], att_recv.at[k], 4 * chunk + group)
+        return remote(out_pack.at[chunk], att_all.at[mine], att_send.at[k], att_recv.at[k], 4 * chunk + group)
 
     summed[...] = jnp.zeros_like(summed)
     mass[...] = jnp.zeros_like(mass)
@@ -349,10 +391,9 @@
         def _():
             loop(0, 4, lambda chunk: z_copy(chunk, 1).wait_recv())
 
-        @pl.when(place_of == 3)
-        def _():
-            loop(0, 4, lambda chunk: (f_copy(chunk, 0).wait_recv(), f_copy(chunk + 4, 1).wait_recv()))
-
+        add_class(place_of, None)
+
+    def add_class(place_of, then):
         for a in range(4):
             rows = pair_rows(a)
             q = q_all[rows, :]
@@ -366,27 +407,35 @@
                     part_mass = part_mass + p[:, 128 * part : 128 * part + 128]
                 mass[rows, :] += part_mass
                 summed[rows, :] += dot(p.astype(BF), block)
-
-            @pl.when(place_of == 3)
+            if then is not None:
+                then(a)
+
+    def hand_over(a):
+        rows = pair_rows(a)
+        one_over = 1.0 / jnp.sum(mass[rows, :], axis=-1, keepdims=True)
+        result = summed[rows, :] * one_over
+        out[rows, :] = result.astype(BF)
+        inverse[rows, :] = one_over
+        for half in range(2):
+            chunk = 2 * a + half
+            value = result[TOK * half : TOK * half + TOK]
+            out_pack[chunk] = packed(swap(value), value, left)
+
+            @pl.when(mine != chunk)
             def _():
-                one_over = 1.0 / jnp.sum(mass[rows, :], axis=-1, keepdims=True)
-                out[rows, :] = (summed[rows, :] * one_over).astype(BF)
-                inverse[rows, :] = one_over
-                for chunk in (2 * a, 2 * a + 1):
-
-                    @pl.when(mine != chunk)
-                    def _():
-                        att_copy(chunk).start()
-
-                    @pl.when(mine == chunk)
-                    def _():
-                        pltpu.make_async_copy(out.at[chunk_rows(chunk)], att_all.at[mine], local.at[0]).start()
-
-    loop(0, 4, attend)
+                att_copy(chunk).start()
+
+            @pl.when(mine == chunk)
+            def _():
+                pltpu.make_async_copy(out_pack.at[chunk], att_all.at[mine], local.at[0]).start()
+
+    loop(0, 3, attend)
+    loop(0, 4, lambda chunk: (f_copy(chunk, 0).wait_recv(), f_copy(chunk + 4, 1).wait_recv()))
+    add_class(3, hand_over)
 
     loads[4].wait()
     loads[5].wait()
-    pltpu.make_async_copy(out.at[chunk_rows(mine)], att_all.at[mine], local.at[0]).wait()
+    pltpu.make_async_copy(out_pack.at[mine], att_all.at[mine], local.at[0]).wait()
 
     def att_arrived(k):
         peer = lax.rem(mine + k, HEADS)
@@ -394,9 +443,7 @@
 
     loop(1, HEADS, att_arrived)
     for pair in range(HEADS // 2):
-        low = att_all[2 * pair].astype(F32)
-        high = att_all[2 * pair + 1].astype(F32)
-        slab = jnp.where(left, swap(low), high)
+        slab = unpacked_pair(att_all[2 * pair], att_all[2 * pair + 1], left)
         att[:, 128 * pair : 128 * pair + 128] = slab.astype(BF)
         att_turned[128 * pair : 128 * pair + 128, :] = jnp.transpose(slab).astype(BF)
     for block in range(4):
@@ -413,18 +460,19 @@
 
     def g_copy(head):
         k = lax.rem(head - mine + HEADS, HEADS)
-        return remote(g_pack.at[head], g_all.at[chunk_rows(mine)], g_send.at[k], g_recv.at[k], 4 * head + group)
+        return remote(g_pack.at[head], g_in.at[mine], g_send.at[k], g_recv.at[k], 4 * head + group)
 
     def g_own():
-        return pltpu.make_async_copy(g_pack.at[mine], g_all.at[chunk_rows(mine)], local.at[1])
+        return pltpu.make_async_copy(g_pack.at[mine], g_in.at[mine], local.at[1])
 
     for block in range(2):
         g = dot_t(affine_grad[...], wo[pl.ds(256 * block, 256), :])
         for half in range(2):
             head = 4 * block + 2 * half
             slab = g[:, 128 * half : 128 * half + 128]
-            g_pack[head] = jnp.where(left, 0.0, swap(slab)).astype(BF)
-            g_pack[head + 1] = jnp.where(left, 0.0, slab).astype(BF)
+            turned_slab = swap(slab)
+            g_pack[head] = packed(slab, turned_slab, left)
+            g_pack[head + 1] = packed(turned_slab, slab, left)
         for head in range(4 * block, 4 * block + 4):
 
             @pl.when(mine != head)
@@ -438,18 +486,23 @@
         for owner in range(N_SEQ):
             for half in range(2):
                 stream, row = OUT_PLACES[2 * block + half]
-                out_sum.terms[stream][slot(stream, owner, bits), row : row + 16, :] = term[
+                out_sum.terms[stream][slot(FLAT_FIRST[stream], owner, bits), row : row + 16, :] = term[
                     16 * owner : 16 * owner + 16, 128 * half : 128 * half + 128
                 ]
-    for stream in range(5):
-        out_sum.hop(stream, 0).start()
+    for stream in out_sum.streams:
+        out_sum.start(stream, 0)
 
     g_own().wait()
     loop(1, HEADS, lambda k: g_copy(lax.rem(mine + k, HEADS)).wait_recv())
 
     for a in range(4):
         rows = pair_rows(a)
-        g = g_all[rows, :].astype(F32)
+        parts = []
+        for chunk in (2 * a, 2 * a + 1):
+            g = g_in[chunk].astype(F32)
+            parts += [jnp.where(short, 0.0, swap(g)), jnp.where(short, 0.0, g)[: TOK - LONG]]
+        g = jnp.concatenate(parts, axis=0)
+        g_all[rows, :] = g.astype(BF)
         correction[rows, :] = jnp.sum(g * out[rows, :].astype(F32), axis=-1, keepdims=True)
         q_turned[a] = jnp.transpose(q_all[rows, :].astype(F32))[:HEAD_DIM].astype(BF)
         g_turned[a] = jnp.transpose(g)[HEAD_DIM:].astype(BF)
@@ -457,19 +510,22 @@
 
     def dq_copy(chunk):
         k = lax.rem(chunk - mine + HEADS, HEADS)
-        return remote(dq.at[chunk_rows(chunk)], dq_all.at[mine], dq_send.at[k], dq_recv.at[k], 4 * chunk + group)
+        return remote(dq.at[chunk], dq_all.at[mine], dq_send.at[k], dq_recv.at[k], 4 * chunk + group)
 
     def dq_own():
-        return pltpu.make_async_copy(dq.at[chunk_rows(mine)], dq_all.at[mine], local.at[2])
+        return pltpu.make_async_copy(dq.at[mine], dq_all.at[mine], local.at[2])
+
+    halves = (pl.ds(0, LOW), pl.ds(LOW, CLASS - LOW))
 
     def far_copy(way):
-        rows = pl.ds(HALF * way, HALF)
-        return remote(dkv.at[3, rows], far_half[way], back_send.at[way], back_recv.at[way], z_back if way else z_next)
-
-    def class_copy(way):
-        if way:
-            return remote(dkv.at[1], from_next, back_send.at[2], back_recv.at[2], z_back)
-        return remote(dkv.at[2], from_back, back_send.at[3], back_recv.at[3], z_next)
+        return remote(
+            dkv.at[3, halves[way]], far_half[way], back_send.at[way], back_recv.at[way], z_back if way else z_next
+        )
+
+    def class_copy(place_of, half):
+        at = 2 * place_of + half
+        target, peer = (from_next, z_back) if place_of == 1 else (from_back, z_next)
+        return remote(dkv.at[place_of, halves[half]], target.at[halves[half]], back_send.at[at], back_recv.at[at], peer)
 
     def dkv_copy(k):
         peer = lax.rem(mine + k, HEADS)
@@ -478,31 +534,40 @@
     def dkv_own():
         return pltpu.make_async_copy(dkv.at[0, chunk_rows(mine)], dkv_all.at[mine], local.at[3])
 
+    def send_keys(chunk):
+        @pl.when(mine != chunk)
+        def _():
+            dkv_copy(lax.rem(chunk - mine + HEADS, HEADS)).start()
+
+        @pl.when(mine == chunk)
+        def _():
+            dkv_own().start()
+
     blocks = [(128 * part, 128) for part in range(8)] + [(1024, CLASS - 1024)]
 
-    def settle(place_of, extra):
-        for first, width in blocks:
+    def settle(place_of, parts, extra):
+        for first, width in parts:
             value = jnp.transpose(total[:, first : first + 128])[:width]
-            for source, low, high in extra:
-                begin, end = max(first, low), min(first + width, high)
-                if begin == first and end == first + width:
-                    value = value + source[first - low : first - low + width, :].astype(F32)
-                elif begin < end:
-                    inside = source[begin - low : end - low, :].astype(F32)
-                    zeros = [jnp.zeros((begin - first, 128), F32), inside, jnp.zeros((first + width - end, 128), F32)]
-                    value = value + jnp.concatenate([z for z in zeros if z.shape[0]], axis=0)
+            for source, begin in extra:
+                value = value + source[first - begin : first - begin + width, :].astype(F32)
             dkv[place_of, first : first + width, :] = value.astype(BF)
 
-    def attend_back(n):
-        place_of = 3 - n
-        total[...] = jnp.zeros_like(total)
+    def spans(a, half):
+        low, high = ((0, LOW), (LOW, CLASS_ROWS))[half]
+        cut = min(max(256 * a, low), high)
+        end = min(256 * a + (384 if a == 3 else 512), high)
+        return [(low, cut - low, False)] * (cut > low) + [(cut, end - cut, True)] * (end > cut)
+
+    def back_class(place_of, half, then):
+        spread = {0: (0, LOW), 1: (LOW, CLASS_ROWS), None: (0, CLASS_ROWS)}[half]
+        total[:, spread[0] : spread[1]] = jnp.zeros((128, spread[1] - spread[0]), F32)
         for a in (3, 2, 1, 0):
             rows = pair_rows(a)
             q = q_all[rows, :]
             g = g_all[rows, :]
             one_over = inverse[rows, :]
             corr = correction[rows, :]
-            for first, width, masked in tiles(a):
+            for first, width, masked in tiles(a) if half is None else spans(a, half):
                 block = kv[place_of, first : first + width, :]
                 p = jnp.exp(dot_t(q, block)) * one_over
                 if masked:
@@ -511,54 +576,54 @@
                 total[:HEAD_DIM, first : first + width] += dot(q_turned[a], ds)
                 total[HEAD_DIM:, first : first + width] += dot(g_turned[a], p.astype(BF))
                 summed[rows, :] += dot(ds, block)
-
-            @pl.when(n == 3)
+            if then is not None:
+                then(a)
+
+    def send_dq(a):
+        result = summed[pair_rows(a), :] * 0.125
+        for half in range(2):
+            chunk = 2 * a + half
+            value = result[TOK * half : TOK * half + TOK]
+            dq[chunk] = packed(value, swap(value), left)
+
+            @pl.when(mine != chunk)
             def _():
-                dq[rows, :] = (summed[rows, :] * 0.125).astype(BF)
-                for chunk in (2 * a, 2 * a + 1):
-
-                    @pl.when(mine != chunk)
-                    def _():
-                        dq_copy(chunk).start()
-
-                    @pl.when(mine == chunk)
-                    def _():
-                        dq_own().start()
-
-        @pl.when(n == 0)
-        def _():
-            settle(3, [])
-            for way in range(2):
-                far_copy(way).start()
-
-        @pl.when(n == 1)
-        def _():
-            far_copy(0).wait_recv()
-            settle(2, [(far_half[0], 0, HALF)])
-            class_copy(0).start()
-
-        @pl.when(n == 2)
-        def _():
-            far_copy(1).wait_recv()
-            settle(1, [(far_half[1], HALF, CLASS)])
-            class_copy(1).start()
-
-        @pl.when(n == 3)
-        def _():
-            for way in range(2):
-                class_copy(way).wait_recv()
-            settle(0, [(from_back, 0, CLASS), (from_next, 0, CLASS)])
-            loop(1, HEADS, lambda k: dkv_copy(k).start())
-            dkv_own().start()
-
-        for step in range(4):
-
-            @pl.when(n == step)
+                dq_copy(chunk).start()
+
+            @pl.when(mine == chunk)
             def _():
-                for stream in range(5):
-                    out_sum.advance(stream, step)
-
-    loop(0, 4, attend_back)
+                dq_own().start()
+
+    lower, upper = blocks[:4], blocks[4:]
+    back_class(3, 0, None)
+    settle(3, lower, [])
+    far_copy(0).start()
+    back_class(3, 1, None)
+    settle(3, upper, [])
+    far_copy(1).start()
+    back_class(1, 0, None)
+    settle(1, lower, [])
+    class_copy(1, 0).start()
+    back_class(2, 1, None)
+    settle(2, upper, [])
+    class_copy(2, 1).start()
+    back_class(2, 0, None)
+    far_copy(0).wait_recv()
+    settle(2, lower, [(far_half[0], 0)])
+    class_copy(2, 0).start()
+    out_sum.advance(0)
+    back_class(1, 1, None)
+    far_copy(1).wait_recv()
+    settle(1, upper, [(far_half[1], LOW)])
+    class_copy(1, 1).start()
+    back_class(0, None, send_dq)
+    for half in (1, 0):
+        for place_of in (2, 1):
+            class_copy(place_of, half).wait_recv()
+        settle(0, upper if half else lower, [(from_back, 0), (from_next, 0)])
+        for chunk in range(4, 8) if half else range(4):
+            send_keys(chunk)
+    out_sum.advance(1)
 
     def unit_back(grad, raw):
         scale = unit_scale(raw, left)
@@ -569,14 +634,15 @@
         return dkv_all[head].astype(F32)
 
     def term_of(which):
+        places, into, first = (Q_PLACES, q_sum, 0) if which == 0 else (KV_PLACES, kv_sum, 8 * (which - 1))
         for block in range(2):
             term = dot(normed_turned[...], grads[which, :, 256 * block : 256 * block + 256]).astype(BF)
             for owner in range(N_SEQ):
                 for part in range(4):
                     slab, half = part // 2, part % 2
-                    stream, row = TERM_PLACES[8 * which + 4 * block + 2 * slab + half]
+                    stream, row = places[first + 4 * block + 2 * slab + half]
                     top = 32 * owner + 16 * half
-                    term_sum.terms[stream][slot(stream, owner, bits), row : row + 16, :] = term[
+                    into.terms[stream][slot(ALL_LINKS[stream], owner, bits), row : row + 16, :] = term[
                         top : top + 16, 128 * slab : 128 * slab + 128
                     ]
 
@@ -584,10 +650,12 @@
     loop(1, HEADS, lambda k: dq_copy(lax.rem(mine + k, HEADS)).wait_recv())
     for pair in range(HEADS // 2):
         at = pl.ds(128 * pair, 128)
-        low, high = dq_all[2 * pair].astype(F32), dq_all[2 * pair + 1].astype(F32)
-        grads[0, :, at] = unit_back(jnp.where(left, low, swap(high)), q_raw[:, at]).astype(BF)
+        q_grad = unpacked_pair(dq_all[2 * pair], dq_all[2 * pair + 1], left)
+        grads[0, :, at] = unit_back(q_grad, q_raw[:, at]).astype(BF)
     term_of(0)
-    term_sum.hop(0, 0).start()
+    for stream in range(5):
+        q_sum.start(stream, 0)
+    out_sum.advance(2)
     for block in range(4):
         at = pl.ds(256 * block, 256)
         gn[:, at] = dot_t(grads[0], wq[at, :])
@@ -599,11 +667,13 @@
         grads[1, :, at] = unit_back(jnp.where(left, low, swap(high)), k_raw[:, at]).astype(BF)
         grads[2, :, at] = jnp.where(left, swap(low), high).astype(BF)
     term_of(1)
-    term_sum.hop(1, 0).start()
-    term_sum.hop(2, 0).start()
+    for stream in range(2):
+        kv_sum.start(stream, 0)
     term_of(2)
-    term_sum.hop(3, 0).start()
-    term_sum.hop(4, 0).start()
+    for stream in range(2, 5):
+        kv_sum.start(stream, 0)
+    q_sum.advance(0)
+    out_sum.advance(3)
     for block in range(4):
         at = pl.ds(256 * block, 256)
         gn[:, at] += dot_t(grads[1], wk[at, :]) + dot_t(grads[2], wv[at, :])
@@ -618,23 +688,31 @@
         device_id={"section": before, "seq": across}, device_id_type=MESH,
     )
     carry.start()
-    for stream in range(5):
+    q_sum.advance(1)
+    kv_sum.advance(0)
+    q_sum.advance(2)
+    for stream in out_sum.streams:
         result = out_sum.result(stream)
         for part in range(16):
             if OUT_PLACES[part][0] == stream:
                 row = OUT_PLACES[part][1]
                 sum_out[:, 128 * part : 128 * part + 128] = result[row : row + 16]
-    for step in range(4):
+    kv_sum.advance(1)
+    q_sum.advance(3)
+
+    def deliver(halving, places, targets):
         for stream in range(5):
-            term_sum.advance(stream, step)
-    for stream in range(5):
-        result = term_sum.result(stream)
-        for part in range(24):
-            if TERM_PLACES[part][0] == stream:
-                row = TERM_PLACES[part][1]
-                target = (sum_q, sum_k, sum_v)[part // 8]
-                column, top = 128 * (part % 8 // 2), 16 * (part % 2)
-                target[top : top + 16, column : column + 128] = result[row : row + 16]
+            result = halving.result(stream)
+            for part in range(8 * len(targets)):
+                if places[part][0] == stream:
+                    row = places[part][1]
+                    column, top = 128 * (part % 8 // 2), 16 * (part % 2)
+                    targets[part // 8][top : top + 16, column : column + 128] = result[row : row + 16]
+
+    kv_sum.advance(2)
+    deliver(q_sum, Q_PLACES, (sum_q,))
+    kv_sum.advance(3)
+    deliver(kv_sum, KV_PLACES, (sum_k, sum_v))
     carry.wait()
 
     def left_all(k):
@@ -655,23 +733,25 @@
     loop(0, 4, lambda chunk: (f_copy(chunk, 0).wait_send(), f_copy(chunk + 4, 1).wait_send()))
     for way in range(2):
         far_copy(way).wait_send()
-        class_copy(way).wait_send()
+        for place_of in (1, 2):
+            class_copy(place_of, way).wait_send()
     out_sum.drain()
-    term_sum.drain()
+    q_sum.drain()
+    kv_sum.drain()
 
 
 def whole_layer(*operands):
-    eight, full = (HEADS * TOK, 128), (TOK, D)
+    eight, full, short = (HEADS * TOK, 128), (TOK, D), (HEADS, LONG, 128)
     scratch = [
         (full, BF), (full, BF), ((D, INNER), BF), ((D, INNER), BF), ((D, INNER), BF), ((INNER, 2 * D), BF),
-        (full, BF), ((D, TOK), BF), ((TOK, INNER), F32), ((TOK, INNER), F32), ((HEADS, TOK, 128), BF), ((HEADS, TOK, 128), BF),
+        (full, BF), ((D, TOK), BF), ((TOK, INNER), F32), ((TOK, INNER), F32), (short, BF), ((HEADS, TOK, 128), BF),
         ((4, CLASS_ROWS, 128), BF), (eight, BF), (eight, BF), ((TOKENS, 1), jnp.int32), (eight, BF), ((CLASS, 1), F32),
-        ((HEADS, TOK, 128), BF), ((TOK, INNER), BF), ((INNER, TOK), BF), ((TOK, 2 * D), BF), ((HEADS, TOK, 128), BF), (full, F32),
-        ((128, CLASS_ROWS), F32), ((4, CLASS, 128), BF), (eight, BF), ((HEADS, TOK, 128), BF), ((HEADS, TOK, 128), BF),
+        (short, BF), ((TOK, INNER), BF), ((INNER, TOK), BF), ((TOK, 2 * D), BF), (short, BF), (full, F32),
+        ((128, CLASS_ROWS), F32), ((4, CLASS, 128), BF), (short, BF), ((HEADS, TOK, 128), BF), (short, BF),
         ((3, TOK, INNER), BF), (full, F32), (full, BF),
         ((40, 128), jnp.int32), ((CLASS, 1), jnp.int32), ((4, 1, CLASS_ROWS), jnp.int32), (eight, F32), (eight, F32),
         ((4, HEAD_DIM, 2 * TOK), BF), ((4, HEAD_DIM, 2 * TOK), BF), ((CLASS, 1), F32), (eight, BF), (eight, BF),
-        ((HALF, 128), BF), ((HALF, 128), BF),
+        ((LOW, 128), BF), ((CLASS - LOW, 128), BF), (short, BF), (short, BF), (short, BF),
     ]
     dma = pltpu.SemaphoreType.DMA
     return pl.pallas_call(
@@ -682,10 +762,11 @@
         out_specs=[VMEM] * 5,
         scratch_shapes=[pltpu.VMEM(shape, dtype) for shape, dtype in scratch]
         + halving_scratch(OUT_ROWS)
-        + halving_scratch(TERM_ROWS)
+        + halving_scratch(Q_ROWS)
+        + halving_scratch(KV_ROWS)
         + [dma((6,)), dma((8,)), dma((8,)), dma((8,)), dma((8,)), dma((2, 8)), dma((2, 8)), dma((8,)), dma((8,))]
         + [dma((8,))] * 8
-        + [dma((4,)), dma((2,)), dma((4,)), dma((4,))],
+        + [dma((4,)), dma((2,)), dma((6,)), dma((6,))],
         compiler_params=pltpu.CompilerParams(collective_id=1, has_side_effects=True, vmem_limit_bytes=BIG),
         name="layer",
     )(*operands)

time: 106 us -> 96.3 us (0.908)
  Pallas kernels: 105 us -> 95.5 us
    pallas_call x1, Pallas kernels: 103 us -> 93.4 us  [whole_layer(): pl.pallas_call(layer_body, out_shape=[jax.ShapeDtypeStruct((32, INNER), F...]
where the time goes in v5:
time: 96.3 us; the launch traced here: 96.1 us
  Pallas kernels  95.5 us (99%)
    pallas_call x1, Pallas kernels, whole_layer(): pl.pallas_call(layer_body, out_shape=[jax.ShapeDtypeStruct((32, INNER), F...  93.4 us
    pallas_call x1, Pallas kernels, hand_out(): pl.pallas_call(hand_out_body, out_shape=[jax.ShapeDtypeStruct((TOK, D), B...  2.16 us

profile of v5, /device:TPU:0, one launch (start us, length us, event | category | flops | bytes accessed | tf_op | source)
XLA Modules:
  0.0 96.1 jit_solution(14764761249211177818)
XLA Ops:
  0.6 93.4 %layer.1 = (f32[32,512]{1,0:T(8,128)}, f32[32,512]{1,0:T(8,128)}, f32[32,512]{1,0:T(8,128)}, f32[16,2048]{1,0:T(8,128)}, bf16[136,1024]{1,0:T(8,128)(2,1)}) custom-call(bf16[136,1024]{1,0:T(8,128)(2,1)} %bitcast.16, bf16[136,1024]{1,0:T(8,128)(2,1)} %bitcast.17, bf16[1024,512]{1,0:T(8,128)(2,1)} %bitcast.13, bf16[1024,512]{1,0:T(8,128)(2,1)} %bitcast.14, ...), custom_call_target="tpu_custom_call" | custom-call | tf_op jit(solution)/shard_map/layer/pallas_call | solution.py:757
  94.0 2.2 %hand_out.1 = (bf16[136,1024]{1,0:T(8,128)(2,1)}, f32[32,512]{1,0:T(8,128)}, f32[32,512]{1,0:T(8,128)}, f32[32,512]{1,0:T(8,128)}, f32[16,2048]{1,0:T(8,128)}) custom-call(f32[32,512]{1,0:T(8,128)} %get-tuple-element.15.sum_q, f32[32,512]{1,0:T(8,128)} %get-tuple-element.16.sum_k, f32[32,512]{1,0:T(8,128)} %get-tuple-element.17.sum_v, ...), custom_call_target="tpu_custom_call" | custom-call | tf_op jit(solution)/shard_map/hand_out/pallas_call | solution.py:789

commit v6 on v5

--- a/solution.py
+++ b/solution.py
@@ -199,7 +199,8 @@
     normed, normed_turned, q_raw, k_raw, q_pack, kv_pack = take(6)
     kv, q_all, g_all, q_ids, out, inverse, att_all, att, att_turned, affine_grad, g_pack, carry_part = take(12)
     total, dkv, dq, dkv_all, dq_all, grads, gn, grad_input = take(8)
-    padded_ids, q_end, tokens, summed, mass, q_turned, g_turned, correction, from_back, from_next = take(10)
+    padded_ids, q_end, tokens, summed, mass, q_turned, g_turned, correction = take(8)
+    from_back, from_next, class_sum = take(2), take(2), take(2)
     far_half = take(2)
     q_in, g_in, out_pack = take(3)
     out_refs, q_refs, kv_refs = take(11), take(17), take(17)
@@ -492,6 +493,8 @@
     for stream in out_sum.streams:
         out_sum.start(stream, 0)
 
+    for a in range(4):
+        q_turned[a] = jnp.transpose(q_all[pair_rows(a), :].astype(F32))[:HEAD_DIM].astype(BF)
     g_own().wait()
     loop(1, HEADS, lambda k: g_copy(lax.rem(mine + k, HEADS)).wait_recv())
 
@@ -504,7 +507,6 @@
         g = jnp.concatenate(parts, axis=0)
         g_all[rows, :] = g.astype(BF)
         correction[rows, :] = jnp.sum(g * out[rows, :].astype(F32), axis=-1, keepdims=True)
-        q_turned[a] = jnp.transpose(q_all[rows, :].astype(F32))[:HEAD_DIM].astype(BF)
         g_turned[a] = jnp.transpose(g)[HEAD_DIM:].astype(BF)
     summed[...] = jnp.zeros_like(summed)
 
@@ -515,24 +517,22 @@
     def dq_own():
         return pltpu.make_async_copy(dq.at[mine], dq_all.at[mine], local.at[2])
 
-    halves = (pl.ds(0, LOW), pl.ds(LOW, CLASS - LOW))
-
     def far_copy(way):
         return remote(
-            dkv.at[3, halves[way]], far_half[way], back_send.at[way], back_recv.at[way], z_back if way else z_next
+            class_sum[way].at[2], far_half[way], back_send.at[way], back_recv.at[way], z_back if way else z_next
         )
 
     def class_copy(place_of, half):
         at = 2 * place_of + half
         target, peer = (from_next, z_back) if place_of == 1 else (from_back, z_next)
-        return remote(dkv.at[place_of, halves[half]], target.at[halves[half]], back_send.at[at], back_recv.at[at], peer)
+        return remote(class_sum[half].at[place_of - 1], target[half], back_send.at[at], back_recv.at[at], peer)
 
     def dkv_copy(k):
         peer = lax.rem(mine + k, HEADS)
-        return remote(dkv.at[0, chunk_rows(peer)], dkv_all.at[mine], dkv_send.at[k], dkv_recv.at[k], 4 * peer + group)
+        return remote(dkv.at[chunk_rows(peer)], dkv_all.at[mine], dkv_send.at[k], dkv_recv.at[k], 4 * peer + group)
 
     def dkv_own():
-        return pltpu.make_async_copy(dkv.at[0, chunk_rows(mine)], dkv_all.at[mine], local.at[3])
+        return pltpu.make_async_copy(dkv.at[chunk_rows(mine)], dkv_all.at[mine], local.at[3])
 
     def send_keys(chunk):
         @pl.when(mine != chunk)
@@ -543,14 +543,22 @@
         def _():
             dkv_own().start()
 
-    blocks = [(128 * part, 128) for part in range(8)] + [(1024, CLASS - 1024)]
-
-    def settle(place_of, parts, extra):
-        for first, width in parts:
-            value = jnp.transpose(total[:, first : first + 128])[:width]
-            for source, begin in extra:
-                value = value + source[first - begin : first - begin + width, :].astype(F32)
-            dkv[place_of, first : first + width, :] = value.astype(BF)
+    columns_of = (slice(0, LOW), slice(LOW, CLASS_ROWS))
+
+    def settle(place_of, half, extra):
+        value = total[:, columns_of[half]]
+        if extra is not None:
+            value = value + extra[...].astype(F32)
+        class_sum[half][place_of - 1] = value.astype(BF)
+
+    def settle_own(half):
+        for first in range(0, LOW, 128) if half == 0 else range(LOW, CLASS, 128):
+            begin = first - LOW * half
+            at = slice(begin, begin + 128)
+            value = total[:, first : first + 128]
+            value = value + from_back[half][:, at].astype(F32) + from_next[half][:, at].astype(F32)
+            width = min(128, CLASS - first)
+            dkv[first : first + width, :] = jnp.transpose(value)[:width].astype(BF)
 
     def spans(a, half):
         low, high = ((0, LOW), (LOW, CLASS_ROWS))[half]
@@ -567,11 +575,17 @@
             g = g_all[rows, :]
             one_over = inverse[rows, :]
             corr = correction[rows, :]
-            for first, width, masked in tiles(a) if half is None else spans(a, half):
+            pieces = tiles(a) if half is None else spans(a, half)
+            if pieces:
+                first = pieces[0][0]
+                width = sum(piece[1] for piece in pieces)
                 block = kv[place_of, first : first + width, :]
                 p = jnp.exp(dot_t(q, block)) * one_over
-                if masked:
-                    p = jnp.where(shown(a, place_of, first, width), p, 0.0)
+                parts = []
+                for begin, size, masked in pieces:
+                    part = p[:, begin - first : begin - first + size]
+                    parts.append(jnp.where(shown(a, place_of, begin, size), part, 0.0) if masked else part)
+                p = jnp.concatenate(parts, axis=1) if len(parts) > 1 else parts[0]
                 ds = (p * (dot_t(g, block) - corr)).astype(BF)
                 total[:HEAD_DIM, first : first + width] += dot(q_turned[a], ds)
                 total[HEAD_DIM:, first : first + width] += dot(g_turned[a], p.astype(BF))
@@ -594,33 +608,31 @@
             def _():
                 dq_own().start()
 
-    lower, upper = blocks[:4], blocks[4:]
-    back_class(3, 0, None)
-    settle(3, lower, [])
+    back_class(3, None, None)
+    settle(3, 0, None)
     far_copy(0).start()
-    back_class(3, 1, None)
-    settle(3, upper, [])
+    settle(3, 1, None)
     far_copy(1).start()
     back_class(1, 0, None)
-    settle(1, lower, [])
+    settle(1, 0, None)
     class_copy(1, 0).start()
     back_class(2, 1, None)
-    settle(2, upper, [])
+    settle(2, 1, None)
     class_copy(2, 1).start()
     back_class(2, 0, None)
     far_copy(0).wait_recv()
-    settle(2, lower, [(far_half[0], 0)])
+    settle(2, 0, far_half[0])
     class_copy(2, 0).start()
     out_sum.advance(0)
     back_class(1, 1, None)
     far_copy(1).wait_recv()
-    settle(1, upper, [(far_half[1], LOW)])
+    settle(1, 1, far_half[1])
     class_copy(1, 1).start()
     back_class(0, None, send_dq)
     for half in (1, 0):
         for place_of in (2, 1):
             class_copy(place_of, half).wait_recv()
-        settle(0, upper if half else lower, [(from_back, 0), (from_next, 0)])
+        settle_own(half)
         for chunk in range(4, 8) if half else range(4):
             send_keys(chunk)
     out_sum.advance(1)
@@ -634,7 +646,7 @@
         return dkv_all[head].astype(F32)
 
     def term_of(which):
-        places, into, first = (Q_PLACES, q_sum, 0) if which == 0 else (KV_PLACES, kv_sum, 8 * (which - 1))
+        places, into, first = (Q_PLACES, q_sum, 0) if which == 0 else (KV_PLACES, kv_sum, 8 * (2 - which))
         for block in range(2):
             term = dot(normed_turned[...], grads[which, :, 256 * block : 256 * block + 256]).astype(BF)
             for owner in range(N_SEQ):
@@ -662,14 +674,16 @@
     dkv_own().wait()
     loop(1, HEADS, lambda k: dkv_copy(k).wait_recv())
     for pair in range(HEADS // 2):
+        low, high = keys_of(2 * pair), keys_of(2 * pair + 1)
+        grads[2, :, 128 * pair : 128 * pair + 128] = jnp.where(left, swap(low), high).astype(BF)
+    term_of(2)
+    for stream in range(2):
+        kv_sum.start(stream, 0)
+    for pair in range(HEADS // 2):
         at = pl.ds(128 * pair, 128)
         low, high = keys_of(2 * pair), keys_of(2 * pair + 1)
         grads[1, :, at] = unit_back(jnp.where(left, low, swap(high)), k_raw[:, at]).astype(BF)
-        grads[2, :, at] = jnp.where(left, swap(low), high).astype(BF)
     term_of(1)
-    for stream in range(2):
-        kv_sum.start(stream, 0)
-    term_of(2)
     for stream in range(2, 5):
         kv_sum.start(stream, 0)
     q_sum.advance(0)
@@ -683,13 +697,19 @@
     grad_normed = gn[...]
     mean = jnp.mean(grad_normed * unit, axis=-1, keepdims=True)
     grad_input[...] = (carry_part[...] + row_scale * (grad_normed - unit * mean)).astype(BF)
-    carry = pltpu.make_async_remote_copy(
-        src_ref=grad_input, dst_ref=moved, send_sem=carry_sem.at[0], recv_sem=carry_sem.at[1],
-        device_id={"section": before, "seq": across}, device_id_type=MESH,
-    )
-    carry.start()
+
+    def carry(piece):
+        first, count = ((0, 48), (48, 32), (80, 32), (112, 24))[piece]
+        rows = pl.ds(first, count)
+        return pltpu.make_async_remote_copy(
+            src_ref=grad_input.at[rows], dst_ref=moved.at[rows], send_sem=carry_sem.at[0, piece],
+            recv_sem=carry_sem.at[1, piece], device_id={"section": before, "seq": across}, device_id_type=MESH,
+        )
+
+    carry(0).start()
     q_sum.advance(1)
     kv_sum.advance(0)
+    carry(1).start()
     q_sum.advance(2)
     for stream in out_sum.streams:
         result = out_sum.result(stream)
@@ -698,6 +718,8 @@
                 row = OUT_PLACES[part][1]
                 sum_out[:, 128 * part : 128 * part + 128] = result[row : row + 16]
     kv_sum.advance(1)
+    carry(2).start()
+    carry(3).start()
     q_sum.advance(3)
 
     def deliver(halving, places, targets):
@@ -712,8 +734,9 @@
     kv_sum.advance(2)
     deliver(q_sum, Q_PLACES, (sum_q,))
     kv_sum.advance(3)
-    deliver(kv_sum, KV_PLACES, (sum_k, sum_v))
-    carry.wait()
+    deliver(kv_sum, KV_PLACES, (sum_v, sum_k))
+    for piece in range(4):
+        carry(piece).wait()
 
     def left_all(k):
         kv_copy(k).wait_send()
@@ -742,16 +765,18 @@
 
 def whole_layer(*operands):
     eight, full, short = (HEADS * TOK, 128), (TOK, D), (HEADS, LONG, 128)
+    low, high = (128, LOW), (128, CLASS_ROWS - LOW)
     scratch = [
         (full, BF), (full, BF), ((D, INNER), BF), ((D, INNER), BF), ((D, INNER), BF), ((INNER, 2 * D), BF),
         (full, BF), ((D, TOK), BF), ((TOK, INNER), F32), ((TOK, INNER), F32), (short, BF), ((HEADS, TOK, 128), BF),
         ((4, CLASS_ROWS, 128), BF), (eight, BF), (eight, BF), ((TOKENS, 1), jnp.int32), (eight, BF), ((CLASS, 1), F32),
         (short, BF), ((TOK, INNER), BF), ((INNER, TOK), BF), ((TOK, 2 * D), BF), (short, BF), (full, F32),
-        ((128, CLASS_ROWS), F32), ((4, CLASS, 128), BF), (short, BF), ((HEADS, TOK, 128), BF), (short, BF),
+        ((128, CLASS_ROWS), F32), (eight, BF), (short, BF), ((HEADS, TOK, 128), BF), (short, BF),
         ((3, TOK, INNER), BF), (full, F32), (full, BF),
         ((40, 128), jnp.int32), ((CLASS, 1), jnp.int32), ((4, 1, CLASS_ROWS), jnp.int32), (eight, F32), (eight, F32),
-        ((4, HEAD_DIM, 2 * TOK), BF), ((4, HEAD_DIM, 2 * TOK), BF), ((CLASS, 1), F32), (eight, BF), (eight, BF),
-        ((LOW, 128), BF), ((CLASS - LOW, 128), BF), (short, BF), (short, BF), (short, BF),
+        ((4, HEAD_DIM, 2 * TOK), BF), ((4, HEAD_DIM, 2 * TOK), BF), ((CLASS, 1), F32),
+        (low, BF), (high, BF), (low, BF), (high, BF), ((3, *low), BF), ((3, *high), BF),
+        (low, BF), (high, BF), (short, BF), (short, BF), (short, BF),
     ]
     dma = pltpu.SemaphoreType.DMA
     return pl.pallas_call(
@@ -766,7 +791,7 @@
         + halving_scratch(KV_ROWS)
         + [dma((6,)), dma((8,)), dma((8,)), dma((8,)), dma((8,)), dma((2, 8)), dma((2, 8)), dma((8,)), dma((8,))]
         + [dma((8,))] * 8
-        + [dma((4,)), dma((2,)), dma((6,)), dma((6,))],
+        + [dma((4,)), dma((2, 4)), dma((6,)), dma((6,))],
         compiler_params=pltpu.CompilerParams(collective_id=1, has_side_effects=True, vmem_limit_bytes=BIG),
         name="layer",
     )(*operands)

time: 96.3 us -> 93.8 us (0.974)
  Pallas kernels: 95.5 us -> 93 us
    pallas_call x1, Pallas kernels: 93.4 us -> 90.8 us  [whole_layer(): pl.pallas_call(layer_body, out_shape=[jax.ShapeDtypeStruct((32, INNER), F...]
where the time goes in v6:
time: 93.8 us; the launch traced here: 93.6 us
  Pallas kernels  93 us (99%)
    pallas_call x1, Pallas kernels, whole_layer(): pl.pallas_call(layer_body, out_shape=[jax.ShapeDtypeStruct((32, INNER), F...  90.8 us
    pallas_call x1, Pallas kernels, hand_out(): pl.pallas_call(hand_out_body, out_shape=[jax.ShapeDtypeStruct((TOK, D), B...  2.16 us

profile of v6, /device:TPU:0, one launch (start us, length us, event | category | flops | bytes accessed | tf_op | source)
XLA Modules:
  0.0 93.6 jit_solution(17125026822477110179)
XLA Ops:
  0.6 90.8 %layer.1 = (f32[32,512]{1,0:T(8,128)}, f32[32,512]{1,0:T(8,128)}, f32[32,512]{1,0:T(8,128)}, f32[16,2048]{1,0:T(8,128)}, bf16[136,1024]{1,0:T(8,128)(2,1)}) custom-call(bf16[136,1024]{1,0:T(8,128)(2,1)} %bitcast.16, bf16[136,1024]{1,0:T(8,128)(2,1)} %bitcast.17, bf16[1024,512]{1,0:T(8,128)(2,1)} %bitcast.13, bf16[1024,512]{1,0:T(8,128)(2,1)} %bitcast.14, ...), custom_call_target="tpu_custom_call" | custom-call | tf_op jit(solution)/shard_map/layer/pallas_call | solution.py:782
  91.5 2.2 %hand_out.1 = (bf16[136,1024]{1,0:T(8,128)(2,1)}, f32[32,512]{1,0:T(8,128)}, f32[32,512]{1,0:T(8,128)}, f32[32,512]{1,0:T(8,128)}, f32[16,2048]{1,0:T(8,128)}) custom-call(f32[32,512]{1,0:T(8,128)} %get-tuple-element.15.sum_q, f32[32,512]{1,0:T(8,128)} %get-tuple-element.16.sum_k, f32[32,512]{1,0:T(8,128)} %get-tuple-element.17.sum_v, ...), custom_call_target="tpu_custom_call" | custom-call | tf_op jit(solution)/shard_map/hand_out/pallas_call | solution.py:814

commit v7 on v6

--- a/solution.py
+++ b/solution.py
@@ -85,20 +85,18 @@
     )
 
 
-ALL_LINKS = tuple(tuple((first + step) % 5 for step in range(5)) for first in range(5))
+ALL_LINKS = tuple(tuple((first + step) % 5 for step in range(5)) for first in (0, 2, 4, 1, 3))
 FLAT_FIRST = ((0, 1, 2, 3, 4), (1, 2, 0, 4, 3), (2, 0, 1, 3, 4))
 
 
-def spread_out(groups, orders):
-    streams = len(orders)
-    counts = [groups // streams + (1 if stream < groups % streams else 0) for stream in range(streams)]
-    places = [(stream, 16 * row) for stream in range(streams) for row in range(counts[stream])]
+def spread_out(counts):
+    places = [(stream, 16 * row) for stream, count in enumerate(counts) for row in range(count)]
     return [16 * count for count in counts], places
 
 
-Q_ROWS, Q_PLACES = spread_out(8, ALL_LINKS)
-KV_ROWS, KV_PLACES = spread_out(16, ALL_LINKS)
-OUT_ROWS, OUT_PLACES = spread_out(16, FLAT_FIRST)
+Q_ROWS, Q_PLACES = spread_out((2, 1, 1, 2, 2))
+KV_ROWS, KV_PLACES = spread_out((3, 3, 2, 4, 4))
+OUT_ROWS, OUT_PLACES = spread_out((6, 5, 5))
 
 
 def slot(order, owner, bits):
@@ -677,14 +675,14 @@
         low, high = keys_of(2 * pair), keys_of(2 * pair + 1)
         grads[2, :, 128 * pair : 128 * pair + 128] = jnp.where(left, swap(low), high).astype(BF)
     term_of(2)
-    for stream in range(2):
+    for stream in range(3):
         kv_sum.start(stream, 0)
     for pair in range(HEADS // 2):
         at = pl.ds(128 * pair, 128)
         low, high = keys_of(2 * pair), keys_of(2 * pair + 1)
         grads[1, :, at] = unit_back(jnp.where(left, low, swap(high)), k_raw[:, at]).astype(BF)
     term_of(1)
-    for stream in range(2, 5):
+    for stream in range(3, 5):
         kv_sum.start(stream, 0)
     q_sum.advance(0)
     out_sum.advance(3)

time: 93.8 us -> 92.8 us (0.989)
  Pallas kernels: 93 us -> 92 us
    pallas_call x1, Pallas kernels: 90.8 us -> 89.9 us  [whole_layer(): pl.pallas_call(layer_body, out_shape=[jax.ShapeDtypeStruct((32, INNER), F...]
where the time goes in v7:
time: 92.8 us; the launch traced here: 92.7 us
  Pallas kernels  92 us (99%)
    pallas_call x1, Pallas kernels, whole_layer(): pl.pallas_call(layer_body, out_shape=[jax.ShapeDtypeStruct((32, INNER), F...  89.9 us
    pallas_call x1, Pallas kernels, hand_out(): pl.pallas_call(hand_out_body, out_shape=[jax.ShapeDtypeStruct((TOK, D), B...  2.16 us

profile of v7, /device:TPU:0, one launch (start us, length us, event | category | flops | bytes accessed | tf_op | source)
XLA Modules:
  0.0 92.7 jit_solution(5245761675768465956)
XLA Ops:
  0.6 89.9 %layer.1 = (f32[32,512]{1,0:T(8,128)}, f32[32,512]{1,0:T(8,128)}, f32[32,512]{1,0:T(8,128)}, f32[16,2048]{1,0:T(8,128)}, bf16[136,1024]{1,0:T(8,128)(2,1)}) custom-call(bf16[136,1024]{1,0:T(8,128)(2,1)} %bitcast.16, bf16[136,1024]{1,0:T(8,128)(2,1)} %bitcast.17, bf16[1024,512]{1,0:T(8,128)(2,1)} %bitcast.13, bf16[1024,512]{1,0:T(8,128)(2,1)} %bitcast.14, ...), custom_call_target="tpu_custom_call" | custom-call | tf_op jit(solution)/shard_map/layer/pallas_call | solution.py:780
  90.5 2.2 %hand_out.1 = (bf16[136,1024]{1,0:T(8,128)(2,1)}, f32[32,512]{1,0:T(8,128)}, f32[32,512]{1,0:T(8,128)}, f32[32,512]{1,0:T(8,128)}, f32[16,2048]{1,0:T(8,128)}) custom-call(f32[32,512]{1,0:T(8,128)} %get-tuple-element.15.sum_q, f32[32,512]{1,0:T(8,128)} %get-tuple-element.16.sum_k, f32[32,512]{1,0:T(8,128)} %get-tuple-element.17.sum_v, ...), custom_call_target="tpu_custom_call" | custom-call | tf_op jit(solution)/shard_map/hand_out/pallas_call | solution.py:812

commit v8 on v7

--- a/solution.py
+++ b/solution.py
@@ -677,6 +677,7 @@
     term_of(2)
     for stream in range(3):
         kv_sum.start(stream, 0)
+    out_sum.advance(3)
     for pair in range(HEADS // 2):
         at = pl.ds(128 * pair, 128)
         low, high = keys_of(2 * pair), keys_of(2 * pair + 1)
@@ -685,7 +686,6 @@
     for stream in range(3, 5):
         kv_sum.start(stream, 0)
     q_sum.advance(0)
-    out_sum.advance(3)
     for block in range(4):
         at = pl.ds(256 * block, 256)
         gn[:, at] += dot_t(grads[1], wk[at, :]) + dot_t(grads[2], wv[at, :])

time: 92.8 us -> 95.4 us (1.028)
  Pallas kernels: 92 us -> 94.5 us
    pallas_call x1, Pallas kernels: 89.9 us -> 92.4 us  [whole_layer(): pl.pallas_call(layer_body, out_shape=[jax.ShapeDtypeStruct((32, INNER), F...]
where the time goes in v8:
time: 95.4 us; the launch traced here: 95.2 us
  Pallas kernels  94.5 us (99%)
    pallas_call x1, Pallas kernels, whole_layer(): pl.pallas_call(layer_body, out_shape=[jax.ShapeDtypeStruct((32, INNER), F...  92.4 us
    pallas_call x1, Pallas kernels, hand_out(): pl.pallas_call(hand_out_body, out_shape=[jax.ShapeDtypeStruct((TOK, D), B...  2.16 us

profile of v8, /device:TPU:0, one launch (start us, length us, event | category | flops | bytes accessed | tf_op | source)
XLA Modules:
  0.0 95.2 jit_solution(17211359230332859490)
XLA Ops:
  0.6 92.4 %layer.1 = (f32[32,512]{1,0:T(8,128)}, f32[32,512]{1,0:T(8,128)}, f32[32,512]{1,0:T(8,128)}, f32[16,2048]{1,0:T(8,128)}, bf16[136,1024]{1,0:T(8,128)(2,1)}) custom-call(bf16[136,1024]{1,0:T(8,128)(2,1)} %bitcast.16, bf16[136,1024]{1,0:T(8,128)(2,1)} %bitcast.17, bf16[1024,512]{1,0:T(8,128)(2,1)} %bitcast.13, bf16[1024,512]{1,0:T(8,128)(2,1)} %bitcast.14, ...), custom_call_target="tpu_custom_call" | custom-call | tf_op jit(solution)/shard_map/layer/pallas_call | solution.py:780
  93.0 2.2 %hand_out.1 = (bf16[136,1024]{1,0:T(8,128)(2,1)}, f32[32,512]{1,0:T(8,128)}, f32[32,512]{1,0:T(8,128)}, f32[32,512]{1,0:T(8,128)}, f32[16,2048]{1,0:T(8,128)}) custom-call(f32[32,512]{1,0:T(8,128)} %get-tuple-element.15.sum_q, f32[32,512]{1,0:T(8,128)} %get-tuple-element.16.sum_k, f32[32,512]{1,0:T(8,128)} %get-tuple-element.17.sum_v, ...), custom_call_target="tpu_custom_call" | custom-call | tf_op jit(solution)/shard_map/hand_out/pallas_call | solution.py:812
